TPU v7x, 256 devices: a whole 4x4x8 slice. The times are simulated.
256 devices in a mesh: sub: 8 (over x, core), lat: 8 (over z_lo, y), lon: 4 (over z_hi).
Axes of the slice: x: 4, y: 4, z: 8 (z_hi: 4, z_lo: 2; z = z_hi * 2 + z_lo), core: 2. Of those that a mesh axis runs over, the one named last changes fastest.
Arguments:
- segment_launch_values: float32 [8, 3, 4096, 1024], P('sub', None, 'lat', 'lon'), may hold values from -1.8 to 1.8
- initial_backdrop: float32 [3, 4096, 1024], P(None, 'lat', 'lon'), may hold values from -1.8 to 1.8
- spectral_inverse_variances: float32 [3, 513], replicated, may hold values from 0.3 to 3
Outputs:
- weighted_defects: float32 [8, 3, 4096, 1024], P('sub', None, 'lat', 'lon')
All inputs are finite; a program needn't handle non-finite values.
Results may differ from a plain program's by a relative error of at most 0.00017.
Values sent between devices are 32-bit elements; how exact they have to be, the bound alone decides.
No kernel may reach another device: no remote copies, remote signals or barrier semaphores. Data moves between devices by JAX's collectives and lax.ppermute only.
A program may use at most 64 MiB of HBM per device.

v0:
```python
import jax
import jax.numpy as jnp
from jax import lax
from jax.sharding import PartitionSpec as P

NLON = 1024
STEPS = 3


time_step = 0.5
coriolis_peak = 0.4


def padded_2(block, sides, width):
    for axis, dim in sides:
        count = lax.axis_size(axis)
        forward = [(i, i + 1) for i in range(count - 1)]
        forward.append((count - 1, 0))
        backward = [(target, source) for source, target in forward]
        low = lax.ppermute(
            lax.slice_in_dim(block, block.shape[dim] - width, None, axis=dim), axis, forward
        )
        high = lax.ppermute(lax.slice_in_dim(block, 0, width, axis=dim), axis, backward)
        block = jnp.concatenate([low, block, high], axis=dim)
    return block


def from_behind(value, axis, steps):
    count = lax.axis_size(axis)
    first, last = (max(0, -steps), min(count, count - steps))
    return lax.ppermute(value, axis, [(source, source + steps) for source in range(first, last)])


def split_up(x, dim, count):
    lengths = x.shape
    parts = x.reshape(*lengths[:dim], count, lengths[dim] // count, *lengths[dim + 1 :])
    return jnp.moveaxis(parts, dim, 0)


def piece_ends(length, count):
    lap = length // count
    if lap >= 8:
        lap -= lap % 8
    return [lap * k for k in range(1, count)]


def joined_along(parts, dim):
    lengths = list(parts.shape[1:])
    lengths[dim] *= parts.shape[0]
    return jnp.moveaxis(parts, 0, dim).reshape(lengths)


def cut_exchange(x, axis, pieces, split_dim, concat_dim):
    parts = split_up(x, split_dim, lax.axis_size(axis))
    widest = max(range(1, max(2, parts.ndim - 1)), key=lambda d: parts.shape[d])
    outs = []
    for share in jnp.split(parts, piece_ends(parts.shape[widest], pieces), axis=widest):
        if share.size:
            outs.append(lax.all_to_all(share, axis, split_axis=0, concat_axis=0, tiled=True))
    return joined_along(jnp.concatenate(outs, axis=widest), concat_dim)


def latitude_tendencies(total_rows, first_row, count):
    index = (first_row + jnp.arange(count)).astype(jnp.float32)
    return (coriolis_peak * jnp.sin(2.0 * jnp.pi * (index + 0.5) / total_rows))[:, None]


def centre(field):
    return field[1:-1, 1:-1]


def along_lon(field):
    return 0.5 * (field[1:-1, 2:] - field[1:-1, :-2])


def along_lat(field):
    return 0.5 * (field[2:, 1:-1] - field[:-2, 1:-1])


def tendency(padded, coriolis):
    height = padded[0]
    zonal = padded[1]
    meridional = padded[2]
    depth = 1.0 + height
    height_rate = -(along_lon(depth * zonal) + along_lat(depth * meridional))
    zonal_mid = centre(zonal)
    merid_mid = centre(meridional)
    zonal_rate = (
        -(zonal_mid * along_lon(zonal) + merid_mid * along_lat(zonal))
        + coriolis * merid_mid
        - along_lon(height)
    )
    merid_rate = (
        -(zonal_mid * along_lon(meridional) + merid_mid * along_lat(meridional))
        - coriolis * zonal_mid
        - along_lat(height)
    )
    return jnp.stack([height_rate, zonal_rate, merid_rate])


def margin_rows(coriolis, outer, keep):
    cut_rows = outer - keep
    return coriolis[cut_rows : coriolis.shape[0] - cut_rows]


def fourier_table(length):
    midpoint_split = length // 2
    index = jnp.arange(length, dtype=jnp.int32)
    wave = jnp.where(index <= midpoint_split, index, index - midpoint_split)
    product = index[:, None] * wave[None, :] % length
    angle = 2.0 * jnp.pi / length * product.astype(jnp.float32)
    return jnp.where(index[None, :] <= midpoint_split, jnp.cos(angle), jnp.sin(angle))


def shards(segment_launch_values, initial_backdrop, spectral_inverse_variances):
    flow_variables = segment_launch_values[0]
    lat_rows = flow_variables.shape[1]
    total_lat = lat_rows * lax.axis_size("lat")
    first_row = lax.axis_index("lat") * lat_rows
    outer = 3 * STEPS
    coriolis = latitude_tendencies(total_lat, first_row - outer, lat_rows + 2 * outer)
    state = padded_2(flow_variables, (("lat", 1), ("lon", 2)), outer)
    for step_number in range(STEPS):
        border_rows = outer - 3 * step_number
        first = state[:, 1:-1, 1:-1] + time_step * tendency(
            state, margin_rows(coriolis, outer, border_rows - 1)
        )
        second = 0.75 * state[:, 2:-2, 2:-2] + 0.25 * (
            first[:, 1:-1, 1:-1]
            + time_step * tendency(first, margin_rows(coriolis, outer, border_rows - 2))
        )
        state = 1.0 / 3.0 * state[:, 3:-3, 3:-3] + 2.0 / 3.0 * (
            second[:, 1:-1, 1:-1]
            + time_step * tendency(second, margin_rows(coriolis, outer, border_rows - 3))
        )
    flow_variables = state
    arrived = from_behind(flow_variables, "sub", 1)
    preceding_interval = jnp.where(lax.axis_index("sub") == 0, initial_backdrop, arrived)
    mismatch_misfits = segment_launch_values[0] - preceding_interval
    table = fourier_table(NLON)
    midpoint_split = NLON // 2
    column = jnp.arange(NLON, dtype=jnp.int32)
    factor = (
        jnp.where((column == 0) | (column == midpoint_split), 1.0, 2.0).astype(jnp.float32) / NLON
    )
    weights_full = (
        jnp.concatenate(
            [spectral_inverse_variances, spectral_inverse_variances[:, 1:midpoint_split]], axis=1
        )
        * factor[None, :]
    )
    whole_rows = cut_exchange(mismatch_misfits, "lon", 2, 1, 2)
    spectral_coefficients = jnp.einsum(
        "fan,nc->fac", whole_rows, table, precision=lax.Precision.HIGHEST
    )
    restored = jnp.einsum(
        "fac,nc->fan",
        spectral_coefficients * weights_full[:, None, :],
        table,
        precision=lax.Precision.HIGHEST,
    )
    weighted = lax.all_to_all(restored, "lon", split_axis=2, concat_axis=1, tiled=True)
    return weighted[None]


def solution(mesh):
    return jax.shard_map(
        shards,
        mesh=mesh,
        in_specs=(P("sub", None, "lat", "lon"), P(None, "lat", "lon"), P()),
        out_specs=P("sub", None, "lat", "lon"),
        check_vma=False,
    )
```

profile of v0, /device:TPU:58, one launch (start us, length us, event | category | flops | bytes accessed | tf_op | source)
XLA Modules:
  0.0 245.9 jit_solution(9439732789657524156)
XLA Ops:
  0.9 2.0 collective-permute-start.1
  2.9 2.1 collective-permute-done
  5.0 2.2 collective-permute-done.1
  9.4 3.3 %collective-permute-start.2 = (f32[3,530,9]{1,0,2:T(4,128)S(1)}, f32[3,530,9]{1,0,2:T(4,128)S(1)}, u32[]{:S(2)}, u32[]{:S(2)}) collective-permute-start(f32[3,530,9]{1,0,2:T(4,128)S(1)} %copy.9), channel_id=1, source_target_pairs={{0,1},{1,2},{2,3},{3,0},{4,5},{5,6},{6,7},{7,4},{8,9},{9,10},{10,1... | collective-permute-start | bytes 171728 | tf_op jit(solution)/shard_map/ppermute | solution.py:20
  13.2 3.3 %collective-permute-start.3 = (f32[3,530,9]{1,0,2:T(4,128)S(1)}, f32[3,530,9]{1,0,2:T(4,128)S(1)}, u32[]{:S(2)}, u32[]{:S(2)}) collective-permute-start(f32[3,530,9]{1,0,2:T(4,128)S(1)} %copy.10), channel_id=1, source_target_pairs={{1,0},{2,1},{3,2},{0,3},{5,4},{6,5},{7,6},{4,7},{9,8},{10,9},{11,1... | collective-permute-start | bytes 171728 | tf_op jit(solution)/shard_map/ppermute | solution.py:23
  17.1 1.9 collective-permute-done.2
  19.3 2.0 collective-permute-done.3
  23.7 2.5 %fusion.107 = (f32[1,528,272]{2,1,0:T(8,128)S(1)}, f32[1,528,272]{2,1,0:T(8,128)S(1)}) fusion(f32[530,274]{1,0:T(8,128)S(1)} %get-tuple-element.11, f32[530,274]{1,0:T(8,128)S(1)} %get-tuple-element.9, f32[530,274]{1,0:T(8,128)S(1)} %get-tuple-element.10, f32[528]{0:T(1024)S(1)} %slice.683), kind=kLoop, calls=%fused_computation.182 | loop fusion | flops 3734016 | bytes 9193536 | tf_op jit(solution)/shard_map/stack | solution.py:98
  28.0 2.5 %fusion.83 = (f32[1,526,270]{2,1,0:T(8,128)S(1)}, f32[1,526,270]{2,1,0:T(8,128)S(1)}) fusion(f32[528,272]{1,0:T(8,128)S(1)} %get-tuple-element.39, f32[528,272]{1,0:T(8,128)S(1)} %get-tuple-element.37, f32[528,272]{1,0:T(8,128)S(1)} %get-tuple-element.38, f32[526]{0:T(1024)S(1)} %slice.706), kind=kLoop, calls=%fused_computation.147 | loop fusion | flops 3692520 | bytes 9091384 | tf_op jit(solution)/shard_map/stack | solution.py:98
  30.5 1.6 fusion.13
  33.4 2.5 %fusion.59 = (f32[1,524,268]{2,1,0:T(8,128)S(1)}, f32[1,524,268]{2,1,0:T(8,128)S(1)}) fusion(f32[526,270]{1,0:T(8,128)S(1)} %get-tuple-element.34, f32[526,270]{1,0:T(8,128)S(1)} %get-tuple-element.32, f32[526,270]{1,0:T(8,128)S(1)} %get-tuple-element.33, f32[524]{0:T(1024)S(1)} %slice.729), kind=kLoop, calls=%fused_computation.112 | loop fusion | flops 3651232 | bytes 8989744 | tf_op jit(solution)/shard_map/stack | solution.py:98
  35.8 1.6 fusion.11
  38.5 2.5 %fusion.35 = (f32[1,522,266]{2,1,0:T(8,128)S(1)}, f32[1,522,266]{2,1,0:T(8,128)S(1)}) fusion(f32[524,268]{1,0:T(8,128)S(1)} %get-tuple-element.29, f32[524,268]{1,0:T(8,128)S(1)} %get-tuple-element.27, f32[524,268]{1,0:T(8,128)S(1)} %get-tuple-element.28, f32[522]{0:T(1024)S(1)} %slice.754), kind=kLoop, calls=%fused_computation.77 | loop fusion | flops 3610152 | bytes 8888616 | tf_op jit(solution)/shard_map/stack | solution.py:98
  42.9 2.6 %fusion.203 = (f32[1,520,264]{2,1,0:T(8,128)S(1)}, f32[1,520,264]{2,1,0:T(8,128)S(1)}) fusion(f32[522,266]{1,0:T(8,128)S(1)} %get-tuple-element.24, f32[522,266]{1,0:T(8,128)S(1)} %get-tuple-element.22, f32[522,266]{1,0:T(8,128)S(1)} %get-tuple-element.23, f32[520]{0:T(1024)S(1)} %slice.777), kind=kLoop, calls=%fused_computation.322 | loop fusion | flops 3569280 | bytes 8788000 | tf_op jit(solution)/shard_map/stack | solution.py:98
  48.2 2.5 fusion.179
  50.7 1.7 fusion.17
  53.5 2.5 fusion.155
  58.2 2.5 %fusion.131 = (f32[1,514,258]{2,1,0:T(8,128)S(1)}, f32[1,514,258]{2,1,0:T(8,128)S(1)}) fusion(f32[516,260]{1,0:T(8,128)S(1)} %get-tuple-element.57, f32[516,260]{1,0:T(8,128)S(1)} %get-tuple-element.55, f32[516,260]{1,0:T(8,128)S(1)} %get-tuple-element.56, f32[514]{0:T(1024)S(1)} %slice.848), kind=kLoop, calls=%fused_computation.217 | loop fusion | flops 3447912 | bytes 8489224 | tf_op jit(solution)/shard_map/stack | solution.py:98
  63.1 1.6 fusion.228
  64.8 2.1 fusion.21
  66.9 1.9 collective-permute-start.4
  68.8 20.1 %collective-permute-done.4 = f32[3,512,256]{2,1,0:T(8,128)} collective-permute-done((f32[3,512,256]{2,1,0:T(8,128)}, f32[3,512,256]{2,1,0:T(8,128)}, u32[]{:S(2)}, u32[]{:S(2)}) %collective-permute-start.4) | collective-permute-done | bytes 1572896 | tf_op jit(solution)/shard_map/ppermute | solution.py:31
  88.9 1.7 select_subtract_fusion
  91.8 5.3 %all-to-all-start = ((f32[4,3,64,256]{3,2,1,0:T(8,128)}), f32[4,3,64,256]{3,2,1,0:T(8,128)S(1)}, u32[]{:S(2)}, u32[]{:S(2)}) async-start(f32[4,3,64,256]{3,2,1,0:T(8,128)} %copy.13), calls=%async_computation | async-start | bytes 1572864 | tf_op jit(solution)/shard_map/all_to_all | solution.py:59
  98.1 18.4 %all-to-all-done = f32[4,3,64,256]{3,2,1,0:T(8,128)S(1)} async-done(((f32[4,3,64,256]{3,2,1,0:T(8,128)}), f32[4,3,64,256]{3,2,1,0:T(8,128)S(1)}, u32[]{:S(2)}, u32[]{:S(2)}) %all-to-all-start) | async-done | bytes 786464 | tf_op jit(solution)/shard_map/all_to_all | solution.py:59
  116.5 5.1 %all-to-all-start.1 = ((f32[4,3,64,256]{3,2,1,0:T(8,128)}), f32[4,3,64,256]{3,2,1,0:T(8,128)}, u32[]{:S(2)}, u32[]{:S(2)}) async-start(f32[4,3,64,256]{3,2,1,0:T(8,128)} %copy.14), calls=%async_computation.1 | async-start | bytes 1572864 | tf_op jit(solution)/shard_map/all_to_all | solution.py:59
  122.2 18.2 %all-to-all-done.1 = f32[4,3,64,256]{3,2,1,0:T(8,128)} async-done(((f32[4,3,64,256]{3,2,1,0:T(8,128)}), f32[4,3,64,256]{3,2,1,0:T(8,128)}, u32[]{:S(2)}, u32[]{:S(2)}) %all-to-all-start.1) | async-done | bytes 786464 | tf_op jit(solution)/shard_map/all_to_all | solution.py:59
  142.5 27.2 %fusion.5 = f32[3,128,1024]{2,1,0:T(8,128)S(1)} fusion(f32[3,128,1024]{1,2,0:T(8,128)S(1)} %bitcast.203, s32[1024]{0:T(1024)S(1)} %add_select_fusion.1, pred[1024]{0:T(1024)(128)(4,1)S(1)} %iota_compare_fusion.2), kind=kOutput, calls=%fused_computation.8 | convolution fusion | flops 4847566848 | bytes 3150848 | tf_op jit(solution)/shard_map/fan,nc->fac/dot_general | solution.py:153
  169.7 23.2 %fusion.3 = f32[3,128,1024]{2,1,0:T(8,128)} fusion(s32[1024]{0:T(1024)S(1)} %add_select_fusion.1, pred[1024]{0:T(1024)(128)(4,1)S(1)} %iota_compare_fusion.2, f32[3,128,1024]{2,1,0:T(8,128)S(1)} %fusion.5, f32[3,1024]{1,0:T(4,128)S(1)} %maximum_multiply_fusion.9), kind=kOutput, calls=%fused_computation.6 | convolution fusion | flops 4847960064 | bytes 3163136 | tf_op jit(solution)/shard_map/fac,nc->fan/dot_general | solution.py:156
  192.9 1.9 copy.18
  194.9 48.1 %all_to_all.25 = f32[3,128,1024]{1,0,2:T(4,128)} all-to-all(f32[3,128,1024]{1,0,2:T(4,128)S(1)} %copy.18), channel_id=1, replica_groups=mesh['sub'=8,'lat'=8,'lon'=4] {'lon'}, dimensions={2} | all-to-all | bytes 3145728 | tf_op jit(solution)/shard_map/all_to_all | solution.py:162
  243.0 2.7 %copy.19 = f32[3,4,128,256]{3,2,1,0:T(8,128)} copy(f32[3,4,128,256]{2,0,3,1:T(4,128)} %bitcast.201) | data formatting | bytes 3145728 | tf_op jit(solution)/shard_map/all_to_all | solution.py:162
  (68 shorter events, 25.8 us)
Async XLA Ops:
  0.8 4.2 %collective-permute-start = (f32[3,9,256]{2,1,0:T(8,128)S(1)}, f32[3,9,256]{2,1,0:T(8,128)S(1)}, u32[]{:S(2)}, u32[]{:S(2)}) collective-permute-start(f32[3,9,256]{2,1,0:T(8,128)S(1)} %get-tuple-element.72), channel_id=1, source_target_pairs={{0,4},{4,8},{8,12},{12,16},{16,20},{20,24},{24,28},{28,0},{1,5},{5... | collective-permute-start | bytes 82952 | tf_op jit(solution)/shard_map/ppermute | solution.py:20
  0.9 6.3 %collective-permute-start.1 = (f32[3,9,256]{2,1,0:T(8,128)S(1)}, f32[3,9,256]{2,1,0:T(8,128)S(1)}, u32[]{:S(2)}, u32[]{:S(2)}) collective-permute-start(f32[3,9,256]{2,1,0:T(8,128)S(1)} %get-tuple-element.73), channel_id=1, source_target_pairs={{4,0},{8,4},{12,8},{16,12},{20,16},{24,20},{28,24},{0,28},{5,1},{9... | collective-permute-start | bytes 82952 | tf_op jit(solution)/shard_map/ppermute | solution.py:23
  9.0 12.6 %copy-start = (f32[1,3,512,256]{3,2,1,0:T(8,128)S(1)}, f32[1,3,512,256]{3,2,1,0:T(8,128)}, u32[]{:S(2)}) copy-start(f32[1,3,512,256]{3,2,1,0:T(8,128)} %param.3) | copy-start | bytes 4718596
  9.4 9.6 %collective-permute-start.2 = (f32[3,530,9]{1,0,2:T(4,128)S(1)}, f32[3,530,9]{1,0,2:T(4,128)S(1)}, u32[]{:S(2)}, u32[]{:S(2)}) collective-permute-start(f32[3,530,9]{1,0,2:T(4,128)S(1)} %copy.9), channel_id=1, source_target_pairs={{0,1},{1,2},{2,3},{3,0},{4,5},{5,6},{6,7},{7,4},{8,9},{9,10},{10,1... | collective-permute-start | bytes 171728 | tf_op jit(solution)/shard_map/ppermute | solution.py:20
  13.2 8.1 %collective-permute-start.3 = (f32[3,530,9]{1,0,2:T(4,128)S(1)}, f32[3,530,9]{1,0,2:T(4,128)S(1)}, u32[]{:S(2)}, u32[]{:S(2)}) collective-permute-start(f32[3,530,9]{1,0,2:T(4,128)S(1)} %copy.10), channel_id=1, source_target_pairs={{1,0},{2,1},{3,2},{0,3},{5,4},{6,5},{7,6},{4,7},{9,8},{10,9},{11,1... | collective-permute-start | bytes 171728 | tf_op jit(solution)/shard_map/ppermute | solution.py:23
  64.8 24.2 %copy-start.1 = (f32[3,512,256]{2,1,0:T(8,128)S(1)}, f32[3,512,256]{2,1,0:T(8,128)}, u32[]{:S(2)}) copy-start(f32[3,512,256]{2,1,0:T(8,128)} %param.4) | copy-start | bytes 4718596
  66.9 22.0 %collective-permute-start.4 = (f32[3,512,256]{2,1,0:T(8,128)}, f32[3,512,256]{2,1,0:T(8,128)}, u32[]{:S(2)}, u32[]{:S(2)}) collective-permute-start(f32[3,512,256]{2,1,0:T(8,128)} %fusion.21), channel_id=1, source_target_pairs={{0,32},{32,64},{64,96},{96,128},{128,160},{160,192},{192,224},{1,3... | collective-permute-start | bytes 4718600 | tf_op jit(solution)/shard_map/ppermute | solution.py:31
  91.8 29.8 %copy-start.2 = (f32[3,513]{1,0:T(4,128)S(1)}, f32[3,513]{1,0:T(4,128)}, u32[]{:S(2)}) copy-start(f32[3,513]{1,0:T(4,128)} %param.5) | copy-start | bytes 18472
  91.8 24.7 %all-to-all-start = ((f32[4,3,64,256]{3,2,1,0:T(8,128)}), f32[4,3,64,256]{3,2,1,0:T(8,128)S(1)}, u32[]{:S(2)}, u32[]{:S(2)}) async-start(f32[4,3,64,256]{3,2,1,0:T(8,128)} %copy.13), calls=%async_computation | async-start | bytes 1572864 | tf_op jit(solution)/shard_map/all_to_all | solution.py:59
  116.5 23.9 %all-to-all-start.1 = ((f32[4,3,64,256]{3,2,1,0:T(8,128)}), f32[4,3,64,256]{3,2,1,0:T(8,128)}, u32[]{:S(2)}, u32[]{:S(2)}) async-start(f32[4,3,64,256]{3,2,1,0:T(8,128)} %copy.14), calls=%async_computation.1 | async-start | bytes 1572864 | tf_op jit(solution)/shard_map/all_to_all | solution.py:59
where the time goes:
time: 250 us; the launch traced here: 246 us
  waiting for transfers between devices  64.8 us (26%)
  matrix products  50.4 us (20%)
  blocking collectives  48.1 us (19%)
  other arithmetic  47.5 us (19%)
  starting transfers between devices  21 us (8%)
  local copies, waits for them, and re-layouts  13.4 us (5%)
    all_to_all x1, blocking collectives, shards(): lax.all_to_all(restored, 'lon', split_axis=2, concat_axis=1, tiled=True)  48.1 us
    all_to_all x2, waiting for transfers between devices, cut_exchange(): lax.all_to_all(share, axis, split_axis=0, concat_axis=0, tiled=True)  36.5 us
    another operation x18, other arithmetic, tendency(): return jnp.stack([height_rate, zonal_rate, merid_rate])  28.8 us
    dot_general x1, matrix products, shards(): jnp.einsum('fan,nc->fac', whole_rows, table, precision=lax.Precision.HIGH...  27.2 us
    dot_general x1, matrix products, shards(): jnp.einsum('fac,nc->fan', spectral_coefficients * weights_full[:, None, :...  23.2 us
    ppermute x1, waiting for transfers between devices, from_behind(): lax.ppermute(value, axis, [(source, source + steps) for source in range(f...  20.1 us
    all_to_all x2, starting transfers between devices, cut_exchange(): lax.all_to_all(share, axis, split_axis=0, concat_axis=0, tiled=True)  10.4 us
    add x3, other arithmetic, shards(): 1.0 / 3.0 * state[:, 3:-3, 3:-3]  5.47 us
  transfers between devices with their start and end apart: 7, of which 7 were waited for; matrix products, arithmetic and copies ran while one was open for 1% of the time, Pallas kernels for 0%

commit v1 on v0

v1 whole, which is shorter than its diff:
```python
import functools

import numpy as np
import jax
import jax.numpy as jnp
from jax import lax
from jax.experimental import pallas as pl
from jax.experimental.pallas import tpu as pltpu
from jax.sharding import PartitionSpec as P

NLON = 1024
STEPS = 3
time_step = 0.5
coriolis_peak = 0.4

SUB = 8
LON = 4
ROWS = 128
HALO = 3 * STEPS
FIRST = 96
MID = 16
HALF = 64
GROUP = 4
F32 = jnp.float32
BF16 = jnp.bfloat16


def unpack_rows(dst, piece, field, first, count, row0, block):
    for r in range(0, count, 8):
        for half in range(2):
            dst[field, pl.ds((row0 + r) * 8 + 2 * block + half, 8, stride=8), :] = piece[
                first + r : first + r + 8, 128 * half : 128 * half + 128
            ]


def stage(src, base, dst, f_ref, lo, rows, kind):
    lane = lax.broadcasted_iota(jnp.int32, (8, 128), 1)
    is_first = lane == 0
    is_last = lane == 127

    def dx(a):
        up = pltpu.roll(a, 127, 1)
        down = pltpu.roll(a, 1, 1)
        up = jnp.where(is_last, pltpu.roll(up, 7, 0), up)
        down = jnp.where(is_first, pltpu.roll(down, 1, 0), down)
        return up - down

    def body(g, carry):
        row = lo + g * GROUP

        def load(ref, c, k):
            return ref[c, pl.ds(pl.multiple_of((row + k) * 8, 8), 8), :]

        h = [load(src, 0, k) for k in range(-1, GROUP + 1)]
        u = [load(src, 1, k) for k in range(-1, GROUP + 1)]
        v = [load(src, 2, k) for k in range(-1, GROUP + 1)]
        flux = [v[k] + h[k] * v[k] for k in range(GROUP + 2)]
        for k in range(1, GROUP + 1):
            f = f_ref[row + k - 1]
            t_h = dx(u[k] + h[k] * u[k]) + (flux[k + 1] - flux[k - 1])
            t_u = u[k] * dx(u[k]) + v[k] * ((u[k + 1] - u[k - 1]) - f) + dx(h[k])
            t_v = u[k] * (dx(v[k]) + f) + v[k] * (v[k + 1] - v[k - 1]) + (h[k + 1] - h[k - 1])
            for c, (now, t) in enumerate(((h[k], t_h), (u[k], t_u), (v[k], t_v))):
                new = now - (0.5 * time_step) * t
                if kind == 1:
                    new = 0.75 * load(base, c, k - 1) + 0.25 * new
                elif kind == 2:
                    new = (1.0 / 3.0) * load(base, c, k - 1) + (2.0 / 3.0) * new
                dst[c, pl.ds(pl.multiple_of((row + k - 1) * 8, 8), 8), :] = new
        return carry

    lax.fori_loop(0, -(-rows // GROUP), body, 0)


def run_model(bufs, f_ref, rows):
    x, b, c, y = bufs
    done = 0
    for _ in range(STEPS):
        for kind, (src, base, dst) in enumerate(((x, x, b), (b, x, c), (c, x, y))):
            done += 1
            stage(src, base, dst, f_ref, done, rows - 2 * done, kind)
        x, y = y, x
    return x


def pack_rows(out, src, out0, count, row0):
    for c in range(3):
        for r in range(0, count, 8):
            for s in range(8):
                out[c, out0 + r : out0 + r + 8, 128 * s : 128 * s + 128] = src[
                    c, pl.ds((row0 + r) * 8 + s, 8, stride=8), :
                ]


ROWS_1 = HALF + 2 * HALO
LOW_1 = MID - HALO


def first_model_kernel(f_ref, p0, p1, p2, p3, out, *bufs):
    for block, piece in enumerate((p0, p1, p2, p3)):
        for c in range(3):
            unpack_rows(bufs[0], piece.at[c], c, 0, FIRST, 0, block)
    views = [b.at[:, pl.ds(LOW_1 * 8, (ROWS_1 + 8) * 8), :] for b in bufs]
    done = run_model(views, f_ref, ROWS_1)
    pack_rows(out, done, 0, HALF, HALO)


TOP = MID + 2 * HALO
REST = ROWS - MID - HALF
BOTTOM = REST + 2 * HALO
ROWS_2 = TOP + BOTTOM


def second_model_kernel(f_ref, p0, p1, p2, p3, q0, q1, q2, q3, out, *bufs):
    x = bufs[0]
    late = ROWS - FIRST
    bottom = TOP + FIRST - (MID + HALF - HALO)
    for block, (p, q) in enumerate(((p0, q0), (p1, q1), (p2, q2), (p3, q3))):
        for c in range(3):
            edge = 3 * late + 2 * HALO * c
            unpack_rows(x, q, c, edge, 16, 0, block)
            unpack_rows(x, p.at[c], c, 0, 24, HALO, block)
            unpack_one_row(x, p.at[c], c, 24, HALO + 24, block)
            unpack_one_row(x, p.at[c], c, 71, TOP, block)
            unpack_rows(x, p.at[c], c, 72, 24, TOP + 1, block)
            unpack_rows(x, q, c, late * c, late, bottom, block)
            unpack_rows(x, q, c, edge + HALO, 8, bottom + late, block)
            unpack_one_row(x, q, c, edge + HALO + 8, bottom + late + 8, block)
    done = run_model(bufs, f_ref, ROWS_2)
    pack_rows(out, done, 0, MID, HALO)
    pack_rows(out, done, MID, REST, TOP + HALO)


def unpack_one_row(dst, piece, field, src_row, row, block):
    for half in range(2):
        dst[field, pl.ds(row * 8 + 2 * block + half, 1), :] = piece[
            src_row : src_row + 1, 128 * half : 128 * half + 128
        ]


def vmem_spec():
    return pl.BlockSpec(memory_space=pltpu.VMEM)


def smem_spec():
    return pl.BlockSpec(memory_space=pltpu.SMEM)


def model_call(kernel, f, pieces, buffer_rows, rows):
    n_ops = rows * 9 * 1024 * 60
    return pl.pallas_call(
        kernel,
        out_shape=jax.ShapeDtypeStruct((3, HALF, NLON), F32),
        in_specs=[smem_spec()] + [vmem_spec()] * len(pieces),
        out_specs=vmem_spec(),
        scratch_shapes=[pltpu.VMEM((3, buffer_rows * 8, 128), F32)] * 4,
        compiler_params=pltpu.CompilerParams(vmem_limit_bytes=32 << 20),
        cost_estimate=pl.CostEstimate(
            flops=n_ops, bytes_accessed=4 * 3 * NLON * rows * 2, transcendentals=0
        ),
    )(f, *pieces)


def cosine_table():
    m = np.arange(NLON // 2 + 1)
    n = np.arange(NLON)
    factor = np.where((m == 0) | (m == NLON // 2), 1.0, 2.0) / NLON
    angle = 2.0 * np.pi / NLON * ((m[:, None] * n[None, :]) % NLON)
    return (factor[:, None] * np.cos(angle)).astype(np.float32)


def split(x):
    high = x.astype(BF16)
    return high, (x - high.astype(F32)).astype(BF16)


def toeplitz(row, size, sign):
    full = pltpu.roll(jnp.broadcast_to(row, (size, size)), 0, 1, stride=1, stride_axis=0)
    if sign < 0:
        c = lax.broadcasted_iota(jnp.int32, (size, size), 0)
        r = lax.broadcasted_iota(jnp.int32, (size, size), 1)
        full = jnp.where(r < c, -full, full)
    return full


def matrices_kernel(a_ref, b_ref, r_ref, ah, al, bh, bl, rh, rl):
    for c in range(3):
        ah[c], al[c] = split(toeplitz(a_ref[c : c + 1, :], 256, 1))
        bh[c], bl[c] = split(toeplitz(b_ref[c : c + 1, :], 256, -1))
        rh[c], rl[c] = split(toeplitz(r_ref[c : c + 1, :], 512, -1))


def weighting_matrices(variances):
    k = jnp.dot(variances, jnp.asarray(cosine_table()), precision=lax.Precision.HIGHEST)
    k0, k1, k2, k3 = (k[:, 256 * j : 256 * j + 256] for j in range(4))
    even = (k0 + k2) * 0.25
    odd = (k1 + k3) * 0.25
    r = (k[:, :512] - k[:, 512:]) * 0.5
    shapes = [(3, n, n) for n in (256, 256, 256, 256, 512, 512)]
    return pl.pallas_call(
        matrices_kernel,
        out_shape=[jax.ShapeDtypeStruct(s, BF16) for s in shapes],
        in_specs=[vmem_spec()] * 3,
        out_specs=[vmem_spec()] * 6,
        compiler_params=pltpu.CompilerParams(vmem_limit_bytes=32 << 20),
    )(even + odd, even - odd, r)


def dot3(x, high, low):
    xh, xl = split(x)
    return (
        jnp.dot(xh, high, preferred_element_type=F32)
        + jnp.dot(xl, high, preferred_element_type=F32)
        + jnp.dot(xh, low, preferred_element_type=F32)
    )


def weight_kernel(pick, n_x, flag, f_ref, b_ref, *refs):
    x_refs = refs[:n_x]
    ah, al, bh, bl, rh, rl = refs[n_x : n_x + 6]
    outs = refs[n_x + 6 :]
    start = flag[0] != 0
    for c in range(3):
        d = []
        for block in range(4):
            cols = slice(256 * block, 256 * block + 256)
            f = f_ref[c, :, cols]
            back = b_ref[:, c, :, cols].reshape(HALF, 256)
            prev = jnp.where(start, back, f)
            d.append(pick(x_refs, block, c) - prev)
        even, odd = d[0] + d[2], d[1] + d[3]
        x = dot3(even + odd, ah[c], al[c])
        y = dot3(even - odd, bh[c], bl[c])
        w = dot3(
            jnp.concatenate([d[0] - d[2], d[1] - d[3]], axis=1), rh[c], rl[c]
        )
        w0, w1 = w[:, :256], w[:, 256:]
        p, q = x + y, x - y
        outs[0][c] = p + w0
        outs[1][c] = q + w1
        outs[2][c] = p - w0
        outs[3][c] = q - w1


def pick_first(refs, block, c):
    return refs[block][c, MID : MID + HALF, :]


def pick_second(refs, block, c):
    early, late = refs[block], refs[4 + block]
    return jnp.concatenate(
        [
            early[c, :MID, :],
            early[c, MID + HALF : FIRST, :],
            late[(ROWS - FIRST) * c : (ROWS - FIRST) * (c + 1), :],
        ],
        axis=0,
    )


def weight_call(pick, flag, f, back, xs, mats):
    return pl.pallas_call(
        functools.partial(weight_kernel, pick, len(xs)),
        out_shape=[jax.ShapeDtypeStruct((3, HALF, 256), F32)] * 4,
        in_specs=[smem_spec()] + [vmem_spec()] * (2 + len(xs) + 6),
        out_specs=[vmem_spec()] * 4,
        compiler_params=pltpu.CompilerParams(vmem_limit_bytes=32 << 20),
        cost_estimate=pl.CostEstimate(
            flops=2 * 3 * HALF * 6 * 256 * 256 * 3, bytes_accessed=8 << 20, transcendentals=0
        ),
    )(flag, f, back, *xs, *mats)


def coriolis_rows(total, first, offsets):
    index = (first + offsets).astype(F32)
    return 2.0 * coriolis_peak * jnp.sin(2.0 * jnp.pi * (index + 0.5) / total)


def ring(count, shift):
    return [(i, (i + shift) % count) for i in range(count)]


def to_next(value, j):
    pairs = [
        (s * LON + a, ((s + 1) % SUB) * LON + (a + j) % LON)
        for s in range(SUB)
        for a in range(LON)
    ]
    return lax.ppermute(value, ("sub", "lon"), pairs)


def to_lon(value, j):
    return lax.ppermute(value, "lon", ring(LON, j))


ORDER = (0, 3, 2, 1)


def shards(segment_launch_values, initial_backdrop, spectral_inverse_variances):
    x = segment_launch_values[0]
    sub, lat, lon = (lax.axis_index(n) for n in ("sub", "lat", "lon"))
    tile_rows = x.shape[1]
    total = tile_rows * lax.axis_size("lat")
    target = [lax.rem(lon + j, LON) for j in range(LON)]
    late = ROWS - FIRST

    above = lax.ppermute(x[:, tile_rows - HALO :], "lat", ring(8, 1))
    below = lax.ppermute(x[:, :HALO], "lat", ring(8, -1))

    p = {}
    for j in (2, 1, 3, 0):
        block = lax.dynamic_slice(x, (0, ROWS * target[j], 0), (3, FIRST, 256))
        p[j] = to_next(block, j)

    b = {}
    for j in (2, 1, 3, 0):
        part = lax.dynamic_slice(
            initial_backdrop, (0, ROWS * target[j] + 16 * sub, 0), (3, 16, 256)
        )
        b[j] = to_lon(part, j) if j else part
    back = lax.all_gather(jnp.concatenate([b[j] for j in ORDER], axis=2), "sub")

    edges = []
    for q in range(LON):
        up = above if q == 0 else x[:, ROWS * q - HALO : ROWS * q]
        down = below if q == LON - 1 else x[:, ROWS * (q + 1) : ROWS * (q + 1) + HALO]
        edges.append(jnp.concatenate([up, down], axis=1).reshape(6 * HALO, 256))
    edges = jnp.stack(edges)
    q = {}
    for j in (2, 1, 3, 0):
        rest = lax.dynamic_slice(x, (0, ROWS * target[j] + FIRST, 0), (3, late, 256))
        edge = lax.dynamic_index_in_dim(edges, target[j], 0, keepdims=False)
        q[j] = to_next(jnp.concatenate([rest.reshape(3 * late, 256), edge], axis=0), j)

    own_p = {j: lax.ppermute(p[j], "sub", ring(SUB, -1)) for j in (0, 1, 3, 2)}
    own_q = {j: lax.ppermute(q[j][: 3 * late], "sub", ring(SUB, -1)) for j in (0, 1, 3, 2)}

    mats = weighting_matrices(spectral_inverse_variances)
    flag = (sub == 0).astype(jnp.int32).reshape(1)
    first_row = lat * tile_rows + lon * ROWS

    ps = [p[j] for j in ORDER]
    qs = [q[j] for j in ORDER]
    own_ps = [own_p[j] for j in ORDER]
    own_qs = [own_q[j] for j in ORDER]

    f1 = coriolis_rows(total, first_row, LOW_1 + jnp.arange(ROWS_1 + 8))
    offsets = np.concatenate([np.arange(TOP) - HALO, np.arange(BOTTOM + 8) + MID + HALF - HALO])
    f2 = coriolis_rows(total, first_row, jnp.asarray(offsets))

    m1 = model_call(first_model_kernel, f1, ps, FIRST + 8, ROWS_1)
    o1 = weight_call(pick_first, flag, m1, back[1:5], own_ps, mats)
    r1 = [to_lon(o1[j], j) if j else o1[j] for j in range(LON)]
    m2 = model_call(second_model_kernel, f2, ps + qs, ROWS_2 + 16, ROWS_2)
    back2 = jnp.concatenate([back[:1], back[5:]], axis=0)
    o2 = weight_call(pick_second, flag, m2, back2, own_ps + own_qs, mats)
    r2 = [to_lon(o2[j], j) if j else o2[j] for j in range(LON)]

    out = jnp.zeros_like(x)
    for j in range(LON):
        row = ROWS * lax.rem(lon - j + LON, LON)
        out = lax.dynamic_update_slice(out, r1[j], (0, row + MID, 0))
        out = lax.dynamic_update_slice(out, r2[j][:, :MID], (0, row, 0))
        out = lax.dynamic_update_slice(out, r2[j][:, MID:], (0, row + MID + HALF, 0))
    return out[None]


def solution(mesh):
    return jax.shard_map(
        shards,
        mesh=mesh,
        in_specs=(P("sub", None, "lat", "lon"), P(None, "lat", "lon"), P()),
        out_specs=P("sub", None, "lat", "lon"),
        check_vma=False,
    )
```

time: 250 us -> 205 us (0.82)
  the two profiles are of different devices: /device:TPU:58 before, /device:TPU:24 now
where the time goes in v1:
time: 205 us; the launch traced here: 202 us
  waiting for transfers between devices  72.4 us (35%)
  Pallas kernels  49 us (24%)
  starting transfers between devices  40 us (20%)
  local copies, waits for them, and re-layouts  18.4 us (9%)
  between operations  13.9 us (7%)
  other arithmetic  4.96 us (2%)
  matrix products  2.96 us (1%)
    pallas_call x2, Pallas kernels, model_call(): pl.pallas_call(kernel, out_shape=jax.ShapeDtypeStruct((3, HALF, NLON), F3...  42.9 us
    ppermute x9, waiting for transfers between devices, to_lon(): return lax.ppermute(value, 'lon', ring(LON, j))  36.5 us
    ppermute x8, waiting for transfers between devices, to_next(): return lax.ppermute(value, ('sub', 'lon'), pairs)  35.9 us
    ppermute x9, starting transfers between devices, to_lon(): return lax.ppermute(value, 'lon', ring(LON, j))  23.4 us
    ppermute x8, starting transfers between devices, to_next(): return lax.ppermute(value, ('sub', 'lon'), pairs)  8.53 us
    unnamed x43, local copies, waits for them, and re-layouts  6.95 us
    slice x4, local copies, waits for them, and re-layouts, shards(): q[j][:3 * late]  6.25 us
    ppermute x4, starting transfers between devices, shards(): own_p = {j: lax.ppermute(p[j], 'sub', ring(SUB, -1)) for j in (0, 1, 3, 2)}  5.96 us
  transfers between devices with their start and end apart: 28, of which 9 were waited for; matrix products, arithmetic and copies ran while one was open for 8% of the time, Pallas kernels for 24%

profile of v1, /device:TPU:24, one launch (start us, length us, event | category | flops | bytes accessed | tf_op | source)
XLA Modules:
  0.0 201.6 jit_solution(8803955303785115254)
XLA Ops:
  7.6 6.4 %collective-permute-start.4 = (f32[3,16,256]{2,1,0:T(8,128)S(1)}, f32[3,16,256]{2,1,0:T(8,128)S(1)}, u32[]{:S(2)}, u32[]{:S(2)}) collective-permute-start(f32[3,16,256]{2,1,0:T(8,128)S(1)} %get-tuple-element.46), channel_id=1, source_target_pairs={{0,3},{1,0},{2,1},{3,2},{4,7},{5,4},{6,5},{7,6},{8,11},{9,8},{10,9... | collective-permute-start | bytes 147464 | tf_op jit(solution)/shard_map/ppermute | solution.py:293
  14.9 2.8 %collective-permute-start.6 = (f32[3,16,256]{2,1,0:T(8,128)S(1)}, f32[3,16,256]{2,1,0:T(8,128)S(1)}, u32[]{:S(2)}, u32[]{:S(2)}) collective-permute-start(f32[3,16,256]{2,1,0:T(8,128)S(1)} %get-tuple-element.47), channel_id=1, source_target_pairs={{0,1},{1,2},{2,3},{3,0},{4,5},{5,6},{6,7},{7,4},{8,9},{9,10},{10,1... | collective-permute-start | bytes 147464 | tf_op jit(solution)/shard_map/ppermute | solution.py:293
  17.7 4.5 %collective-permute-done.5 = f32[3,16,256]{2,1,0:T(8,128)S(1)} collective-permute-done((f32[3,16,256]{2,1,0:T(8,128)S(1)}, f32[3,16,256]{2,1,0:T(8,128)S(1)}, u32[]{:S(2)}, u32[]{:S(2)}) %collective-permute-start.5) | collective-permute-done | bytes 49184 | tf_op jit(solution)/shard_map/ppermute | solution.py:293
  23.0 1.7 fusion.11
  26.8 3.5 %collective-permute-start.1 = (f32[3,96,256]{2,1,0:T(8,128)S(1)}, f32[3,96,256]{2,1,0:T(8,128)}, u32[]{:S(2)}, u32[]{:S(2)}) collective-permute-start(f32[3,96,256]{2,1,0:T(8,128)S(1)} %get-tuple-element.51), channel_id=1, source_target_pairs={{0,35},{1,32},{2,33},{3,34},{32,67},{33,64},{34,65},{35,66},{64,99... | collective-permute-start | bytes 884744 | tf_op jit(solution)/shard_map/ppermute | solution.py:289
  30.4 1.5 collective-permute-start.2
  31.9 3.0 %convolution_bitcast_fusion = f32[3,1024]{1,0:T(4,128)S(1)} fusion(f32[513,1024]{1,0:T(8,128)} %constant.130.clone, f32[3,513]{1,0:T(4,128)S(1)} %copy-done), kind=kOutput, calls=%fused_computation | convolution fusion | flops 18911232 | bytes 2119692 | tf_op jit(solution)/shard_map/dot_general | solution.py:194
  36.8 1.4 collective-permute-start.13
  38.2 2.1 %collective-permute-start.14 = (f32[150,256]{1,0:T(8,128)S(1)}, f32[150,256]{1,0:T(8,128)}, u32[]{:S(2)}, u32[]{:S(2)}) collective-permute-start(f32[150,256]{1,0:T(8,128)S(1)} %pad_maximum_fusion.3), channel_id=1, source_target_pairs={{0,35},{1,32},{2,33},{3,34},{32,67},{33,64},{34,65},{35,66},{64,99... | collective-permute-start | bytes 460808 | tf_op jit(solution)/shard_map/ppermute | solution.py:289
  40.9 7.5 %collective-permute-done.13.q0 = f32[150,256]{1,0:T(8,128)} collective-permute-done((f32[150,256]{1,0:T(8,128)S(1)}, f32[150,256]{1,0:T(8,128)}, u32[]{:S(2)}, u32[]{:S(2)}) %collective-permute-start.13) | collective-permute-done | bytes 153632 | tf_op jit(solution)/shard_map/ppermute | solution.py:289
  48.4 17.3 %collective-permute-done.14.q1 = f32[150,256]{1,0:T(8,128)} collective-permute-done((f32[150,256]{1,0:T(8,128)S(1)}, f32[150,256]{1,0:T(8,128)}, u32[]{:S(2)}, u32[]{:S(2)}) %collective-permute-start.14) | collective-permute-done | bytes 153632 | tf_op jit(solution)/shard_map/ppermute | solution.py:289
  67.0 11.0 %collective-permute-done.15.q2 = f32[150,256]{1,0:T(8,128)S(1)} collective-permute-done((f32[150,256]{1,0:T(8,128)S(1)}, f32[150,256]{1,0:T(8,128)S(1)}, u32[]{:S(2)}, u32[]{:S(2)}) %collective-permute-start.15) | collective-permute-done | bytes 153632 | tf_op jit(solution)/shard_map/ppermute | solution.py:289
  78.0 5.9 %collective-permute-start.10 = (f32[3,96,256]{2,1,0:T(8,128)}, f32[3,96,256]{2,1,0:T(8,128)}, u32[]{:S(2)}, u32[]{:S(2)}) collective-permute-start(f32[3,96,256]{2,1,0:T(8,128)} %collective-permute-done.3.p3), channel_id=1, source_target_pairs={{0,224},{32,0},{64,32},{96,64},{128,96},{160,128},{192,160},{224,1... | collective-permute-start | bytes 884744 | tf_op jit(solution)/shard_map/ppermute | solution.py:335
  88.2 1.6 slice.136
  89.9 1.5 slice.137
  91.4 1.5 slice.138
  93.0 1.5 slice.139
  94.5 19.2 %shard_map.55.f_ref = f32[3,64,1024]{2,1,0:T(8,128)S(1)} custom-call(f32[90]{0:T(128)S(1)} %sine_multiply_fusion.1.f_ref, f32[3,96,256]{2,1,0:T(8,128)} %collective-permute-done.p0, f32[3,96,256]{2,1,0:T(8,128)} %collective-permute-done.1.p1, f32[3,96,256]{2,1,0:T(8,128)} %collective-permute-done.2.p2, f32[3,96,256]{2,1,0:T(8,128)} %collective-permute-done.3.p3), custom_call_target="tpu_custom_call" | custom-call | flops 45342720 | bytes 2015232 | tf_op jit(solution)/shard_map/pallas_call | solution.py:151
  114.5 23.7 %shard_map.58.f_ref = f32[3,64,1024]{2,1,0:T(8,128)S(1)} custom-call(f32[108]{0:T(128)S(1)} %copy-done.15, f32[3,96,256]{2,1,0:T(8,128)} %collective-permute-done.p0, f32[3,96,256]{2,1,0:T(8,128)} %collective-permute-done.1.p1, f32[3,96,256]{2,1,0:T(8,128)} %collective-permute-done.2.p2, f32[3,96,256]{2,1,0:T(8,128)} %collective-permute-done.3.p3, ...), custom_call_target="tpu_custom_call" | custom-call | flops 55296000 | bytes 2457600 | tf_op jit(solution)/shard_map/pallas_call | solution.py:151
  139.2 1.3 slice.119
  141.8 2.8 %shard_map.57 = (f32[3,64,256]{2,1,0:T(8,128)S(1)}, f32[3,64,256]{2,1,0:T(8,128)S(1)}, f32[3,64,256]{2,1,0:T(8,128)S(1)}, f32[3,64,256]{2,1,0:T(8,128)S(1)}) custom-call(s32[1]{0:T(128)} %bitcast.flag, f32[3,64,1024]{2,1,0:T(8,128)S(1)} %copy-done.2, f32[4,3,16,1024]{3,2,1,0:T(8,128)S(1)} %bitcast.66, f32[3,96,256]{2,1,0:T(8,128)} %collective-permute-done.7.refs_0_, ...), custom_call_target="tpu_custom_call" | custom-call | flops 452984832 | bytes 8388608 | tf_op jit(solution)/shard_map/pallas_call | solution.py:262
  144.6 2.5 %collective-permute-start.21 = (f32[3,64,256]{2,1,0:T(8,128)S(1)}, f32[3,64,256]{2,1,0:T(8,128)S(1)}, u32[]{:S(2)}, u32[]{:S(2)}) collective-permute-start(f32[3,64,256]{2,1,0:T(8,128)S(1)} %get-tuple-element.27), channel_id=1, source_target_pairs={{0,1},{1,2},{2,3},{3,0},{4,5},{5,6},{6,7},{7,4},{8,9},{9,10},{10,1... | collective-permute-start | bytes 589832 | tf_op jit(solution)/shard_map/ppermute | solution.py:293
  147.3 2.7 %shard_map.59 = (f32[3,64,256]{2,1,0:T(8,128)S(1)}, f32[3,64,256]{2,1,0:T(8,128)S(1)}, f32[3,64,256]{2,1,0:T(8,128)S(1)}, f32[3,64,256]{2,1,0:T(8,128)S(1)}) custom-call(s32[1]{0:T(128)} %bitcast.flag, f32[3,64,1024]{2,1,0:T(8,128)S(1)} %copy-done.4, f32[4,3,16,1024]{3,2,1,0:T(8,128)S(1)} %pad_maximum_fusion.b_ref, ...), custom_call_target="tpu_custom_call" | custom-call | flops 452984832 | bytes 8388608 | tf_op jit(solution)/shard_map/pallas_call | solution.py:262
  149.9 1.5 collective-permute-start.22
  151.5 2.6 %collective-permute-start.23 = (f32[3,64,256]{2,1,0:T(8,128)S(1)}, f32[3,64,256]{2,1,0:T(8,128)S(1)}, u32[]{:S(2)}, u32[]{:S(2)}) collective-permute-start(f32[3,64,256]{2,1,0:T(8,128)S(1)} %get-tuple-element.29), channel_id=1, source_target_pairs={{0,2},{1,3},{2,0},{3,1},{4,6},{5,7},{6,4},{7,5},{8,10},{9,11},{10,... | collective-permute-start | bytes 589832 | tf_op jit(solution)/shard_map/ppermute | solution.py:293
  154.1 3.3 %collective-permute-start.24 = (f32[3,64,256]{2,1,0:T(8,128)S(1)}, f32[3,64,256]{2,1,0:T(8,128)S(1)}, u32[]{:S(2)}, u32[]{:S(2)}) collective-permute-start(f32[3,64,256]{2,1,0:T(8,128)S(1)} %get-tuple-element.30), channel_id=1, source_target_pairs={{0,2},{1,3},{2,0},{3,1},{4,6},{5,7},{6,4},{7,5},{8,10},{9,11},{10,... | collective-permute-start | bytes 589832 | tf_op jit(solution)/shard_map/ppermute | solution.py:293
  157.4 2.7 %collective-permute-start.25 = (f32[3,64,256]{2,1,0:T(8,128)S(1)}, f32[3,64,256]{2,1,0:T(8,128)S(1)}, u32[]{:S(2)}, u32[]{:S(2)}) collective-permute-start(f32[3,64,256]{2,1,0:T(8,128)S(1)} %get-tuple-element.31), channel_id=1, source_target_pairs={{0,3},{1,0},{2,1},{3,2},{4,7},{5,4},{6,5},{7,6},{8,11},{9,8},{10,9... | collective-permute-start | bytes 589832 | tf_op jit(solution)/shard_map/ppermute | solution.py:293
  160.9 8.3 %collective-permute-done.22 = f32[3,64,256]{2,1,0:T(8,128)S(1)} collective-permute-done((f32[3,64,256]{2,1,0:T(8,128)S(1)}, f32[3,64,256]{2,1,0:T(8,128)S(1)}, u32[]{:S(2)}, u32[]{:S(2)}) %collective-permute-start.22) | collective-permute-done | bytes 196640 | tf_op jit(solution)/shard_map/ppermute | solution.py:293
  169.2 6.4 %collective-permute-done.23 = f32[3,64,256]{2,1,0:T(8,128)S(1)} collective-permute-done((f32[3,64,256]{2,1,0:T(8,128)S(1)}, f32[3,64,256]{2,1,0:T(8,128)S(1)}, u32[]{:S(2)}, u32[]{:S(2)}) %collective-permute-start.23) | collective-permute-done | bytes 196640 | tf_op jit(solution)/shard_map/ppermute | solution.py:293
  175.6 6.3 %collective-permute-done.24 = f32[3,64,256]{2,1,0:T(8,128)S(1)} collective-permute-done((f32[3,64,256]{2,1,0:T(8,128)S(1)}, f32[3,64,256]{2,1,0:T(8,128)S(1)}, u32[]{:S(2)}, u32[]{:S(2)}) %collective-permute-start.24) | collective-permute-done | bytes 196640 | tf_op jit(solution)/shard_map/ppermute | solution.py:293
  181.9 6.9 %collective-permute-done.25 = f32[3,64,256]{2,1,0:T(8,128)S(1)} collective-permute-done((f32[3,64,256]{2,1,0:T(8,128)S(1)}, f32[3,64,256]{2,1,0:T(8,128)S(1)}, u32[]{:S(2)}, u32[]{:S(2)}) %collective-permute-start.25) | collective-permute-done | bytes 196640 | tf_op jit(solution)/shard_map/ppermute | solution.py:293
  188.8 4.1 %collective-permute-done.26 = f32[3,64,256]{2,1,0:T(8,128)S(1)} collective-permute-done((f32[3,64,256]{2,1,0:T(8,128)S(1)}, f32[3,64,256]{2,1,0:T(8,128)S(1)}, u32[]{:S(2)}, u32[]{:S(2)}) %collective-permute-start.26) | collective-permute-done | bytes 196640 | tf_op jit(solution)/shard_map/ppermute | solution.py:293
  (118 shorter events, 18.6 us)
Async XLA Ops:
  6.5 25.4 %copy-start = (f32[3,513]{1,0:T(4,128)S(1)}, f32[3,513]{1,0:T(4,128)}, u32[]{:S(2)}) copy-start(f32[3,513]{1,0:T(4,128)} %param.7) | copy-start | bytes 18472
  6.5 132.6 %all-gather.3.cloned.1.call-start = ((), (), s32[]{:S(2)}) async-start(), calls=%async_computation | async-start | bytes 1769472 | tf_op jit(solution)/shard_map/all_gather | solution.py:321
  7.6 10.2 %collective-permute-start.4 = (f32[3,16,256]{2,1,0:T(8,128)S(1)}, f32[3,16,256]{2,1,0:T(8,128)S(1)}, u32[]{:S(2)}, u32[]{:S(2)}) collective-permute-start(f32[3,16,256]{2,1,0:T(8,128)S(1)} %get-tuple-element.46), channel_id=1, source_target_pairs={{0,3},{1,0},{2,1},{3,2},{4,7},{5,4},{6,5},{7,6},{8,11},{9,8},{10,9... | collective-permute-start | bytes 147464 | tf_op jit(solution)/shard_map/ppermute | solution.py:293
  13.9 8.3 %collective-permute-start.5 = (f32[3,16,256]{2,1,0:T(8,128)S(1)}, f32[3,16,256]{2,1,0:T(8,128)S(1)}, u32[]{:S(2)}, u32[]{:S(2)}) collective-permute-start(f32[3,16,256]{2,1,0:T(8,128)S(1)} %get-tuple-element.48), channel_id=1, source_target_pairs={{0,2},{1,3},{2,0},{3,1},{4,6},{5,7},{6,4},{7,5},{8,10},{9,11},{10,... | collective-permute-start | bytes 147464 | tf_op jit(solution)/shard_map/ppermute | solution.py:293
  14.9 7.3 %collective-permute-start.6 = (f32[3,16,256]{2,1,0:T(8,128)S(1)}, f32[3,16,256]{2,1,0:T(8,128)S(1)}, u32[]{:S(2)}, u32[]{:S(2)}) collective-permute-start(f32[3,16,256]{2,1,0:T(8,128)S(1)} %get-tuple-element.47), channel_id=1, source_target_pairs={{0,1},{1,2},{2,3},{3,0},{4,5},{5,6},{6,7},{7,4},{8,9},{9,10},{10,1... | collective-permute-start | bytes 147464 | tf_op jit(solution)/shard_map/ppermute | solution.py:293
  24.7 10.3 %collective-permute-start.11 = (f32[3,9,256]{2,1,0:T(8,128)}, f32[3,9,256]{2,1,0:T(8,128)}, u32[]{:S(2)}, u32[]{:S(2)}) collective-permute-start(f32[3,9,256]{2,1,0:T(8,128)} %get-tuple-element.44), channel_id=1, source_target_pairs={{0,4},{4,8},{8,12},{12,16},{16,20},{20,24},{24,28},{28,0},{1,5},{5... | collective-permute-start | bytes 82952 | tf_op jit(solution)/shard_map/ppermute | solution.py:307
  25.9 9.9 %collective-permute-start.12 = (f32[3,9,256]{2,1,0:T(8,128)S(1)}, f32[3,9,256]{2,1,0:T(8,128)}, u32[]{:S(2)}, u32[]{:S(2)}) collective-permute-start(f32[3,9,256]{2,1,0:T(8,128)S(1)} %get-tuple-element.38), channel_id=1, source_target_pairs={{0,28},{4,0},{8,4},{12,8},{16,12},{20,16},{24,20},{28,24},{1,29},{... | collective-permute-start | bytes 82952 | tf_op jit(solution)/shard_map/ppermute | solution.py:308
  26.8 57.1 %collective-permute-start = (f32[3,96,256]{2,1,0:T(8,128)S(1)}, f32[3,96,256]{2,1,0:T(8,128)}, u32[]{:S(2)}, u32[]{:S(2)}) collective-permute-start(f32[3,96,256]{2,1,0:T(8,128)S(1)} %get-tuple-element.52), channel_id=1, source_target_pairs={{0,32},{1,33},{2,34},{3,35},{32,64},{33,65},{34,66},{35,67},{64,96... | collective-permute-start | bytes 884744 | tf_op jit(solution)/shard_map/ppermute | solution.py:289
  26.8 57.1 %collective-permute-start.1 = (f32[3,96,256]{2,1,0:T(8,128)S(1)}, f32[3,96,256]{2,1,0:T(8,128)}, u32[]{:S(2)}, u32[]{:S(2)}) collective-permute-start(f32[3,96,256]{2,1,0:T(8,128)S(1)} %get-tuple-element.51), channel_id=1, source_target_pairs={{0,35},{1,32},{2,33},{3,34},{32,67},{33,64},{34,65},{35,66},{64,99... | collective-permute-start | bytes 884744 | tf_op jit(solution)/shard_map/ppermute | solution.py:289
  30.4 53.6 %collective-permute-start.2 = (f32[3,96,256]{2,1,0:T(8,128)S(1)}, f32[3,96,256]{2,1,0:T(8,128)}, u32[]{:S(2)}, u32[]{:S(2)}) collective-permute-start(f32[3,96,256]{2,1,0:T(8,128)S(1)} %get-tuple-element.50), channel_id=1, source_target_pairs={{0,34},{1,35},{2,32},{3,33},{32,66},{33,67},{34,64},{35,65},{64,98... | collective-permute-start | bytes 884744 | tf_op jit(solution)/shard_map/ppermute | solution.py:289
  34.9 49.1 %copy-start.19 = (s32[108]{0:T(128)S(1)}, s32[108]{0:T(128)}, u32[]{:S(2)}) copy-start(s32[108]{0:T(128)} %constant.131.clone) | copy-start | bytes 1300
  36.8 11.6 %collective-permute-start.13 = (f32[150,256]{1,0:T(8,128)S(1)}, f32[150,256]{1,0:T(8,128)}, u32[]{:S(2)}, u32[]{:S(2)}) collective-permute-start(f32[150,256]{1,0:T(8,128)S(1)} %pad_maximum_fusion.2), channel_id=1, source_target_pairs={{0,32},{1,33},{2,34},{3,35},{32,64},{33,65},{34,66},{35,67},{64,96... | collective-permute-start | bytes 460808 | tf_op jit(solution)/shard_map/ppermute | solution.py:289
  38.2 27.5 %collective-permute-start.14 = (f32[150,256]{1,0:T(8,128)S(1)}, f32[150,256]{1,0:T(8,128)}, u32[]{:S(2)}, u32[]{:S(2)}) collective-permute-start(f32[150,256]{1,0:T(8,128)S(1)} %pad_maximum_fusion.3), channel_id=1, source_target_pairs={{0,35},{1,32},{2,33},{3,34},{32,67},{33,64},{34,65},{35,66},{64,99... | collective-permute-start | bytes 460808 | tf_op jit(solution)/shard_map/ppermute | solution.py:289
  48.4 29.6 %collective-permute-start.3 = (f32[3,96,256]{2,1,0:T(8,128)S(1)}, f32[3,96,256]{2,1,0:T(8,128)}, u32[]{:S(2)}, u32[]{:S(2)}) collective-permute-start(f32[3,96,256]{2,1,0:T(8,128)S(1)} %get-tuple-element.49), channel_id=1, source_target_pairs={{0,33},{1,34},{2,35},{3,32},{32,65},{33,66},{34,67},{35,64},{64,97... | collective-permute-start | bytes 884744 | tf_op jit(solution)/shard_map/ppermute | solution.py:289
  65.8 12.3 %collective-permute-start.15 = (f32[150,256]{1,0:T(8,128)S(1)}, f32[150,256]{1,0:T(8,128)S(1)}, u32[]{:S(2)}, u32[]{:S(2)}) collective-permute-start(f32[150,256]{1,0:T(8,128)S(1)} %pad_maximum_fusion.4), channel_id=1, source_target_pairs={{0,34},{1,35},{2,32},{3,33},{32,66},{33,67},{34,64},{35,65},{64,98... | collective-permute-start | bytes 460808 | tf_op jit(solution)/shard_map/ppermute | solution.py:289
  78.0 14.9 %collective-permute-start.16 = (f32[150,256]{1,0:T(8,128)}, f32[150,256]{1,0:T(8,128)}, u32[]{:S(2)}, u32[]{:S(2)}) collective-permute-start(f32[150,256]{1,0:T(8,128)} %pad_maximum_fusion.5), channel_id=1, source_target_pairs={{0,33},{1,34},{2,35},{3,32},{32,65},{33,66},{34,67},{35,64},{64,97... | collective-permute-start | bytes 460808 | tf_op jit(solution)/shard_map/ppermute | solution.py:289
  78.0 62.5 %collective-permute-start.10 = (f32[3,96,256]{2,1,0:T(8,128)}, f32[3,96,256]{2,1,0:T(8,128)}, u32[]{:S(2)}, u32[]{:S(2)}) collective-permute-start(f32[3,96,256]{2,1,0:T(8,128)} %collective-permute-done.3.p3), channel_id=1, source_target_pairs={{0,224},{32,0},{64,32},{96,64},{128,96},{160,128},{192,160},{224,1... | collective-permute-start | bytes 884744 | tf_op jit(solution)/shard_map/ppermute | solution.py:335
  83.9 56.6 %collective-permute-start.7 = (f32[3,96,256]{2,1,0:T(8,128)}, f32[3,96,256]{2,1,0:T(8,128)}, u32[]{:S(2)}, u32[]{:S(2)}) collective-permute-start(f32[3,96,256]{2,1,0:T(8,128)} %collective-permute-done.p0), channel_id=1, source_target_pairs={{0,224},{32,0},{64,32},{96,64},{128,96},{160,128},{192,160},{224,1... | collective-permute-start | bytes 884744 | tf_op jit(solution)/shard_map/ppermute | solution.py:335
  84.0 56.7 %collective-permute-start.8 = (f32[3,96,256]{2,1,0:T(8,128)}, f32[3,96,256]{2,1,0:T(8,128)}, u32[]{:S(2)}, u32[]{:S(2)}) collective-permute-start(f32[3,96,256]{2,1,0:T(8,128)} %collective-permute-done.1.p1), channel_id=1, source_target_pairs={{0,224},{32,0},{64,32},{96,64},{128,96},{160,128},{192,160},{224,1... | collective-permute-start | bytes 884744 | tf_op jit(solution)/shard_map/ppermute | solution.py:335
  84.0 56.6 %collective-permute-start.9 = (f32[3,96,256]{2,1,0:T(8,128)}, f32[3,96,256]{2,1,0:T(8,128)}, u32[]{:S(2)}, u32[]{:S(2)}) collective-permute-start(f32[3,96,256]{2,1,0:T(8,128)} %collective-permute-done.2.p2), channel_id=1, source_target_pairs={{0,224},{32,0},{64,32},{96,64},{128,96},{160,128},{192,160},{224,1... | collective-permute-start | bytes 884744 | tf_op jit(solution)/shard_map/ppermute | solution.py:335
  84.6 30.0 %copy-start.15 = (f32[108]{0:T(128)S(1)}, f32[108]{0:T(128)}, u32[]{:S(2)}) copy-start(f32[108]{0:T(128)} %sine_multiply_fusion.f_ref) | copy-start | bytes 1300
  86.0 28.6 %copy-start.12 = (f32[150,256]{1,0:T(8,128)S(1)}, f32[150,256]{1,0:T(8,128)}, u32[]{:S(2)}) copy-start(f32[150,256]{1,0:T(8,128)} %copy-done.11) | copy-start | bytes 460804
  92.9 54.3 %collective-permute-start.17 = (f32[96,256]{1,0:T(8,128)}, f32[96,256]{1,0:T(8,128)}, u32[]{:S(2)}, u32[]{:S(2)}) collective-permute-start(f32[96,256]{1,0:T(8,128)} %slice.136), channel_id=1, source_target_pairs={{0,224},{32,0},{64,32},{96,64},{128,96},{160,128},{192,160},{224,1... | collective-permute-start | bytes 294920 | tf_op jit(solution)/shard_map/ppermute | solution.py:336
  140.5 6.7 %collective-permute-start.18 = (f32[96,256]{1,0:T(8,128)}, f32[96,256]{1,0:T(8,128)S(1)}, u32[]{:S(2)}, u32[]{:S(2)}) collective-permute-start(f32[96,256]{1,0:T(8,128)} %slice.137), channel_id=1, source_target_pairs={{0,224},{32,0},{64,32},{96,64},{128,96},{160,128},{192,160},{224,1... | collective-permute-start | bytes 294920 | tf_op jit(solution)/shard_map/ppermute | solution.py:336
  140.6 6.7 %collective-permute-start.19 = (f32[96,256]{1,0:T(8,128)}, f32[96,256]{1,0:T(8,128)S(1)}, u32[]{:S(2)}, u32[]{:S(2)}) collective-permute-start(f32[96,256]{1,0:T(8,128)} %slice.138), channel_id=1, source_target_pairs={{0,224},{32,0},{64,32},{96,64},{128,96},{160,128},{192,160},{224,1... | collective-permute-start | bytes 294920 | tf_op jit(solution)/shard_map/ppermute | solution.py:336
  140.6 6.6 %collective-permute-start.20 = (f32[96,256]{1,0:T(8,128)}, f32[96,256]{1,0:T(8,128)S(1)}, u32[]{:S(2)}, u32[]{:S(2)}) collective-permute-start(f32[96,256]{1,0:T(8,128)} %slice.139), channel_id=1, source_target_pairs={{0,224},{32,0},{64,32},{96,64},{128,96},{160,128},{192,160},{224,1... | collective-permute-start | bytes 294920 | tf_op jit(solution)/shard_map/ppermute | solution.py:336
  144.6 15.7 %collective-permute-start.21 = (f32[3,64,256]{2,1,0:T(8,128)S(1)}, f32[3,64,256]{2,1,0:T(8,128)S(1)}, u32[]{:S(2)}, u32[]{:S(2)}) collective-permute-start(f32[3,64,256]{2,1,0:T(8,128)S(1)} %get-tuple-element.27), channel_id=1, source_target_pairs={{0,1},{1,2},{2,3},{3,0},{4,5},{5,6},{6,7},{7,4},{8,9},{9,10},{10,1... | collective-permute-start | bytes 589832 | tf_op jit(solution)/shard_map/ppermute | solution.py:293
  149.9 19.2 %collective-permute-start.22 = (f32[3,64,256]{2,1,0:T(8,128)S(1)}, f32[3,64,256]{2,1,0:T(8,128)S(1)}, u32[]{:S(2)}, u32[]{:S(2)}) collective-permute-start(f32[3,64,256]{2,1,0:T(8,128)S(1)} %get-tuple-element.28), channel_id=1, source_target_pairs={{0,1},{1,2},{2,3},{3,0},{4,5},{5,6},{6,7},{7,4},{8,9},{9,10},{10,1... | collective-permute-start | bytes 589832 | tf_op jit(solution)/shard_map/ppermute | solution.py:293
  151.5 24.2 %collective-permute-start.23 = (f32[3,64,256]{2,1,0:T(8,128)S(1)}, f32[3,64,256]{2,1,0:T(8,128)S(1)}, u32[]{:S(2)}, u32[]{:S(2)}) collective-permute-start(f32[3,64,256]{2,1,0:T(8,128)S(1)} %get-tuple-element.29), channel_id=1, source_target_pairs={{0,2},{1,3},{2,0},{3,1},{4,6},{5,7},{6,4},{7,5},{8,10},{9,11},{10,... | collective-permute-start | bytes 589832 | tf_op jit(solution)/shard_map/ppermute | solution.py:293
  154.1 27.8 %collective-permute-start.24 = (f32[3,64,256]{2,1,0:T(8,128)S(1)}, f32[3,64,256]{2,1,0:T(8,128)S(1)}, u32[]{:S(2)}, u32[]{:S(2)}) collective-permute-start(f32[3,64,256]{2,1,0:T(8,128)S(1)} %get-tuple-element.30), channel_id=1, source_target_pairs={{0,2},{1,3},{2,0},{3,1},{4,6},{5,7},{6,4},{7,5},{8,10},{9,11},{10,... | collective-permute-start | bytes 589832 | tf_op jit(solution)/shard_map/ppermute | solution.py:293
  157.4 31.4 %collective-permute-start.25 = (f32[3,64,256]{2,1,0:T(8,128)S(1)}, f32[3,64,256]{2,1,0:T(8,128)S(1)}, u32[]{:S(2)}, u32[]{:S(2)}) collective-permute-start(f32[3,64,256]{2,1,0:T(8,128)S(1)} %get-tuple-element.31), channel_id=1, source_target_pairs={{0,3},{1,0},{2,1},{3,2},{4,7},{5,4},{6,5},{7,6},{8,11},{9,8},{10,9... | collective-permute-start | bytes 589832 | tf_op jit(solution)/shard_map/ppermute | solution.py:293
  160.3 32.7 %collective-permute-start.26 = (f32[3,64,256]{2,1,0:T(8,128)S(1)}, f32[3,64,256]{2,1,0:T(8,128)S(1)}, u32[]{:S(2)}, u32[]{:S(2)}) collective-permute-start(f32[3,64,256]{2,1,0:T(8,128)S(1)} %get-tuple-element.32), channel_id=1, source_target_pairs={{0,3},{1,0},{2,1},{3,2},{4,7},{5,4},{6,5},{7,6},{8,11},{9,8},{10,9... | collective-permute-start | bytes 589832 | tf_op jit(solution)/shard_map/ppermute | solution.py:293
  (17 other events, 53.4 us)
Sparse Core Ops, SparseCore 0:
  23.1 31.6 all-gather.2

commit v2 on v1

v2 whole, which is shorter than its diff:
```python
import functools

import numpy as np
import jax
import jax.numpy as jnp
from jax import lax
from jax.experimental import pallas as pl
from jax.experimental.pallas import tpu as pltpu
from jax.sharding import PartitionSpec as P

NLON = 1024
STEPS = 3
time_step = 0.5
coriolis_peak = 0.4

SUB = 8
LON = 4
ROWS = 128
HALO = 3 * STEPS
CHUNK = ROWS // 2
PART = ROWS // SUB
SENT = 440
TILES = CHUNK + 2 * HALO
GROUP = 16
SPARE = 2 * GROUP
F32 = jnp.float32
BF16 = jnp.bfloat16


def vmem_spec():
    return pl.BlockSpec(memory_space=pltpu.VMEM)


def smem_spec():
    return pl.BlockSpec(memory_space=pltpu.SMEM)


def hbm_spec():
    return pl.BlockSpec(memory_space=pltpu.HBM)


def call(kernel, outs, in_specs, out_specs, scratch, mib, **kwargs):
    return pl.pallas_call(
        kernel,
        out_shape=outs,
        in_specs=in_specs,
        out_specs=out_specs,
        scratch_shapes=scratch,
        compiler_params=pltpu.CompilerParams(vmem_limit_bytes=mib << 20),
        cost_estimate=pl.CostEstimate(flops=0, bytes_accessed=1, transcendentals=0),
        **kwargs,
    )


def array(*shape):
    return jax.ShapeDtypeStruct(shape, F32)


def dma_sems(n):
    return pltpu.SemaphoreType.DMA((n,))


def start_all(sem, pairs):
    copies = [pltpu.make_async_copy(a, b, sem.at[n]) for n, (a, b) in enumerate(pairs)]
    for copy in copies:
        copy.start()
    return copies


def aligned(row):
    return pl.multiple_of(row, 16)


def unpack_rows(dst, piece, field, first, count, row0, block):
    done = 0
    while done < count:
        n = min(8, count - done)
        for half in range(2):
            value = piece[first + done : first + done + n, 128 * half : 128 * half + 128]
            start = (row0 + done) * 8 + 2 * block + half
            where = pl.ds(start, n, stride=8) if n > 1 else pl.ds(start, 1)
            dst[field, where, :] = value + 1.0 if field == 0 else value
        done += n


def stage(src, base, dst, f_ref, lo, rows, kind):
    lane = lax.broadcasted_iota(jnp.int32, (8, 128), 1)
    is_first = lane == 0
    is_last = lane == 127

    def neighbours(a):
        up = pltpu.roll(a, 127, 1)
        down = pltpu.roll(a, 1, 1)
        up = jnp.where(is_last, pltpu.roll(up, 7, 0), up)
        down = jnp.where(is_first, pltpu.roll(down, 1, 0), down)
        return up, down

    def body(g, carry):
        row = lo + g * GROUP

        def load(ref, c, k):
            return ref[c, pl.ds(pl.multiple_of((row + k) * 8, 8), 8), :]

        d = [load(src, 0, k) for k in range(-1, GROUP + 1)]
        u = [load(src, 1, k) for k in range(-1, GROUP + 1)]
        v = [load(src, 2, k) for k in range(-1, GROUP + 1)]
        flux = [d[k] * v[k] for k in range(GROUP + 2)]
        for k in range(1, GROUP + 1):
            f = f_ref[row + k - 1]
            d_up, d_down = neighbours(d[k])
            u_up, u_down = neighbours(u[k])
            v_up, v_down = neighbours(v[k])
            t_h = (d_up * u_up - d_down * u_down) + (flux[k + 1] - flux[k - 1])
            t_u = u[k] * (u_up - u_down) + v[k] * ((u[k + 1] - u[k - 1]) - f) + (d_up - d_down)
            t_v = u[k] * ((v_up - v_down) + f) + v[k] * (v[k + 1] - v[k - 1]) + (d[k + 1] - d[k - 1])
            for c, (now, t) in enumerate(((d[k], t_h), (u[k], t_u), (v[k], t_v))):
                new = now - (0.5 * time_step) * t
                if kind == 1:
                    new = 0.75 * load(base, c, k - 1) + 0.25 * new
                elif kind == 2:
                    new = (1.0 / 3.0) * load(base, c, k - 1) + (2.0 / 3.0) * new
                dst[c, pl.ds(pl.multiple_of((row + k - 1) * 8, 8), 8), :] = new
        return carry

    lax.fori_loop(0, -(-rows // GROUP), body, 0)


def model_kernel(second, f_ref, s0, s3, s2, s1, out, *bufs):
    x, b, c, y = bufs
    for block, s in enumerate((s0, s3, s2, s1)):
        for field in range(3):
            row = ROWS * field
            edge = 3 * ROWS + 2 * HALO * field
            if second:
                unpack_rows(x, s, field, row + CHUNK - HALO, 1, 0, block)
                unpack_rows(x, s, field, row + CHUNK - HALO + 1, CHUNK + HALO - 1, 1, block)
                unpack_rows(x, s, field, edge + HALO, HALO, CHUNK + HALO, block)
            else:
                unpack_rows(x, s, field, edge, HALO, 0, block)
                unpack_rows(x, s, field, row, CHUNK + HALO, HALO, block)
    done = 0
    for _ in range(STEPS):
        for kind, (src, base, dst) in enumerate(((x, x, b), (b, x, c), (c, x, y))):
            done += 1
            stage(src, base, dst, f_ref, done, TILES - 2 * done, kind)
        x, y = y, x
    for field in range(3):
        for r in range(0, CHUNK, 8):
            for s in range(8):
                value = x[field, pl.ds((HALO + r) * 8 + s, 8, stride=8), :]
                out[field, r : r + 8, 128 * s : 128 * s + 128] = (
                    value - 1.0 if field == 0 else value
                )


def model_call(second, f, pieces):
    return call(
        functools.partial(model_kernel, second),
        array(3, CHUNK, NLON),
        [smem_spec()] + [vmem_spec()] * 4,
        vmem_spec(),
        [pltpu.VMEM((3, (TILES + SPARE) * 8, 128), F32)] * 4,
        10,
    )(f, *pieces)


def prepare_kernel(t_ref, x, back, b2, b1, b3, b0, last, first, sem):
    rows = x.shape[1]
    pairs = []
    for j, b in ((2, b2), (1, b1), (3, b3), (0, b0)):
        row = aligned(t_ref[j] * ROWS + t_ref[4] * PART)
        pairs.append((back.at[:, pl.ds(row, PART), :], b))
    pairs += [(x.at[:, pl.ds(rows - 16, 16), :], last), (x.at[:, pl.ds(0, 16), :], first)]
    for copy in start_all(sem, pairs):
        copy.wait()


def prepare(t, x, back):
    return call(
        prepare_kernel,
        [array(3, PART, 256)] * 4 + [array(3, 16, 256)] * 2,
        [smem_spec(), hbm_spec(), hbm_spec()],
        [vmem_spec()] * 6,
        [dma_sems(6)],
        60,
    )(t, x, back)


def send_kernel(t_ref, x, above, below, s2, s1, s3, s0, edges, sem):
    rows = x.shape[1]
    pairs = []
    for q in range(1, LON):
        pairs.append((x.at[:, pl.ds(ROWS * q - 16, 32), :], edges.at[q]))
    pairs += [
        (above, edges.at[0, :, pl.ds(0, 16), :]),
        (x.at[:, pl.ds(rows - 16, 16), :], edges.at[LON, :, pl.ds(0, 16), :]),
        (below, edges.at[LON, :, pl.ds(16, 16), :]),
    ]
    small = len(pairs)
    for j, s in ((2, s2), (1, s1), (3, s3), (0, s0)):
        for c in range(3):
            row = aligned(t_ref[j] * ROWS)
            pairs.append((x.at[c, pl.ds(row, ROWS), :], s.at[pl.ds(ROWS * c, ROWS), :]))
    copies = start_all(sem, pairs)
    for copy in copies[:small]:
        copy.wait()
    for j, s in ((2, s2), (1, s1), (3, s3), (0, s0)):
        for c in range(3):
            edge = 3 * ROWS + 2 * HALO * c
            s[edge : edge + HALO, :] = edges[t_ref[j], c, 16 - HALO : 16, :]
            s[edge + HALO : edge + 2 * HALO, :] = edges[t_ref[j] + 1, c, 16 : 16 + HALO, :]
    for copy in copies[small:]:
        copy.wait()


def send(t, x, above, below):
    return call(
        send_kernel,
        [array(SENT, 256)] * 4,
        [smem_spec()] + [hbm_spec()] * 3,
        [vmem_spec()] * 4,
        [pltpu.VMEM((LON + 1, 3, 32, 256), F32), dma_sems(18)],
        6,
    )(t, x, above, below)


def place_kernel(first, t_ref, o0, r1, r2, r3, *refs):
    out, sem = refs[-2:]
    pairs = [
        (r, out.at[:, pl.ds(aligned(t_ref[5 + j] * ROWS + first), CHUNK), :])
        for j, r in enumerate((o0, r1, r2, r3))
    ]
    for copy in start_all(sem, pairs):
        copy.wait()


def place(t, pieces, rows, begun=None):
    extra = [] if begun is None else [begun]
    return call(
        functools.partial(place_kernel, CHUNK if extra else 0),
        [array(3, rows, 256)],
        [smem_spec()] + [hbm_spec()] * (4 + len(extra)),
        [hbm_spec()],
        [dma_sems(4)],
        2,
        input_output_aliases={5: 0} if extra else {},
    )(t, *pieces, *extra)[0]


def cosine_table():
    m = np.arange(NLON // 2 + 1)
    n = np.arange(NLON)
    factor = np.where((m == 0) | (m == NLON // 2), 1.0, 2.0) / NLON
    angle = 2.0 * np.pi / NLON * ((m[:, None] * n[None, :]) % NLON)
    return (factor[:, None] * np.cos(angle)).astype(np.float32)


def split(x):
    high = x.astype(BF16)
    return high, (x - high.astype(F32)).astype(BF16)


def toeplitz(row, size, sign):
    full = pltpu.roll(jnp.broadcast_to(row, (size, size)), 0, 1, stride=1, stride_axis=0)
    if sign < 0:
        c = lax.broadcasted_iota(jnp.int32, (size, size), 0)
        r = lax.broadcasted_iota(jnp.int32, (size, size), 1)
        full = jnp.where(r < c, -full, full)
    return full


def weighting_rows(variances):
    k = jnp.dot(variances, jnp.asarray(cosine_table()), precision=lax.Precision.HIGHEST)
    k0, k1, k2, k3 = (k[:, 256 * j : 256 * j + 256] for j in range(4))
    even = (k0 + k2) * 0.25
    odd = (k1 + k3) * 0.25
    return even + odd, even - odd, (k[:, :512] - k[:, 512:]) * 0.5


def dot3(x, high, low):
    n = x.shape[0]
    xh, xl = split(x)
    y = jnp.dot(jnp.concatenate([xh, xl], axis=0), high, preferred_element_type=F32)
    return y[:n] + y[n:] + jnp.dot(xh, low, preferred_element_type=F32)


def weight_kernel(half, flag, f_ref, a_ref, b_ref, r_ref, back, w0, w3, w2, w1, *refs):
    outs = refs[:4]
    back_v, sem = refs[4:]
    parts = CHUNK // PART
    copies = start_all(sem, [(back.at[parts * half + n], back_v.at[n]) for n in range(parts)])
    start = flag[0] != 0
    for c in range(3):
        a = split(toeplitz(a_ref[c : c + 1, :], 256, 1))
        b = split(toeplitz(b_ref[c : c + 1, :], 256, -1))
        r = split(toeplitz(r_ref[c : c + 1, :], 512, -1))
        if c == 0:
            for copy in copies:
                copy.wait()
        d = []
        for block, own in enumerate((w0, w3, w2, w1)):
            rows = jnp.concatenate([back_v[n, block, c] for n in range(parts)], axis=0)
            prev = jnp.where(start, rows, f_ref[c, :, 256 * block : 256 * block + 256])
            row = ROWS * c + CHUNK * half
            d.append(own[row : row + CHUNK, :] - prev)
        even, odd = d[0] + d[2], d[1] + d[3]
        x = dot3(even + odd, *a)
        y = dot3(even - odd, *b)
        w = dot3(jnp.concatenate([d[0] - d[2], d[1] - d[3]], axis=1), *r)
        p, q = x + y, x - y
        outs[0][c] = p + w[:, :256]
        outs[1][c] = q + w[:, 256:]
        outs[2][c] = p - w[:, :256]
        outs[3][c] = q - w[:, 256:]


def weight_call(half, flag, f, back, own, rows):
    parts = CHUNK // PART
    return call(
        functools.partial(weight_kernel, half),
        [array(3, CHUNK, 256)] * 4,
        [smem_spec()] + [vmem_spec()] * 4 + [hbm_spec()] + [vmem_spec()] * 4,
        [vmem_spec()] * 4,
        [pltpu.VMEM((parts, 4, 3, PART, 256), F32), dma_sems(parts)],
        10,
    )(flag, f, *rows, back, *own)


def coriolis_rows(total, first, offsets):
    index = (first + offsets).astype(F32)
    return 2.0 * coriolis_peak * jnp.sin(2.0 * jnp.pi * (index + 0.5) / total)


def ring(count, shift):
    return [(i, (i + shift) % count) for i in range(count)]


def to_next(value, j):
    pairs = [
        (s * LON + a, ((s + 1) % SUB) * LON + (a + j) % LON)
        for s in range(SUB)
        for a in range(LON)
    ]
    return lax.ppermute(value, ("sub", "lon"), pairs)


def to_lon(value, j):
    return lax.ppermute(value, "lon", ring(LON, j))


ORDER = (0, 3, 2, 1)


def shards(segment_launch_values, initial_backdrop, spectral_inverse_variances):
    x = segment_launch_values[0]
    sub, lat, lon = (lax.axis_index(n) for n in ("sub", "lat", "lon"))
    tile_rows = x.shape[1]
    total = tile_rows * lax.axis_size("lat")
    t = jnp.stack(
        [lax.rem(lon + j, LON) for j in range(LON)]
        + [sub]
        + [lax.rem(lon - j + LON, LON) for j in range(LON)]
    )

    *parts, last, first = prepare(t, x, initial_backdrop)
    above = lax.ppermute(last, "lat", ring(8, 1))
    below = lax.ppermute(first, "lat", ring(8, -1))
    b2, b1, b3 = (to_lon(v, j) for v, j in zip(parts, (2, 1, 3)))
    back = lax.all_gather(jnp.stack([parts[3], b3, b2, b1]), "sub")

    flag = (sub == 0).astype(jnp.int32).reshape(1)
    first_row = lat * tile_rows + lon * ROWS
    offsets = jnp.arange(TILES + SPARE) - HALO
    f1 = coriolis_rows(total, first_row, offsets)
    f2 = coriolis_rows(total, first_row, offsets + CHUNK)
    rows = weighting_rows(spectral_inverse_variances)
    above, *tied = lax.optimization_barrier((above, f1, f2, flag, *rows))
    f1, f2, flag, *rows = tied

    sent = send(t, x, above, below)
    s2, s1, s3, s0 = (to_next(v, j) for v, j in zip(sent, (2, 1, 3, 0)))
    come = [s0, s3, s2, s1]
    own = [lax.ppermute(v, "sub", ring(SUB, -1)) for v in come]

    m1 = model_call(False, f1, come)
    o1 = weight_call(0, flag, m1, back, own, rows)
    r1 = [to_lon(o1[j], j) if j else o1[j] for j in range(LON)]
    f2, *o1 = lax.optimization_barrier((f2, *o1))
    m2 = model_call(True, f2, come)
    o2 = weight_call(1, flag, m2, back, own, rows)
    r2 = [to_lon(o2[j], j) if j else o2[j] for j in range(LON)]
    return place(t, r2, tile_rows, place(t, r1, tile_rows))[None]


def solution(mesh):
    return jax.shard_map(
        shards,
        mesh=mesh,
        in_specs=(P("sub", None, "lat", "lon"), P(None, "lat", "lon"), P()),
        out_specs=P("sub", None, "lat", "lon"),
        check_vma=False,
    )
```

time: 205 us -> 150 us (0.73); the launches traced: 202 us -> 150 us
  Pallas kernels: 49 us -> 30.7 us
  local copies, waits for them, and re-layouts: 18.4 us -> 2.07 us
  waiting for transfers between devices: 72.4 us -> 61.4 us
  other arithmetic: 4.96 us -> 1.56 us
  starting transfers between devices: 40 us -> 37.5 us
    ppermute x9, waiting for transfers between devices: 36.5 us -> 18.1 us  [to_lon(): return lax.ppermute(value, 'lon', ring(LON, j))]
    pallas_call x5 -> x8, Pallas kernels: 49 us -> 30.7 us  [the longest x2 17.6 us: model_call(): call(functools.partial(model_kernel, second), array(3, CHUNK, NLON), [sme...]
    slice x9 -> x0, local copies, waits for them, and re-layouts: 9.31 us -> none  [the longest x4 6.25 us: shards(): q[j][:3 * late]]
    ppermute x10 -> x6, waiting for transfers between devices: 0.03 us -> 7.54 us  [the longest x4 5.01 us: shards(): own = [lax.ppermute(v, 'sub', ring(SUB, -1)) for v in come]]
    unnamed x43 -> x18, local copies, waits for them, and re-layouts: 6.95 us -> 1.44 us
    ppermute x10 -> x6, starting transfers between devices: 8.07 us -> 4.16 us  [the longest x4 2.06 us: shards(): own = [lax.ppermute(v, 'sub', ring(SUB, -1)) for v in come]]
    concatenate x9 -> x0, other arithmetic: 3.17 us -> none  [the longest x3 1.68 us: shards(): edges.append(jnp.concatenate([up, down], axis=1).reshape(6 * HALO, 256))]
    ppermute x8 -> x4, starting transfers between devices: 8.53 us -> 8.74 us  [to_next(): return lax.ppermute(value, ('sub', 'lon'), pairs)]
  transfers between devices with their start and end apart: 28 -> 20, of which waited for: 9 -> 9; matrix products, arithmetic and copies ran while one was open for 8% -> 2% of each run, Pallas kernels for 24% -> 16%
where the time goes in v2:
time: 150 us
  waiting for transfers between devices  61.4 us (41%)
  starting transfers between devices  37.5 us (25%)
  Pallas kernels  30.7 us (20%)
  between operations  13.6 us (9%)
  matrix products  2.96 us (2%)
  local copies, waits for them, and re-layouts  2.07 us (1%)
  other arithmetic  1.56 us (1%)
    ppermute x4, waiting for transfers between devices, to_next(): return lax.ppermute(value, ('sub', 'lon'), pairs)  35.8 us
    ppermute x9, starting transfers between devices, to_lon(): return lax.ppermute(value, 'lon', ring(LON, j))  24.6 us
    ppermute x9, waiting for transfers between devices, to_lon(): return lax.ppermute(value, 'lon', ring(LON, j))  18.1 us
    pallas_call x2, Pallas kernels, model_call(): call(functools.partial(model_kernel, second), array(3, CHUNK, NLON), [sme...  17.6 us
    ppermute x4, starting transfers between devices, to_next(): return lax.ppermute(value, ('sub', 'lon'), pairs)  8.74 us
    ppermute x4, waiting for transfers between devices, shards(): own = [lax.ppermute(v, 'sub', ring(SUB, -1)) for v in come]  5.01 us
    pallas_call x2, Pallas kernels, weight_call(): call(functools.partial(weight_kernel, half), [array(3, CHUNK, 256)] * 4,...  4.89 us
  transfers between devices with their start and end apart: 20, of which 9 were waited for; matrix products, arithmetic and copies ran while one was open for 2% of the time, Pallas kernels for 16%

profile of v2, /device:TPU:24, one launch (start us, length us, event | category | flops | bytes accessed | tf_op | source)
XLA Modules:
  0.0 149.8 jit_solution(1855038008770026226)
XLA Ops:
  7.2 2.3 %shard_map.46 = (f32[3,16,256]{2,1,0:T(8,128)}, f32[3,16,256]{2,1,0:T(8,128)}, f32[3,16,256]{2,1,0:T(8,128)}, f32[3,16,256]{2,1,0:T(8,128)}, f32[3,16,256]{2,1,0:T(8,128)}, /*index=5*/f32[3,16,256]{2,1,0:T(8,128)}) custom-call(s32[9]{0:T(128)} %stack.45.t_ref, f32[3,512,256]{2,1,0:T(8,128)} %bitcast.20, f32[3,512,256]{2,1,0:T(8,128)} %back.1), custom_call_target="tpu_custom_call" | custom-call | bytes 1 | tf_op jit(solution)/shard_map/pallas_call | solution.py:179
  9.5 6.4 %collective-permute-start.6 = (f32[3,16,256]{2,1,0:T(8,128)}, f32[3,16,256]{2,1,0:T(8,128)S(1)}, u32[]{:S(2)}, u32[]{:S(2)}) collective-permute-start(f32[3,16,256]{2,1,0:T(8,128)} %get-tuple-element.45), channel_id=1, source_target_pairs={{0,3},{1,0},{2,1},{3,2},{4,7},{5,4},{6,5},{7,6},{8,11},{9,8},{10,9... | collective-permute-start | bytes 147464 | tf_op jit(solution)/shard_map/ppermute | solution.py:348
  15.9 1.0 collective-permute-start.7
  16.9 2.8 %collective-permute-start.8 = (f32[3,16,256]{2,1,0:T(8,128)}, f32[3,16,256]{2,1,0:T(8,128)S(1)}, u32[]{:S(2)}, u32[]{:S(2)}) collective-permute-start(f32[3,16,256]{2,1,0:T(8,128)} %get-tuple-element.47), channel_id=1, source_target_pairs={{0,1},{1,2},{2,3},{3,0},{4,5},{5,6},{6,7},{7,4},{8,9},{9,10},{10,1... | collective-permute-start | bytes 147464 | tf_op jit(solution)/shard_map/ppermute | solution.py:348
  19.7 4.7 %collective-permute-done.7 = f32[3,16,256]{2,1,0:T(8,128)S(1)} collective-permute-done((f32[3,16,256]{2,1,0:T(8,128)}, f32[3,16,256]{2,1,0:T(8,128)S(1)}, u32[]{:S(2)}, u32[]{:S(2)}) %collective-permute-start.7) | collective-permute-done | bytes 49184 | tf_op jit(solution)/shard_map/ppermute | solution.py:348
  24.4 1.5 pad_maximum_fusion
  25.9 1.3 collective-permute-start
  28.1 3.0 %convolution_bitcast_fusion = f32[3,1024]{1,0:T(4,128)S(1)} fusion(f32[513,1024]{1,0:T(8,128)} %constant.71.clone, f32[3,513]{1,0:T(4,128)S(1)} %copy-done), kind=kOutput, calls=%fused_computation | convolution fusion | flops 18911232 | bytes 2119692 | tf_op jit(solution)/shard_map/dot_general | solution.py:273
  31.1 2.5 %collective-permute-done.1.below = f32[3,16,256]{2,1,0:T(8,128)S(1)} collective-permute-done((f32[3,16,256]{2,1,0:T(8,128)}, f32[3,16,256]{2,1,0:T(8,128)S(1)}, u32[]{:S(2)}, u32[]{:S(2)}) %collective-permute-start.1) | collective-permute-done | bytes 49184 | tf_op jit(solution)/shard_map/ppermute | solution.py:367
  33.7 3.0 %shard_map.47 = (f32[440,256]{1,0:T(8,128)S(1)}, f32[440,256]{1,0:T(8,128)S(1)}, f32[440,256]{1,0:T(8,128)S(1)}, f32[440,256]{1,0:T(8,128)S(1)}) custom-call(s32[9]{0:T(128)S(1)} %copy-done.8, f32[3,512,256]{2,1,0:T(8,128)S(1)} %bitcast.21, f32[3,16,256]{2,1,0:T(8,128)S(1)} %collective-permute-done.above, f32[3,16,256]{2,1,0:T(8,128)S(1)} %collective-permute-done.1.below), custom_call_target="tpu_custom_call" | custom-call | bytes 1 | tf_op jit(solution)/shard_map/pallas_call | solution.py:217
  36.7 3.2 %collective-permute-start.3 = (f32[440,256]{1,0:T(8,128)S(1)}, f32[440,256]{1,0:T(8,128)S(1)}, u32[]{:S(2)}, u32[]{:S(2)}) collective-permute-start(f32[440,256]{1,0:T(8,128)S(1)} %get-tuple-element.38), channel_id=1, source_target_pairs={{0,35},{1,32},{2,33},{3,34},{32,67},{33,64},{34,65},{35,66},{64,99... | collective-permute-start | bytes 1351688 | tf_op jit(solution)/shard_map/ppermute | solution.py:344
  39.9 2.0 %collective-permute-start.4 = (f32[440,256]{1,0:T(8,128)S(1)}, f32[440,256]{1,0:T(8,128)S(1)}, u32[]{:S(2)}, u32[]{:S(2)}) collective-permute-start(f32[440,256]{1,0:T(8,128)S(1)} %get-tuple-element.39), channel_id=1, source_target_pairs={{0,34},{1,35},{2,32},{3,33},{32,66},{33,67},{34,64},{35,65},{64,98... | collective-permute-start | bytes 1351688 | tf_op jit(solution)/shard_map/ppermute | solution.py:344
  41.8 3.6 %collective-permute-start.5 = (f32[440,256]{1,0:T(8,128)S(1)}, f32[440,256]{1,0:T(8,128)S(1)}, u32[]{:S(2)}, u32[]{:S(2)}) collective-permute-start(f32[440,256]{1,0:T(8,128)S(1)} %get-tuple-element.40), channel_id=1, source_target_pairs={{0,33},{1,34},{2,35},{3,32},{32,65},{33,66},{34,67},{35,64},{64,97... | collective-permute-start | bytes 1351688 | tf_op jit(solution)/shard_map/ppermute | solution.py:344
  45.4 8.1 %collective-permute-done.2.s0 = f32[440,256]{1,0:T(8,128)S(1)} collective-permute-done((f32[440,256]{1,0:T(8,128)S(1)}, f32[440,256]{1,0:T(8,128)S(1)}, u32[]{:S(2)}, u32[]{:S(2)}) %collective-permute-start.2) | collective-permute-done | bytes 450592 | tf_op jit(solution)/shard_map/ppermute | solution.py:344
  53.5 27.6 %collective-permute-done.3.s3 = f32[440,256]{1,0:T(8,128)S(1)} collective-permute-done((f32[440,256]{1,0:T(8,128)S(1)}, f32[440,256]{1,0:T(8,128)S(1)}, u32[]{:S(2)}, u32[]{:S(2)}) %collective-permute-start.3) | collective-permute-done | bytes 450592 | tf_op jit(solution)/shard_map/ppermute | solution.py:344
  81.5 1.3 collective-permute-start.11
  83.2 8.8 %shard_map.48.f_ref = f32[3,64,1024]{2,1,0:T(8,128)S(1)} custom-call(f32[114]{0:T(128)S(1)} %get-tuple-element.34.f_ref, f32[440,256]{1,0:T(8,128)S(1)} %collective-permute-done.2.s0, f32[440,256]{1,0:T(8,128)S(1)} %collective-permute-done.3.s3, f32[440,256]{1,0:T(8,128)S(1)} %collective-permute-done.4.s2, f32[440,256]{1,0:T(8,128)S(1)} %collective-permute-done.5.s1), custom_call_target="tpu_custom_call" | custom-call | bytes 1 | tf_op jit(solution)/shard_map/pallas_call | solution.py:157
  92.3 4.8 %collective-permute-done.12.w1 = f32[440,256]{1,0:T(8,128)S(1)} collective-permute-done((f32[440,256]{1,0:T(8,128)S(1)}, f32[440,256]{1,0:T(8,128)S(1)}, u32[]{:S(2)}, u32[]{:S(2)}) %collective-permute-start.12) | collective-permute-done | bytes 450592 | tf_op jit(solution)/shard_map/ppermute | solution.py:383
  97.1 1.4 copy-done.1
  98.5 2.4 %shard_map.49 = (f32[3,64,256]{2,1,0:T(8,128)S(1)}, f32[3,64,256]{2,1,0:T(8,128)S(1)}, f32[3,64,256]{2,1,0:T(8,128)S(1)}, f32[3,64,256]{2,1,0:T(8,128)S(1)}) custom-call(s32[1]{0:T(128)} %bitcast.7.flag, f32[3,64,1024]{2,1,0:T(8,128)S(1)} %shard_map.48.f_ref, f32[3,256]{1,0:T(4,128)S(1)} %get-tuple-element.41.a_ref, f32[3,256]{1,0:T(4,128)S(1)} %get-tuple-element.42.b_ref, ...), custom_call_target="tpu_custom_call" | custom-call | bytes 1 | tf_op jit(solution)/shard_map/pallas_call | solution.py:319
  101.0 2.1 %collective-permute-start.16 = (f32[3,64,256]{2,1,0:T(8,128)S(1)}, f32[3,64,256]{2,1,0:T(8,128)S(1)}, u32[]{:S(2)}, u32[]{:S(2)}) collective-permute-start(f32[3,64,256]{2,1,0:T(8,128)S(1)} %get-tuple-element.49), channel_id=1, source_target_pairs={{0,1},{1,2},{2,3},{3,0},{4,5},{5,6},{6,7},{7,4},{8,9},{9,10},{10,1... | collective-permute-start | bytes 589832 | tf_op jit(solution)/shard_map/ppermute | solution.py:348
  103.1 3.5 %collective-permute-start.17 = (f32[3,64,256]{2,1,0:T(8,128)S(1)}, f32[3,64,256]{2,1,0:T(8,128)S(1)}, u32[]{:S(2)}, u32[]{:S(2)}) collective-permute-start(f32[3,64,256]{2,1,0:T(8,128)S(1)} %get-tuple-element.50), channel_id=1, source_target_pairs={{0,2},{1,3},{2,0},{3,1},{4,6},{5,7},{6,4},{7,5},{8,10},{9,11},{10,... | collective-permute-start | bytes 589832 | tf_op jit(solution)/shard_map/ppermute | solution.py:348
  106.6 2.5 %collective-permute-start.18 = (f32[3,64,256]{2,1,0:T(8,128)S(1)}, f32[3,64,256]{2,1,0:T(8,128)S(1)}, u32[]{:S(2)}, u32[]{:S(2)}) collective-permute-start(f32[3,64,256]{2,1,0:T(8,128)S(1)} %get-tuple-element.51), channel_id=1, source_target_pairs={{0,3},{1,0},{2,1},{3,2},{4,7},{5,4},{6,5},{7,6},{8,11},{9,8},{10,9... | collective-permute-start | bytes 589832 | tf_op jit(solution)/shard_map/ppermute | solution.py:348
  109.1 8.8 %shard_map.50.f_ref = f32[3,64,1024]{2,1,0:T(8,128)S(1)} custom-call(f32[114]{0:T(128)S(1)} %get-tuple-element.52.f_ref, f32[440,256]{1,0:T(8,128)S(1)} %collective-permute-done.2.s0, f32[440,256]{1,0:T(8,128)S(1)} %collective-permute-done.3.s3, f32[440,256]{1,0:T(8,128)S(1)} %copy-done.5, f32[440,256]{1,0:T(8,128)S(1)} %copy-done.7), custom_call_target="tpu_custom_call" | custom-call | bytes 1 | tf_op jit(solution)/shard_map/pallas_call | solution.py:157
  118.0 2.5 %shard_map.51 = (f32[3,64,256]{2,1,0:T(8,128)S(1)}, f32[3,64,256]{2,1,0:T(8,128)S(1)}, f32[3,64,256]{2,1,0:T(8,128)S(1)}, f32[3,64,256]{2,1,0:T(8,128)S(1)}) custom-call(s32[1]{0:T(128)} %bitcast.7.flag, f32[3,64,1024]{2,1,0:T(8,128)S(1)} %shard_map.50.f_ref, f32[3,256]{1,0:T(4,128)S(1)} %get-tuple-element.41.a_ref, f32[3,256]{1,0:T(4,128)S(1)} %get-tuple-element.42.b_ref, ...), custom_call_target="tpu_custom_call" | custom-call | bytes 1 | tf_op jit(solution)/shard_map/pallas_call | solution.py:319
  120.9 2.4 %collective-permute-start.14 = (f32[3,64,256]{2,1,0:T(8,128)S(1)}, f32[3,64,256]{2,1,0:T(8,128)S(1)}, u32[]{:S(2)}, u32[]{:S(2)}) collective-permute-start(f32[3,64,256]{2,1,0:T(8,128)S(1)} %get-tuple-element.55), channel_id=1, source_target_pairs={{0,2},{1,3},{2,0},{3,1},{4,6},{5,7},{6,4},{7,5},{8,10},{9,11},{10,... | collective-permute-start | bytes 589832 | tf_op jit(solution)/shard_map/ppermute | solution.py:348
  123.4 3.3 %collective-permute-start.15 = (f32[3,64,256]{2,1,0:T(8,128)S(1)}, f32[3,64,256]{2,1,0:T(8,128)S(1)}, u32[]{:S(2)}, u32[]{:S(2)}) collective-permute-start(f32[3,64,256]{2,1,0:T(8,128)S(1)} %get-tuple-element.56), channel_id=1, source_target_pairs={{0,3},{1,0},{2,1},{3,2},{4,7},{5,4},{6,5},{7,6},{8,11},{9,8},{10,9... | collective-permute-start | bytes 589832 | tf_op jit(solution)/shard_map/ppermute | solution.py:348
  126.6 1.4 shard_map.52.refs_0_
  128.1 6.8 %collective-permute-done.13.r1 = f32[3,64,256]{2,1,0:T(8,128)S(1)} collective-permute-done((f32[3,64,256]{2,1,0:T(8,128)S(1)}, f32[3,64,256]{2,1,0:T(8,128)S(1)}, u32[]{:S(2)}, u32[]{:S(2)}) %collective-permute-start.13) | collective-permute-done | bytes 196640 | tf_op jit(solution)/shard_map/ppermute | solution.py:348
  134.9 3.2 %collective-permute-done.14.r2 = f32[3,64,256]{2,1,0:T(8,128)S(1)} collective-permute-done((f32[3,64,256]{2,1,0:T(8,128)S(1)}, f32[3,64,256]{2,1,0:T(8,128)S(1)}, u32[]{:S(2)}, u32[]{:S(2)}) %collective-permute-start.14) | collective-permute-done | bytes 196640 | tf_op jit(solution)/shard_map/ppermute | solution.py:348
  138.1 3.4 %collective-permute-done.15.r3 = f32[3,64,256]{2,1,0:T(8,128)S(1)} collective-permute-done((f32[3,64,256]{2,1,0:T(8,128)S(1)}, f32[3,64,256]{2,1,0:T(8,128)S(1)}, u32[]{:S(2)}, u32[]{:S(2)}) %collective-permute-start.15) | collective-permute-done | bytes 196640 | tf_op jit(solution)/shard_map/ppermute | solution.py:348
  141.5 1.4 shard_map.53
  (41 shorter events, 3.0 us)
Async XLA Ops:
  6.5 21.5 %copy-start = (f32[3,513]{1,0:T(4,128)S(1)}, f32[3,513]{1,0:T(4,128)}, u32[]{:S(2)}) copy-start(f32[3,513]{1,0:T(4,128)} %param.6) | copy-start | bytes 18472
  6.5 90.6 %all-gather.3.cloned.1.call-start = ((), (), s32[]{:S(2)}) async-start(), calls=%async_computation | async-start | bytes 1769472 | tf_op jit(solution)/shard_map/all_gather | solution.py:369
  9.5 24.1 %copy-start.3 = (f32[1,3,512,256]{3,2,1,0:T(8,128)S(1)}, f32[1,3,512,256]{3,2,1,0:T(8,128)}, u32[]{:S(2)}) copy-start(f32[1,3,512,256]{3,2,1,0:T(8,128)} %param.4) | copy-start | bytes 4718596
  9.5 24.1 %copy-start.8 = (s32[9]{0:T(128)S(1)}, s32[9]{0:T(128)}, u32[]{:S(2)}) copy-start(s32[9]{0:T(128)} %stack.45.t_ref) | copy-start | bytes 112
  9.5 10.2 %collective-permute-start.6 = (f32[3,16,256]{2,1,0:T(8,128)}, f32[3,16,256]{2,1,0:T(8,128)S(1)}, u32[]{:S(2)}, u32[]{:S(2)}) collective-permute-start(f32[3,16,256]{2,1,0:T(8,128)} %get-tuple-element.45), channel_id=1, source_target_pairs={{0,3},{1,0},{2,1},{3,2},{4,7},{5,4},{6,5},{7,6},{8,11},{9,8},{10,9... | collective-permute-start | bytes 147464 | tf_op jit(solution)/shard_map/ppermute | solution.py:348
  15.9 8.5 %collective-permute-start.7 = (f32[3,16,256]{2,1,0:T(8,128)}, f32[3,16,256]{2,1,0:T(8,128)S(1)}, u32[]{:S(2)}, u32[]{:S(2)}) collective-permute-start(f32[3,16,256]{2,1,0:T(8,128)} %get-tuple-element.46), channel_id=1, source_target_pairs={{0,2},{1,3},{2,0},{3,1},{4,6},{5,7},{6,4},{7,5},{8,10},{9,11},{10,... | collective-permute-start | bytes 147464 | tf_op jit(solution)/shard_map/ppermute | solution.py:348
  16.9 7.5 %collective-permute-start.8 = (f32[3,16,256]{2,1,0:T(8,128)}, f32[3,16,256]{2,1,0:T(8,128)S(1)}, u32[]{:S(2)}, u32[]{:S(2)}) collective-permute-start(f32[3,16,256]{2,1,0:T(8,128)} %get-tuple-element.47), channel_id=1, source_target_pairs={{0,1},{1,2},{2,3},{3,0},{4,5},{5,6},{6,7},{7,4},{8,9},{9,10},{10,1... | collective-permute-start | bytes 147464 | tf_op jit(solution)/shard_map/ppermute | solution.py:348
  25.9 5.2 %collective-permute-start = (f32[3,16,256]{2,1,0:T(8,128)}, f32[3,16,256]{2,1,0:T(8,128)S(1)}, u32[]{:S(2)}, u32[]{:S(2)}) collective-permute-start(f32[3,16,256]{2,1,0:T(8,128)} %get-tuple-element.31), channel_id=1, source_target_pairs={{0,4},{4,8},{8,12},{12,16},{16,20},{20,24},{24,28},{28,0},{1,5},{5... | collective-permute-start | bytes 147464 | tf_op jit(solution)/shard_map/ppermute | solution.py:366
  27.2 6.4 %collective-permute-start.1 = (f32[3,16,256]{2,1,0:T(8,128)}, f32[3,16,256]{2,1,0:T(8,128)S(1)}, u32[]{:S(2)}, u32[]{:S(2)}) collective-permute-start(f32[3,16,256]{2,1,0:T(8,128)} %get-tuple-element.36), channel_id=1, source_target_pairs={{0,28},{4,0},{8,4},{12,8},{16,12},{20,16},{24,20},{28,24},{1,29},{... | collective-permute-start | bytes 147464 | tf_op jit(solution)/shard_map/ppermute | solution.py:367
  36.7 16.9 %collective-permute-start.2 = (f32[440,256]{1,0:T(8,128)S(1)}, f32[440,256]{1,0:T(8,128)S(1)}, u32[]{:S(2)}, u32[]{:S(2)}) collective-permute-start(f32[440,256]{1,0:T(8,128)S(1)} %get-tuple-element.37), channel_id=1, source_target_pairs={{0,32},{1,33},{2,34},{3,35},{32,64},{33,65},{34,66},{35,67},{64,96... | collective-permute-start | bytes 1351688 | tf_op jit(solution)/shard_map/ppermute | solution.py:344
  36.7 44.5 %collective-permute-start.3 = (f32[440,256]{1,0:T(8,128)S(1)}, f32[440,256]{1,0:T(8,128)S(1)}, u32[]{:S(2)}, u32[]{:S(2)}) collective-permute-start(f32[440,256]{1,0:T(8,128)S(1)} %get-tuple-element.38), channel_id=1, source_target_pairs={{0,35},{1,32},{2,33},{3,34},{32,67},{33,64},{34,65},{35,66},{64,99... | collective-permute-start | bytes 1351688 | tf_op jit(solution)/shard_map/ppermute | solution.py:344
  39.9 41.7 %collective-permute-start.4 = (f32[440,256]{1,0:T(8,128)S(1)}, f32[440,256]{1,0:T(8,128)S(1)}, u32[]{:S(2)}, u32[]{:S(2)}) collective-permute-start(f32[440,256]{1,0:T(8,128)S(1)} %get-tuple-element.39), channel_id=1, source_target_pairs={{0,34},{1,35},{2,32},{3,33},{32,66},{33,67},{34,64},{35,65},{64,98... | collective-permute-start | bytes 1351688 | tf_op jit(solution)/shard_map/ppermute | solution.py:344
  41.8 41.0 %collective-permute-start.5 = (f32[440,256]{1,0:T(8,128)S(1)}, f32[440,256]{1,0:T(8,128)S(1)}, u32[]{:S(2)}, u32[]{:S(2)}) collective-permute-start(f32[440,256]{1,0:T(8,128)S(1)} %get-tuple-element.40), channel_id=1, source_target_pairs={{0,33},{1,34},{2,35},{3,32},{32,65},{33,66},{34,67},{35,64},{64,97... | collective-permute-start | bytes 1351688 | tf_op jit(solution)/shard_map/ppermute | solution.py:344
  53.5 38.5 %collective-permute-start.9 = (f32[440,256]{1,0:T(8,128)S(1)}, f32[440,256]{1,0:T(8,128)S(1)}, u32[]{:S(2)}, u32[]{:S(2)}) collective-permute-start(f32[440,256]{1,0:T(8,128)S(1)} %collective-permute-done.2.s0), channel_id=1, source_target_pairs={{0,224},{32,0},{64,32},{96,64},{128,96},{160,128},{192,160},{224,1... | collective-permute-start | bytes 1351688 | tf_op jit(solution)/shard_map/ppermute | solution.py:383
  81.2 10.9 %collective-permute-start.10 = (f32[440,256]{1,0:T(8,128)S(1)}, f32[440,256]{1,0:T(8,128)S(1)}, u32[]{:S(2)}, u32[]{:S(2)}) collective-permute-start(f32[440,256]{1,0:T(8,128)S(1)} %collective-permute-done.3.s3), channel_id=1, source_target_pairs={{0,224},{32,0},{64,32},{96,64},{128,96},{160,128},{192,160},{224,1... | collective-permute-start | bytes 1351688 | tf_op jit(solution)/shard_map/ppermute | solution.py:383
  81.5 10.7 %copy-start.4 = (f32[440,256]{1,0:T(8,128)}, f32[440,256]{1,0:T(8,128)S(1)}, u32[]{:S(2)}) copy-start(f32[440,256]{1,0:T(8,128)S(1)} %collective-permute-done.4.s2) | copy-start | bytes 1351684
  81.5 10.7 %collective-permute-start.11 = (f32[440,256]{1,0:T(8,128)S(1)}, f32[440,256]{1,0:T(8,128)S(1)}, u32[]{:S(2)}, u32[]{:S(2)}) collective-permute-start(f32[440,256]{1,0:T(8,128)S(1)} %collective-permute-done.4.s2), channel_id=1, source_target_pairs={{0,224},{32,0},{64,32},{96,64},{128,96},{160,128},{192,160},{224,1... | collective-permute-start | bytes 1351688 | tf_op jit(solution)/shard_map/ppermute | solution.py:383
  82.9 9.4 %copy-start.6 = (f32[440,256]{1,0:T(8,128)}, f32[440,256]{1,0:T(8,128)S(1)}, u32[]{:S(2)}) copy-start(f32[440,256]{1,0:T(8,128)S(1)} %collective-permute-done.5.s1) | copy-start | bytes 1351684
  82.9 14.2 %collective-permute-start.12 = (f32[440,256]{1,0:T(8,128)S(1)}, f32[440,256]{1,0:T(8,128)S(1)}, u32[]{:S(2)}, u32[]{:S(2)}) collective-permute-start(f32[440,256]{1,0:T(8,128)S(1)} %collective-permute-done.5.s1), channel_id=1, source_target_pairs={{0,224},{32,0},{64,32},{96,64},{128,96},{160,128},{192,160},{224,1... | collective-permute-start | bytes 1351688 | tf_op jit(solution)/shard_map/ppermute | solution.py:383
  97.1 1.4 copy-start.1
  98.5 10.6 %copy-start.5 = (f32[440,256]{1,0:T(8,128)S(1)}, f32[440,256]{1,0:T(8,128)}, u32[]{:S(2)}) copy-start(f32[440,256]{1,0:T(8,128)} %copy-done.4) | copy-start | bytes 1351684
  98.5 10.6 %copy-start.7 = (f32[440,256]{1,0:T(8,128)S(1)}, f32[440,256]{1,0:T(8,128)}, u32[]{:S(2)}) copy-start(f32[440,256]{1,0:T(8,128)} %copy-done.6) | copy-start | bytes 1351684
  101.0 17.0 %copy-start.2 = (f32[32,3,16,256]{3,2,1,0:T(8,128)S(1)}, f32[32,3,16,256]{3,2,1,0:T(8,128)}, u32[]{:S(2)}) copy-start(f32[32,3,16,256]{3,2,1,0:T(8,128)} %all-gather.3.cloned.1.call-done) | copy-start | bytes 4718596
  101.0 22.4 %collective-permute-start.16 = (f32[3,64,256]{2,1,0:T(8,128)S(1)}, f32[3,64,256]{2,1,0:T(8,128)S(1)}, u32[]{:S(2)}, u32[]{:S(2)}) collective-permute-start(f32[3,64,256]{2,1,0:T(8,128)S(1)} %get-tuple-element.49), channel_id=1, source_target_pairs={{0,1},{1,2},{2,3},{3,0},{4,5},{5,6},{6,7},{7,4},{8,9},{9,10},{10,1... | collective-permute-start | bytes 589832 | tf_op jit(solution)/shard_map/ppermute | solution.py:348
  103.1 23.5 %collective-permute-start.17 = (f32[3,64,256]{2,1,0:T(8,128)S(1)}, f32[3,64,256]{2,1,0:T(8,128)S(1)}, u32[]{:S(2)}, u32[]{:S(2)}) collective-permute-start(f32[3,64,256]{2,1,0:T(8,128)S(1)} %get-tuple-element.50), channel_id=1, source_target_pairs={{0,2},{1,3},{2,0},{3,1},{4,6},{5,7},{6,4},{7,5},{8,10},{9,11},{10,... | collective-permute-start | bytes 589832 | tf_op jit(solution)/shard_map/ppermute | solution.py:348
  106.6 20.1 %collective-permute-start.18 = (f32[3,64,256]{2,1,0:T(8,128)S(1)}, f32[3,64,256]{2,1,0:T(8,128)S(1)}, u32[]{:S(2)}, u32[]{:S(2)}) collective-permute-start(f32[3,64,256]{2,1,0:T(8,128)S(1)} %get-tuple-element.51), channel_id=1, source_target_pairs={{0,3},{1,0},{2,1},{3,2},{4,7},{5,4},{6,5},{7,6},{8,11},{9,8},{10,9... | collective-permute-start | bytes 589832 | tf_op jit(solution)/shard_map/ppermute | solution.py:348
  120.4 14.4 %collective-permute-start.13 = (f32[3,64,256]{2,1,0:T(8,128)S(1)}, f32[3,64,256]{2,1,0:T(8,128)S(1)}, u32[]{:S(2)}, u32[]{:S(2)}) collective-permute-start(f32[3,64,256]{2,1,0:T(8,128)S(1)} %get-tuple-element.54), channel_id=1, source_target_pairs={{0,1},{1,2},{2,3},{3,0},{4,5},{5,6},{6,7},{7,4},{8,9},{9,10},{10,1... | collective-permute-start | bytes 589832 | tf_op jit(solution)/shard_map/ppermute | solution.py:348
  120.9 17.2 %collective-permute-start.14 = (f32[3,64,256]{2,1,0:T(8,128)S(1)}, f32[3,64,256]{2,1,0:T(8,128)S(1)}, u32[]{:S(2)}, u32[]{:S(2)}) collective-permute-start(f32[3,64,256]{2,1,0:T(8,128)S(1)} %get-tuple-element.55), channel_id=1, source_target_pairs={{0,2},{1,3},{2,0},{3,1},{4,6},{5,7},{6,4},{7,5},{8,10},{9,11},{10,... | collective-permute-start | bytes 589832 | tf_op jit(solution)/shard_map/ppermute | solution.py:348
  123.4 18.1 %collective-permute-start.15 = (f32[3,64,256]{2,1,0:T(8,128)S(1)}, f32[3,64,256]{2,1,0:T(8,128)S(1)}, u32[]{:S(2)}, u32[]{:S(2)}) collective-permute-start(f32[3,64,256]{2,1,0:T(8,128)S(1)} %get-tuple-element.56), channel_id=1, source_target_pairs={{0,3},{1,0},{2,1},{3,2},{4,7},{5,4},{6,5},{7,6},{8,11},{9,8},{10,9... | collective-permute-start | bytes 589832 | tf_op jit(solution)/shard_map/ppermute | solution.py:348
Sparse Core Ops, SparseCore 0:
  26.1 28.2 all-gather.2

commit v3 on v2

--- a/solution.py
+++ b/solution.py
@@ -18,7 +18,6 @@
 ROWS = 128
 HALO = 3 * STEPS
 CHUNK = ROWS // 2
-PART = ROWS // SUB
 SENT = 440
 TILES = CHUNK + 2 * HALO
 GROUP = 16
@@ -164,70 +163,77 @@
     )(f, *pieces)
 
 
-def prepare_kernel(t_ref, x, back, b2, b1, b3, b0, last, first, sem):
-    rows = x.shape[1]
+def rows_kernel(t_ref, x, s2, s1, s3, s0, sem):
     pairs = []
-    for j, b in ((2, b2), (1, b1), (3, b3), (0, b0)):
-        row = aligned(t_ref[j] * ROWS + t_ref[4] * PART)
-        pairs.append((back.at[:, pl.ds(row, PART), :], b))
-    pairs += [(x.at[:, pl.ds(rows - 16, 16), :], last), (x.at[:, pl.ds(0, 16), :], first)]
+    for j, s in ((2, s2), (1, s1), (3, s3), (0, s0)):
+        for c in range(3):
+            row = aligned(t_ref[j] * ROWS)
+            pairs.append((x.at[c, pl.ds(row, ROWS), :], s.at[pl.ds(ROWS * c, ROWS), :]))
     for copy in start_all(sem, pairs):
         copy.wait()
-
-
-def prepare(t, x, back):
+    for s in (s2, s1, s3, s0):
+        s[3 * ROWS :, :] = jnp.zeros((SENT - 3 * ROWS, 256), F32)
+
+
+def rows_to_send(t, x):
     return call(
-        prepare_kernel,
-        [array(3, PART, 256)] * 4 + [array(3, 16, 256)] * 2,
-        [smem_spec(), hbm_spec(), hbm_spec()],
-        [vmem_spec()] * 6,
-        [dma_sems(6)],
+        rows_kernel,
+        [array(SENT, 256)] * 4,
+        [smem_spec(), hbm_spec()],
+        [vmem_spec()] * 4,
+        [dma_sems(12)],
         60,
-    )(t, x, back)
-
-
-def send_kernel(t_ref, x, above, below, s2, s1, s3, s0, edges, sem):
+    )(t, x)
+
+
+def edges_kernel(t_ref, x, above, below, *refs):
+    outs = refs[4:8]
+    edges, ready, sem, sem_out = refs[8:]
     rows = x.shape[1]
     pairs = []
     for q in range(1, LON):
         pairs.append((x.at[:, pl.ds(ROWS * q - 16, 32), :], edges.at[q]))
     pairs += [
+        (x.at[:, pl.ds(0, 16), :], edges.at[0, :, pl.ds(16, 16), :]),
         (above, edges.at[0, :, pl.ds(0, 16), :]),
         (x.at[:, pl.ds(rows - 16, 16), :], edges.at[LON, :, pl.ds(0, 16), :]),
         (below, edges.at[LON, :, pl.ds(16, 16), :]),
     ]
-    small = len(pairs)
-    for j, s in ((2, s2), (1, s1), (3, s3), (0, s0)):
+    for copy in start_all(sem, pairs):
+        copy.wait()
+    pairs = []
+    for n, j in enumerate((2, 1, 3, 0)):
         for c in range(3):
-            row = aligned(t_ref[j] * ROWS)
-            pairs.append((x.at[c, pl.ds(row, ROWS), :], s.at[pl.ds(ROWS * c, ROWS), :]))
-    copies = start_all(sem, pairs)
-    for copy in copies[:small]:
+            edge = 2 * HALO * c
+            ready[n, edge : edge + HALO, :] = edges[t_ref[j], c, 16 - HALO : 16, :]
+            ready[n, edge + HALO : edge + 2 * HALO, :] = edges[t_ref[j] + 1, c, 16 : 16 + HALO, :]
+        ready[n, 6 * HALO :, :] = jnp.zeros((SENT - 3 * ROWS - 6 * HALO, 256), F32)
+        pairs.append((ready.at[n], outs[n].at[pl.ds(3 * ROWS, SENT - 3 * ROWS), :]))
+    for copy in start_all(sem_out, pairs):
         copy.wait()
-    for j, s in ((2, s2), (1, s1), (3, s3), (0, s0)):
-        for c in range(3):
-            edge = 3 * ROWS + 2 * HALO * c
-            s[edge : edge + HALO, :] = edges[t_ref[j], c, 16 - HALO : 16, :]
-            s[edge + HALO : edge + 2 * HALO, :] = edges[t_ref[j] + 1, c, 16 : 16 + HALO, :]
-    for copy in copies[small:]:
-        copy.wait()
-
-
-def send(t, x, above, below):
+
+
+def add_edges(t, x, above, below, sent):
     return call(
-        send_kernel,
+        edges_kernel,
         [array(SENT, 256)] * 4,
-        [smem_spec()] + [hbm_spec()] * 3,
-        [vmem_spec()] * 4,
-        [pltpu.VMEM((LON + 1, 3, 32, 256), F32), dma_sems(18)],
-        6,
-    )(t, x, above, below)
+        [smem_spec()] + [hbm_spec()] * 7,
+        [hbm_spec()] * 4,
+        [
+            pltpu.VMEM((LON + 1, 3, 32, 256), F32),
+            pltpu.VMEM((4, SENT - 3 * ROWS, 256), F32),
+            dma_sems(7),
+            dma_sems(4),
+        ],
+        60,
+        input_output_aliases={4: 0, 5: 1, 6: 2, 7: 3},
+    )(t, x, above, below, *sent)
 
 
 def place_kernel(first, t_ref, o0, r1, r2, r3, *refs):
     out, sem = refs[-2:]
     pairs = [
-        (r, out.at[:, pl.ds(aligned(t_ref[5 + j] * ROWS + first), CHUNK), :])
+        (r, out.at[:, pl.ds(aligned(t_ref[LON + j] * ROWS + first), CHUNK), :])
         for j, r in enumerate((o0, r1, r2, r3))
     ]
     for copy in start_all(sem, pairs):
@@ -284,25 +290,20 @@
     return y[:n] + y[n:] + jnp.dot(xh, low, preferred_element_type=F32)
 
 
-def weight_kernel(half, flag, f_ref, a_ref, b_ref, r_ref, back, w0, w3, w2, w1, *refs):
-    outs = refs[:4]
-    back_v, sem = refs[4:]
-    parts = CHUNK // PART
-    copies = start_all(sem, [(back.at[parts * half + n], back_v.at[n]) for n in range(parts)])
+def weight_kernel(half, flag, f_ref, a_ref, b_ref, r_ref, *refs):
+    own, back, outs = refs[:4], refs[4:8], refs[8:]
     start = flag[0] != 0
+    rows = slice(CHUNK * half, CHUNK * half + CHUNK)
     for c in range(3):
         a = split(toeplitz(a_ref[c : c + 1, :], 256, 1))
         b = split(toeplitz(b_ref[c : c + 1, :], 256, -1))
         r = split(toeplitz(r_ref[c : c + 1, :], 512, -1))
-        if c == 0:
-            for copy in copies:
-                copy.wait()
         d = []
-        for block, own in enumerate((w0, w3, w2, w1)):
-            rows = jnp.concatenate([back_v[n, block, c] for n in range(parts)], axis=0)
-            prev = jnp.where(start, rows, f_ref[c, :, 256 * block : 256 * block + 256])
+        for block in range(4):
+            f = f_ref[c, :, 256 * block : 256 * block + 256]
             row = ROWS * c + CHUNK * half
-            d.append(own[row : row + CHUNK, :] - prev)
+            prev = jnp.where(start, back[block][c, rows, :], f)
+            d.append(own[block][row : row + CHUNK, :] - prev)
         even, odd = d[0] + d[2], d[1] + d[3]
         x = dot3(even + odd, *a)
         y = dot3(even - odd, *b)
@@ -315,15 +316,14 @@
 
 
 def weight_call(half, flag, f, back, own, rows):
-    parts = CHUNK // PART
     return call(
         functools.partial(weight_kernel, half),
         [array(3, CHUNK, 256)] * 4,
-        [smem_spec()] + [vmem_spec()] * 4 + [hbm_spec()] + [vmem_spec()] * 4,
+        [smem_spec()] + [vmem_spec()] * 12,
         [vmem_spec()] * 4,
-        [pltpu.VMEM((parts, 4, 3, PART, 256), F32), dma_sems(parts)],
+        [],
         10,
-    )(flag, f, *rows, back, *own)
+    )(flag, f, *rows, *own, *back)
 
 
 def coriolis_rows(total, first, offsets):
@@ -358,15 +358,11 @@
     total = tile_rows * lax.axis_size("lat")
     t = jnp.stack(
         [lax.rem(lon + j, LON) for j in range(LON)]
-        + [sub]
         + [lax.rem(lon - j + LON, LON) for j in range(LON)]
     )
 
-    *parts, last, first = prepare(t, x, initial_backdrop)
-    above = lax.ppermute(last, "lat", ring(8, 1))
-    below = lax.ppermute(first, "lat", ring(8, -1))
-    b2, b1, b3 = (to_lon(v, j) for v, j in zip(parts, (2, 1, 3)))
-    back = lax.all_gather(jnp.stack([parts[3], b3, b2, b1]), "sub")
+    above = lax.ppermute(x[:, tile_rows - 16 :], "lat", ring(8, 1))
+    below = lax.ppermute(x[:, :16], "lat", ring(8, -1))
 
     flag = (sub == 0).astype(jnp.int32).reshape(1)
     first_row = lat * tile_rows + lon * ROWS
@@ -377,10 +373,15 @@
     above, *tied = lax.optimization_barrier((above, f1, f2, flag, *rows))
     f1, f2, flag, *rows = tied
 
-    sent = send(t, x, above, below)
+    sent = add_edges(t, x, above, below, rows_to_send(t, x))
     s2, s1, s3, s0 = (to_next(v, j) for v, j in zip(sent, (2, 1, 3, 0)))
     come = [s0, s3, s2, s1]
     own = [lax.ppermute(v, "sub", ring(SUB, -1)) for v in come]
+    back = {}
+    for j in (2, 1, 3, 0):
+        block = lax.dynamic_slice(initial_backdrop, (0, ROWS * t[j], 0), (3, ROWS, 256))
+        back[j] = lax.ppermute(block, ("sub", "lon"), ring(LON, j)) if j else block
+    back = [back[j] for j in (0, 3, 2, 1)]
 
     m1 = model_call(False, f1, come)
     o1 = weight_call(0, flag, m1, back, own, rows)

time: 150 us -> 132 us (0.88)
  waiting for transfers between devices: 61.4 us -> 44.4 us
  starting transfers between devices: 37.5 us -> 51.6 us
  between operations: 13.6 us -> 0.4 us
  local copies, waits for them, and re-layouts: 2.07 us -> 4.6 us
  Pallas kernels: 30.7 us -> 29.1 us
  matrix products: 2.96 us -> 1.39 us
    ppermute x2 -> x5, starting transfers between devices: 2.1 us -> 18.3 us  [the longest x3 14.1 us: shards(): back[j] = lax.ppermute(block, ('sub', 'lon'), ring(LON, j)) if j else block]
    ppermute x9 -> x6, waiting for transfers between devices: 18.1 us -> 4.28 us  [to_lon(): return lax.ppermute(value, 'lon', ring(LON, j))]
    ppermute x4, waiting for transfers between devices: 5.01 us -> 0.01 us  [shards(): own = [lax.ppermute(v, 'sub', ring(SUB, -1)) for v in come]]
    ppermute x2 -> x5, waiting for transfers between devices: 2.54 us -> 7.49 us  [the longest x3 7.49 us: shards(): back[j] = lax.ppermute(block, ('sub', 'lon'), ring(LON, j)) if j else block]
    ppermute x4, waiting for transfers between devices: 35.8 us -> 32.6 us  [to_next(): return lax.ppermute(value, ('sub', 'lon'), pairs)]
    dynamic_slice x0 -> x1, local copies, waits for them, and re-layouts: none -> 2.5 us  [shards(): lax.dynamic_slice(initial_backdrop, (0, ROWS * t[j], 0), (3, ROWS, 256))]
    pallas_call x2, Pallas kernels: 4.89 us -> 2.52 us  [weight_call(): call(functools.partial(weight_kernel, half), [array(3, CHUNK, 256)] * 4,...]
    dot_general x1, matrix products: 2.96 us -> 1.39 us  [weighting_rows(): jnp.dot(variances, jnp.asarray(cosine_table()), precision=lax.Precision.H...]
  transfers between devices with their start and end apart: 20 -> 19, of which waited for: 9 -> 6; matrix products, arithmetic and copies ran while one was open for 2% -> 3% of each run, Pallas kernels for 16% -> 20%
where the time goes in v3:
time: 132 us
  starting transfers between devices  51.6 us (39%)
  waiting for transfers between devices  44.4 us (34%)
  Pallas kernels  29.1 us (22%)
  local copies, waits for them, and re-layouts  4.6 us (3%)
  matrix products  1.39 us (1%)
    ppermute x4, waiting for transfers between devices, to_next(): return lax.ppermute(value, ('sub', 'lon'), pairs)  32.6 us
    ppermute x6, starting transfers between devices, to_lon(): return lax.ppermute(value, 'lon', ring(LON, j))  23.2 us
    pallas_call x2, Pallas kernels, model_call(): call(functools.partial(model_kernel, second), array(3, CHUNK, NLON), [sme...  17.7 us
    ppermute x3, starting transfers between devices, shards(): back[j] = lax.ppermute(block, ('sub', 'lon'), ring(LON, j)) if j else block  14.1 us
    ppermute x3, waiting for transfers between devices, shards(): back[j] = lax.ppermute(block, ('sub', 'lon'), ring(LON, j)) if j else block  7.49 us
    ppermute x4, starting transfers between devices, to_next(): return lax.ppermute(value, ('sub', 'lon'), pairs)  7.48 us
    ppermute x6, waiting for transfers between devices, to_lon(): return lax.ppermute(value, 'lon', ring(LON, j))  4.28 us
    pallas_call x1, Pallas kernels, rows_to_send(): call(rows_kernel, [array(SENT, 256)] * 4, [smem_spec(), hbm_spec()], [vme...  3.44 us
  transfers between devices with their start and end apart: 19, of which 6 were waited for; matrix products, arithmetic and copies ran while one was open for 3% of the time, Pallas kernels for 20%

profile of v3, /device:TPU:24, one launch (start us, length us, event | category | flops | bytes accessed | tf_op | source)
XLA Modules:
  0.0 131.6 jit_solution(3185886822243437950)
XLA Ops:
  0.0 0.8 fusion.5
  0.8 0.8 collective-permute-start.1
  1.6 3.4 %collective-permute-start = (f32[3,16,256]{2,1,0:T(8,128)S(1)}, f32[3,16,256]{2,1,0:T(8,128)S(1)}, u32[]{:S(2)}, u32[]{:S(2)}) collective-permute-start(f32[3,16,256]{2,1,0:T(8,128)S(1)} %get-tuple-element.58), channel_id=1, source_target_pairs={{0,4},{4,8},{8,12},{12,16},{16,20},{20,24},{24,28},{28,0},{1,5},{5... | collective-permute-start | bytes 147464 | tf_op jit(solution)/shard_map/ppermute | solution.py:364
  5.0 2.5 %constant_dynamic-slice_fusion = (f32[3,128,256]{2,1,0:T(8,128)}, f32[3,128,256]{2,1,0:T(8,128)}, f32[3,128,256]{2,1,0:T(8,128)S(1)}, f32[3,128,256]{2,1,0:T(8,128)S(1)}) fusion(f32[3,512,256]{2,1,0:T(8,128)} %param.5, s32[]{:T(128)S(6)} %select_n.15, s32[]{:T(128)S(6)} %select_n.13, s32[]{:T(128)S(6)} %select_n.12, s32[]{:T(128)S(6)} %select_n.14), kind=kLoop, calls=%fused_computation.7 | loop fusion | bytes 3145744 | tf_op jit(solution)/shard_map/dynamic_slice | solution.py:382
  7.5 5.2 %collective-permute-start.12 = (f32[3,128,256]{2,1,0:T(8,128)}, f32[3,128,256]{2,1,0:T(8,128)S(1)}, u32[]{:S(2)}, u32[]{:S(2)}) collective-permute-start(f32[3,128,256]{2,1,0:T(8,128)} %get-tuple-element.53), channel_id=1, source_target_pairs={{0,1},{1,2},{2,3},{3,0},{4,5},{5,6},{6,7},{7,4},{8,9},{9,10},{10,1... | collective-permute-start | bytes 1179656 | tf_op jit(solution)/shard_map/ppermute | solution.py:383
  12.7 1.4 %convolution_bitcast_fusion = f32[3,1024]{1,0:T(4,128)S(1)} fusion(f32[513,1024]{1,0:T(8,128)S(1)} %copy-done.2, f32[3,513]{1,0:T(4,128)S(1)} %copy-done), kind=kOutput, calls=%fused_computation | convolution fusion | flops 18911232 | bytes 2119692 | tf_op jit(solution)/shard_map/dot_general | solution.py:279
  14.2 0.6 stack.26.t_ref
  14.9 3.4 %shard_map.46 = (f32[440,256]{1,0:T(8,128)}, f32[440,256]{1,0:T(8,128)}, f32[440,256]{1,0:T(8,128)}, f32[440,256]{1,0:T(8,128)}) custom-call(s32[8]{0:T(128)} %stack.26.t_ref, f32[3,512,256]{2,1,0:T(8,128)} %bitcast.13), custom_call_target="tpu_custom_call" | custom-call | bytes 1 | tf_op jit(solution)/shard_map/pallas_call | solution.py:179
  18.4 0.6 copy-done.5
  19.0 2.6 %shard_map.47 = (f32[440,256]{1,0:T(8,128)}, f32[440,256]{1,0:T(8,128)}, f32[440,256]{1,0:T(8,128)}, f32[440,256]{1,0:T(8,128)}) custom-call(s32[8]{0:T(128)} %stack.26.t_ref, f32[3,512,256]{2,1,0:T(8,128)} %bitcast.14, f32[3,16,256]{2,1,0:T(8,128)} %copy-done.5, ...), custom_call_target="tpu_custom_call", output_to_operand_aliasing={{0}: (4, {}), {1}: (5, {}), {2}: (6, {}), {3}: (7, {})} | custom-call | bytes 1 | tf_op jit(solution)/shard_map/pallas_call | solution.py:217
  21.6 3.0 %collective-permute-start.3 = (f32[440,256]{1,0:T(8,128)}, f32[440,256]{1,0:T(8,128)S(1)}, u32[]{:S(2)}, u32[]{:S(2)}) collective-permute-start(f32[440,256]{1,0:T(8,128)} %get-tuple-element.38), channel_id=1, source_target_pairs={{0,35},{1,32},{2,33},{3,34},{32,67},{33,64},{34,65},{35,66},{64,99... | collective-permute-start | bytes 1351688 | tf_op jit(solution)/shard_map/ppermute | solution.py:344
  24.6 0.9 collective-permute-start.4
  25.5 3.6 %collective-permute-start.5 = (f32[440,256]{1,0:T(8,128)}, f32[440,256]{1,0:T(8,128)S(1)}, u32[]{:S(2)}, u32[]{:S(2)}) collective-permute-start(f32[440,256]{1,0:T(8,128)} %get-tuple-element.40), channel_id=1, source_target_pairs={{0,33},{1,34},{2,35},{3,32},{32,65},{33,66},{34,67},{35,64},{64,97... | collective-permute-start | bytes 1351688 | tf_op jit(solution)/shard_map/ppermute | solution.py:344
  29.1 2.8 %collective-permute-start.10 = (f32[3,128,256]{2,1,0:T(8,128)S(1)}, f32[3,128,256]{2,1,0:T(8,128)S(1)}, u32[]{:S(2)}, u32[]{:S(2)}) collective-permute-start(f32[3,128,256]{2,1,0:T(8,128)S(1)} %copy-done.3), channel_id=1, source_target_pairs={{0,3},{1,0},{2,1},{3,2},{4,7},{5,4},{6,5},{7,6},{8,11},{9,8},{10,9... | collective-permute-start | bytes 1179656 | tf_op jit(solution)/shard_map/ppermute | solution.py:383
  31.9 20.0 %collective-permute-done.3.s3 = f32[440,256]{1,0:T(8,128)S(1)} collective-permute-done((f32[440,256]{1,0:T(8,128)}, f32[440,256]{1,0:T(8,128)S(1)}, u32[]{:S(2)}, u32[]{:S(2)}) %collective-permute-start.3) | collective-permute-done | bytes 450592 | tf_op jit(solution)/shard_map/ppermute | solution.py:344
  52.0 2.3 %collective-permute-start.8 = (f32[440,256]{1,0:T(8,128)S(1)}, f32[440,256]{1,0:T(8,128)S(1)}, u32[]{:S(2)}, u32[]{:S(2)}) collective-permute-start(f32[440,256]{1,0:T(8,128)S(1)} %collective-permute-done.4.s2), channel_id=1, source_target_pairs={{0,224},{32,0},{64,32},{96,64},{128,96},{160,128},{192,160},{224,1... | collective-permute-start | bytes 1351688 | tf_op jit(solution)/shard_map/ppermute | solution.py:379
  54.2 12.5 %collective-permute-done.5.s1 = f32[440,256]{1,0:T(8,128)S(1)} collective-permute-done((f32[440,256]{1,0:T(8,128)}, f32[440,256]{1,0:T(8,128)S(1)}, u32[]{:S(2)}, u32[]{:S(2)}) %collective-permute-start.5) | collective-permute-done | bytes 450592 | tf_op jit(solution)/shard_map/ppermute | solution.py:344
  67.1 5.1 %collective-permute-done.10.refs_5_ = f32[3,128,256]{2,1,0:T(8,128)S(1)} collective-permute-done((f32[3,128,256]{2,1,0:T(8,128)S(1)}, f32[3,128,256]{2,1,0:T(8,128)S(1)}, u32[]{:S(2)}, u32[]{:S(2)}) %collective-permute-start.10) | collective-permute-done | bytes 393248 | tf_op jit(solution)/shard_map/ppermute | solution.py:383
  72.2 6.1 %collective-permute-start.11 = (f32[3,128,256]{2,1,0:T(8,128)S(1)}, f32[3,128,256]{2,1,0:T(8,128)S(1)}, u32[]{:S(2)}, u32[]{:S(2)}) collective-permute-start(f32[3,128,256]{2,1,0:T(8,128)S(1)} %get-tuple-element.56), channel_id=1, source_target_pairs={{0,2},{1,3},{2,0},{3,1},{4,6},{5,7},{6,4},{7,5},{8,10},{9,11},{10,... | collective-permute-start | bytes 1179656 | tf_op jit(solution)/shard_map/ppermute | solution.py:383
  78.4 8.8 %shard_map.48.f_ref = f32[3,64,1024]{2,1,0:T(8,128)S(1)} custom-call(f32[114]{0:T(128)S(1)} %get-tuple-element.31.f_ref, f32[440,256]{1,0:T(8,128)S(1)} %collective-permute-done.2.s0, f32[440,256]{1,0:T(8,128)S(1)} %collective-permute-done.3.s3, f32[440,256]{1,0:T(8,128)S(1)} %collective-permute-done.4.s2, f32[440,256]{1,0:T(8,128)S(1)} %collective-permute-done.5.s1), custom_call_target="tpu_custom_call" | custom-call | bytes 1 | tf_op jit(solution)/shard_map/pallas_call | solution.py:156
  87.2 2.4 %collective-permute-done.11.refs_6_ = f32[3,128,256]{2,1,0:T(8,128)S(1)} collective-permute-done((f32[3,128,256]{2,1,0:T(8,128)S(1)}, f32[3,128,256]{2,1,0:T(8,128)S(1)}, u32[]{:S(2)}, u32[]{:S(2)}) %collective-permute-start.11) | collective-permute-done | bytes 393248 | tf_op jit(solution)/shard_map/ppermute | solution.py:383
  89.6 1.3 shard_map.49
  90.9 8.9 %collective-permute-start.16 = (f32[3,64,256]{2,1,0:T(8,128)S(1)}, f32[3,64,256]{2,1,0:T(8,128)S(1)}, u32[]{:S(2)}, u32[]{:S(2)}) collective-permute-start(f32[3,64,256]{2,1,0:T(8,128)S(1)} %get-tuple-element.45), channel_id=1, source_target_pairs={{0,1},{1,2},{2,3},{3,0},{4,5},{5,6},{6,7},{7,4},{8,9},{9,10},{10,1... | collective-permute-start | bytes 589832 | tf_op jit(solution)/shard_map/ppermute | solution.py:348
  99.8 6.4 %collective-permute-start.17 = (f32[3,64,256]{2,1,0:T(8,128)S(1)}, f32[3,64,256]{2,1,0:T(8,128)S(1)}, u32[]{:S(2)}, u32[]{:S(2)}) collective-permute-start(f32[3,64,256]{2,1,0:T(8,128)S(1)} %get-tuple-element.46), channel_id=1, source_target_pairs={{0,2},{1,3},{2,0},{3,1},{4,6},{5,7},{6,4},{7,5},{8,10},{9,11},{10,... | collective-permute-start | bytes 589832 | tf_op jit(solution)/shard_map/ppermute | solution.py:348
  106.2 8.8 %shard_map.50.f_ref = f32[3,64,1024]{2,1,0:T(8,128)S(1)} custom-call(f32[114]{0:T(128)S(1)} %get-tuple-element.48.f_ref, f32[440,256]{1,0:T(8,128)S(1)} %collective-permute-done.2.s0, f32[440,256]{1,0:T(8,128)S(1)} %collective-permute-done.3.s3, f32[440,256]{1,0:T(8,128)S(1)} %collective-permute-done.4.s2, f32[440,256]{1,0:T(8,128)S(1)} %collective-permute-done.5.s1), custom_call_target="tpu_custom_call" | custom-call | bytes 1 | tf_op jit(solution)/shard_map/pallas_call | solution.py:156
  115.1 1.3 shard_map.51
  116.3 3.0 %collective-permute-start.13 = (f32[3,64,256]{2,1,0:T(8,128)S(1)}, f32[3,64,256]{2,1,0:T(8,128)S(1)}, u32[]{:S(2)}, u32[]{:S(2)}) collective-permute-start(f32[3,64,256]{2,1,0:T(8,128)S(1)} %get-tuple-element.50), channel_id=1, source_target_pairs={{0,1},{1,2},{2,3},{3,0},{4,5},{5,6},{6,7},{7,4},{8,9},{9,10},{10,1... | collective-permute-start | bytes 589832 | tf_op jit(solution)/shard_map/ppermute | solution.py:348
  119.3 0.8 collective-permute-start.14
  120.2 4.0 %collective-permute-start.15 = (f32[3,64,256]{2,1,0:T(8,128)S(1)}, f32[3,64,256]{2,1,0:T(8,128)S(1)}, u32[]{:S(2)}, u32[]{:S(2)}) collective-permute-start(f32[3,64,256]{2,1,0:T(8,128)S(1)} %get-tuple-element.52), channel_id=1, source_target_pairs={{0,3},{1,0},{2,1},{3,2},{4,7},{5,4},{6,5},{7,6},{8,11},{9,8},{10,9... | collective-permute-start | bytes 589832 | tf_op jit(solution)/shard_map/ppermute | solution.py:348
  124.2 1.5 %shard_map.52.refs_0_ = f32[3,512,256]{2,1,0:T(8,128)} custom-call(s32[8]{0:T(128)S(1)} %copy-done.1, f32[3,64,256]{2,1,0:T(8,128)S(1)} %get-tuple-element.44.o0, f32[3,64,256]{2,1,0:T(8,128)S(1)} %collective-permute-done.16.r1, f32[3,64,256]{2,1,0:T(8,128)S(1)} %collective-permute-done.17.r2, f32[3,64,256]{2,1,0:T(8,128)S(1)} %collective-permute-done.18.r3), custom_call_target="tpu_custom_call" | custom-call | bytes 1 | tf_op jit(solution)/shard_map/pallas_call | solution.py:245
  125.7 4.3 %collective-permute-done.14.r2 = f32[3,64,256]{2,1,0:T(8,128)S(1)} collective-permute-done((f32[3,64,256]{2,1,0:T(8,128)S(1)}, f32[3,64,256]{2,1,0:T(8,128)S(1)}, u32[]{:S(2)}, u32[]{:S(2)}) %collective-permute-start.14) | collective-permute-done | bytes 196640 | tf_op jit(solution)/shard_map/ppermute | solution.py:348
  130.0 1.4 %shard_map.53 = f32[3,512,256]{2,1,0:T(8,128)} custom-call(s32[8]{0:T(128)S(1)} %copy-done.1, f32[3,64,256]{2,1,0:T(8,128)S(1)} %get-tuple-element.49.o0, f32[3,64,256]{2,1,0:T(8,128)S(1)} %collective-permute-done.13.r1, f32[3,64,256]{2,1,0:T(8,128)S(1)} %collective-permute-done.14.r2, ...), custom_call_target="tpu_custom_call", output_to_operand_aliasing={{}: (5, {})} | custom-call | bytes 1 | tf_op jit(solution)/shard_map/pallas_call | solution.py:245
  (33 shorter events, 0.6 us)
Async XLA Ops:
  0.0 12.7 %copy-start = (f32[3,513]{1,0:T(4,128)S(1)}, f32[3,513]{1,0:T(4,128)}, u32[]{:S(2)}) copy-start(f32[3,513]{1,0:T(4,128)} %param.6) | copy-start | bytes 18472
  0.8 17.5 %collective-permute-start.1 = (f32[3,16,256]{2,1,0:T(8,128)S(1)}, f32[3,16,256]{2,1,0:T(8,128)S(1)}, u32[]{:S(2)}, u32[]{:S(2)}) collective-permute-start(f32[3,16,256]{2,1,0:T(8,128)S(1)} %get-tuple-element.57), channel_id=1, source_target_pairs={{0,28},{4,0},{8,4},{12,8},{16,12},{20,16},{24,20},{28,24},{1,29},{... | collective-permute-start | bytes 147464 | tf_op jit(solution)/shard_map/ppermute | solution.py:365
  1.6 16.7 %collective-permute-start = (f32[3,16,256]{2,1,0:T(8,128)S(1)}, f32[3,16,256]{2,1,0:T(8,128)S(1)}, u32[]{:S(2)}, u32[]{:S(2)}) collective-permute-start(f32[3,16,256]{2,1,0:T(8,128)S(1)} %get-tuple-element.58), channel_id=1, source_target_pairs={{0,4},{4,8},{8,12},{12,16},{16,20},{20,24},{24,28},{28,0},{1,5},{5... | collective-permute-start | bytes 147464 | tf_op jit(solution)/shard_map/ppermute | solution.py:364
  5.0 7.7 %copy-start.2 = (f32[513,1024]{1,0:T(8,128)S(1)}, f32[513,1024]{1,0:T(8,128)}, u32[]{:S(2)}) copy-start(f32[513,1024]{1,0:T(8,128)} %constant.71.clone) | copy-start | bytes 6303748
  7.5 21.5 %collective-permute-start.12 = (f32[3,128,256]{2,1,0:T(8,128)}, f32[3,128,256]{2,1,0:T(8,128)S(1)}, u32[]{:S(2)}, u32[]{:S(2)}) collective-permute-start(f32[3,128,256]{2,1,0:T(8,128)} %get-tuple-element.53), channel_id=1, source_target_pairs={{0,1},{1,2},{2,3},{3,0},{4,5},{5,6},{6,7},{7,4},{8,9},{9,10},{10,1... | collective-permute-start | bytes 1179656 | tf_op jit(solution)/shard_map/ppermute | solution.py:383
  18.3 0.6 copy-start.5
  18.4 0.6 copy-start.4
  19.0 10.1 %copy-start.3 = (f32[3,128,256]{2,1,0:T(8,128)S(1)}, f32[3,128,256]{2,1,0:T(8,128)}, u32[]{:S(2)}) copy-start(f32[3,128,256]{2,1,0:T(8,128)} %get-tuple-element.54) | copy-start | bytes 1179652
  21.6 10.3 %collective-permute-start.2 = (f32[440,256]{1,0:T(8,128)}, f32[440,256]{1,0:T(8,128)S(1)}, u32[]{:S(2)}, u32[]{:S(2)}) collective-permute-start(f32[440,256]{1,0:T(8,128)} %get-tuple-element.37), channel_id=1, source_target_pairs={{0,32},{1,33},{2,34},{3,35},{32,64},{33,65},{34,66},{35,67},{64,96... | collective-permute-start | bytes 1351688 | tf_op jit(solution)/shard_map/ppermute | solution.py:344
  21.6 30.3 %collective-permute-start.3 = (f32[440,256]{1,0:T(8,128)}, f32[440,256]{1,0:T(8,128)S(1)}, u32[]{:S(2)}, u32[]{:S(2)}) collective-permute-start(f32[440,256]{1,0:T(8,128)} %get-tuple-element.38), channel_id=1, source_target_pairs={{0,35},{1,32},{2,33},{3,34},{32,67},{33,64},{34,65},{35,66},{64,99... | collective-permute-start | bytes 1351688 | tf_op jit(solution)/shard_map/ppermute | solution.py:344
  24.6 27.3 %collective-permute-start.4 = (f32[440,256]{1,0:T(8,128)}, f32[440,256]{1,0:T(8,128)S(1)}, u32[]{:S(2)}, u32[]{:S(2)}) collective-permute-start(f32[440,256]{1,0:T(8,128)} %get-tuple-element.39), channel_id=1, source_target_pairs={{0,34},{1,35},{2,32},{3,33},{32,66},{33,67},{34,64},{35,65},{64,98... | collective-permute-start | bytes 1351688 | tf_op jit(solution)/shard_map/ppermute | solution.py:344
  25.5 41.3 %collective-permute-start.5 = (f32[440,256]{1,0:T(8,128)}, f32[440,256]{1,0:T(8,128)S(1)}, u32[]{:S(2)}, u32[]{:S(2)}) collective-permute-start(f32[440,256]{1,0:T(8,128)} %get-tuple-element.40), channel_id=1, source_target_pairs={{0,33},{1,34},{2,35},{3,32},{32,65},{33,66},{34,67},{35,64},{64,97... | collective-permute-start | bytes 1351688 | tf_op jit(solution)/shard_map/ppermute | solution.py:344
  29.1 43.1 %collective-permute-start.10 = (f32[3,128,256]{2,1,0:T(8,128)S(1)}, f32[3,128,256]{2,1,0:T(8,128)S(1)}, u32[]{:S(2)}, u32[]{:S(2)}) collective-permute-start(f32[3,128,256]{2,1,0:T(8,128)S(1)} %copy-done.3), channel_id=1, source_target_pairs={{0,3},{1,0},{2,1},{3,2},{4,7},{5,4},{6,5},{7,6},{8,11},{9,8},{10,9... | collective-permute-start | bytes 1179656 | tf_op jit(solution)/shard_map/ppermute | solution.py:383
  31.9 57.7 %collective-permute-start.6 = (f32[440,256]{1,0:T(8,128)S(1)}, f32[440,256]{1,0:T(8,128)S(1)}, u32[]{:S(2)}, u32[]{:S(2)}) collective-permute-start(f32[440,256]{1,0:T(8,128)S(1)} %collective-permute-done.2.s0), channel_id=1, source_target_pairs={{0,224},{32,0},{64,32},{96,64},{128,96},{160,128},{192,160},{224,1... | collective-permute-start | bytes 1351688 | tf_op jit(solution)/shard_map/ppermute | solution.py:379
  51.9 37.7 %collective-permute-start.7 = (f32[440,256]{1,0:T(8,128)S(1)}, f32[440,256]{1,0:T(8,128)S(1)}, u32[]{:S(2)}, u32[]{:S(2)}) collective-permute-start(f32[440,256]{1,0:T(8,128)S(1)} %collective-permute-done.3.s3), channel_id=1, source_target_pairs={{0,224},{32,0},{64,32},{96,64},{128,96},{160,128},{192,160},{224,1... | collective-permute-start | bytes 1351688 | tf_op jit(solution)/shard_map/ppermute | solution.py:379
  52.0 37.6 %collective-permute-start.8 = (f32[440,256]{1,0:T(8,128)S(1)}, f32[440,256]{1,0:T(8,128)S(1)}, u32[]{:S(2)}, u32[]{:S(2)}) collective-permute-start(f32[440,256]{1,0:T(8,128)S(1)} %collective-permute-done.4.s2), channel_id=1, source_target_pairs={{0,224},{32,0},{64,32},{96,64},{128,96},{160,128},{192,160},{224,1... | collective-permute-start | bytes 1351688 | tf_op jit(solution)/shard_map/ppermute | solution.py:379
  66.8 22.8 %collective-permute-start.9 = (f32[440,256]{1,0:T(8,128)S(1)}, f32[440,256]{1,0:T(8,128)S(1)}, u32[]{:S(2)}, u32[]{:S(2)}) collective-permute-start(f32[440,256]{1,0:T(8,128)S(1)} %collective-permute-done.5.s1), channel_id=1, source_target_pairs={{0,224},{32,0},{64,32},{96,64},{128,96},{160,128},{192,160},{224,1... | collective-permute-start | bytes 1351688 | tf_op jit(solution)/shard_map/ppermute | solution.py:379
  72.2 17.4 %collective-permute-start.11 = (f32[3,128,256]{2,1,0:T(8,128)S(1)}, f32[3,128,256]{2,1,0:T(8,128)S(1)}, u32[]{:S(2)}, u32[]{:S(2)}) collective-permute-start(f32[3,128,256]{2,1,0:T(8,128)S(1)} %get-tuple-element.56), channel_id=1, source_target_pairs={{0,2},{1,3},{2,0},{3,1},{4,6},{5,7},{6,4},{7,5},{8,10},{9,11},{10,... | collective-permute-start | bytes 1179656 | tf_op jit(solution)/shard_map/ppermute | solution.py:383
  90.9 29.3 %collective-permute-start.16 = (f32[3,64,256]{2,1,0:T(8,128)S(1)}, f32[3,64,256]{2,1,0:T(8,128)S(1)}, u32[]{:S(2)}, u32[]{:S(2)}) collective-permute-start(f32[3,64,256]{2,1,0:T(8,128)S(1)} %get-tuple-element.45), channel_id=1, source_target_pairs={{0,1},{1,2},{2,3},{3,0},{4,5},{5,6},{6,7},{7,4},{8,9},{9,10},{10,1... | collective-permute-start | bytes 589832 | tf_op jit(solution)/shard_map/ppermute | solution.py:348
  99.8 24.4 %collective-permute-start.17 = (f32[3,64,256]{2,1,0:T(8,128)S(1)}, f32[3,64,256]{2,1,0:T(8,128)S(1)}, u32[]{:S(2)}, u32[]{:S(2)}) collective-permute-start(f32[3,64,256]{2,1,0:T(8,128)S(1)} %get-tuple-element.46), channel_id=1, source_target_pairs={{0,2},{1,3},{2,0},{3,1},{4,6},{5,7},{6,4},{7,5},{8,10},{9,11},{10,... | collective-permute-start | bytes 589832 | tf_op jit(solution)/shard_map/ppermute | solution.py:348
  106.2 18.0 %collective-permute-start.18 = (f32[3,64,256]{2,1,0:T(8,128)S(1)}, f32[3,64,256]{2,1,0:T(8,128)S(1)}, u32[]{:S(2)}, u32[]{:S(2)}) collective-permute-start(f32[3,64,256]{2,1,0:T(8,128)S(1)} %get-tuple-element.47), channel_id=1, source_target_pairs={{0,3},{1,0},{2,1},{3,2},{4,7},{5,4},{6,5},{7,6},{8,11},{9,8},{10,9... | collective-permute-start | bytes 589832 | tf_op jit(solution)/shard_map/ppermute | solution.py:348
  115.1 9.2 %copy-start.1 = (s32[8]{0:T(128)S(1)}, s32[8]{0:T(128)}, u32[]{:S(2)}) copy-start(s32[8]{0:T(128)} %stack.26.t_ref) | copy-start | bytes 100
  116.3 9.4 %collective-permute-start.13 = (f32[3,64,256]{2,1,0:T(8,128)S(1)}, f32[3,64,256]{2,1,0:T(8,128)S(1)}, u32[]{:S(2)}, u32[]{:S(2)}) collective-permute-start(f32[3,64,256]{2,1,0:T(8,128)S(1)} %get-tuple-element.50), channel_id=1, source_target_pairs={{0,1},{1,2},{2,3},{3,0},{4,5},{5,6},{6,7},{7,4},{8,9},{9,10},{10,1... | collective-permute-start | bytes 589832 | tf_op jit(solution)/shard_map/ppermute | solution.py:348
  119.3 10.6 %collective-permute-start.14 = (f32[3,64,256]{2,1,0:T(8,128)S(1)}, f32[3,64,256]{2,1,0:T(8,128)S(1)}, u32[]{:S(2)}, u32[]{:S(2)}) collective-permute-start(f32[3,64,256]{2,1,0:T(8,128)S(1)} %get-tuple-element.51), channel_id=1, source_target_pairs={{0,2},{1,3},{2,0},{3,1},{4,6},{5,7},{6,4},{7,5},{8,10},{9,11},{10,... | collective-permute-start | bytes 589832 | tf_op jit(solution)/shard_map/ppermute | solution.py:348
  120.2 9.8 %collective-permute-start.15 = (f32[3,64,256]{2,1,0:T(8,128)S(1)}, f32[3,64,256]{2,1,0:T(8,128)S(1)}, u32[]{:S(2)}, u32[]{:S(2)}) collective-permute-start(f32[3,64,256]{2,1,0:T(8,128)S(1)} %get-tuple-element.52), channel_id=1, source_target_pairs={{0,3},{1,0},{2,1},{3,2},{4,7},{5,4},{6,5},{7,6},{8,11},{9,8},{10,9... | collective-permute-start | bytes 589832 | tf_op jit(solution)/shard_map/ppermute | solution.py:348

commit v4 on v3

--- a/solution.py
+++ b/solution.py
@@ -163,27 +163,56 @@
     )(f, *pieces)
 
 
-def rows_kernel(t_ref, x, s2, s1, s3, s0, sem):
+def rows_kernel(t_ref, x, back, s2, s1, s3, s0, e2, e1, e3, e0, sem, sem_extra):
+    order = ((2, s2, e2), (1, s1, e1), (3, s3, e3), (0, s0, e0))
+    at = [aligned(t_ref[j] * ROWS) for j, _, _ in order]
     pairs = []
-    for j, s in ((2, s2), (1, s1), (3, s3), (0, s0)):
+    for row, (_, s, _) in zip(at, order):
         for c in range(3):
-            row = aligned(t_ref[j] * ROWS)
             pairs.append((x.at[c, pl.ds(row, ROWS), :], s.at[pl.ds(ROWS * c, ROWS), :]))
-    for copy in start_all(sem, pairs):
+    copies = start_all(sem, pairs)
+
+    @pl.when(t_ref[2 * LON] == 0)
+    def _():
+        pairs = [
+            (back.at[:, pl.ds(aligned(row + CHUNK), CHUNK), :], e)
+            for row, (_, _, e) in zip(at, order)
+        ]
+        for copy in start_all(sem_extra, pairs):
+            copy.wait()
+
+    @pl.when(t_ref[2 * LON] == SUB - 1)
+    def _():
+        pairs = [(x.at[:, pl.ds(row, CHUNK), :], e) for row, (_, _, e) in zip(at, order)]
+        for copy in start_all(sem_extra, pairs):
+            copy.wait()
+
+    for copy in copies:
         copy.wait()
-    for s in (s2, s1, s3, s0):
+
+    @pl.when(t_ref[2 * LON] == SUB - 1)
+    def _():
+        pairs = []
+        for row, (_, s, _) in zip(at, order):
+            for c in range(3):
+                pairs.append((back.at[c, pl.ds(row, CHUNK), :], s.at[pl.ds(ROWS * c, CHUNK), :]))
+        for copy in start_all(sem, pairs):
+            copy.wait()
+
+    for _, s, _ in order:
         s[3 * ROWS :, :] = jnp.zeros((SENT - 3 * ROWS, 256), F32)
 
 
-def rows_to_send(t, x):
-    return call(
+def rows_to_send(t, x, back):
+    out = call(
         rows_kernel,
-        [array(SENT, 256)] * 4,
-        [smem_spec(), hbm_spec()],
-        [vmem_spec()] * 4,
-        [dma_sems(12)],
+        [array(SENT, 256)] * 4 + [array(3, CHUNK, 256)] * 4,
+        [smem_spec(), hbm_spec(), hbm_spec()],
+        [vmem_spec()] * 8,
+        [dma_sems(12), dma_sems(4)],
         60,
-    )(t, x)
+    )(t, x, back)
+    return out[:4], out[4:]
 
 
 def edges_kernel(t_ref, x, above, below, *refs):
@@ -290,40 +319,56 @@
     return y[:n] + y[n:] + jnp.dot(xh, low, preferred_element_type=F32)
 
 
-def weight_kernel(half, flag, f_ref, a_ref, b_ref, r_ref, *refs):
-    own, back, outs = refs[:4], refs[4:8], refs[8:]
-    start = flag[0] != 0
-    rows = slice(CHUNK * half, CHUNK * half + CHUNK)
+def weight_kernel(half, t_ref, f_ref, a_ref, b_ref, r_ref, x, *refs):
+    own, extra = refs[:3], refs[3:7]
+    come = refs[7:11] if half == 0 else None
+    outs = refs[-6:-2]
+    mine, sem = refs[-2:]
+    copy = pltpu.make_async_copy(
+        x.at[:, pl.ds(aligned(t_ref[0] * ROWS + CHUNK * half), CHUNK), :], mine, sem.at[0]
+    )
+    copy.start()
+    first = t_ref[2 * LON] == 0
+    last = t_ref[2 * LON] == SUB - 1
     for c in range(3):
         a = split(toeplitz(a_ref[c : c + 1, :], 256, 1))
         b = split(toeplitz(b_ref[c : c + 1, :], 256, -1))
         r = split(toeplitz(r_ref[c : c + 1, :], 512, -1))
+        if c == 0:
+            copy.wait()
         d = []
+        row = ROWS * c + CHUNK * half
         for block in range(4):
             f = f_ref[c, :, 256 * block : 256 * block + 256]
-            row = ROWS * c + CHUNK * half
-            prev = jnp.where(start, back[block][c, rows, :], f)
-            d.append(own[block][row : row + CHUNK, :] - prev)
+            now = mine[c] if block == 0 else own[block - 1][row : row + CHUNK, :]
+            if half == 0:
+                if block:
+                    now = jnp.where(last, extra[block][c], now)
+                prev = jnp.where(first, come[block][row : row + CHUNK, :], f)
+            else:
+                prev = jnp.where(first, extra[block][c], f)
+            d.append(now - prev)
         even, odd = d[0] + d[2], d[1] + d[3]
-        x = dot3(even + odd, *a)
-        y = dot3(even - odd, *b)
+        x0 = dot3(even + odd, *a)
+        y0 = dot3(even - odd, *b)
         w = dot3(jnp.concatenate([d[0] - d[2], d[1] - d[3]], axis=1), *r)
-        p, q = x + y, x - y
+        p, q = x0 + y0, x0 - y0
         outs[0][c] = p + w[:, :256]
         outs[1][c] = q + w[:, 256:]
         outs[2][c] = p - w[:, :256]
         outs[3][c] = q - w[:, 256:]
 
 
-def weight_call(half, flag, f, back, own, rows):
+def weight_call(half, t, f, rows, x, own, extra, come):
+    pieces = [*own, *extra, *(come if half == 0 else ())]
     return call(
         functools.partial(weight_kernel, half),
         [array(3, CHUNK, 256)] * 4,
-        [smem_spec()] + [vmem_spec()] * 12,
+        [smem_spec()] + [vmem_spec()] * 4 + [hbm_spec()] + [vmem_spec()] * len(pieces),
         [vmem_spec()] * 4,
-        [],
+        [pltpu.VMEM((3, CHUNK, 256), F32), dma_sems(1)],
         10,
-    )(flag, f, *rows, *own, *back)
+    )(t, f, *rows, x, *pieces)
 
 
 def coriolis_rows(total, first, offsets):
@@ -356,39 +401,38 @@
     sub, lat, lon = (lax.axis_index(n) for n in ("sub", "lat", "lon"))
     tile_rows = x.shape[1]
     total = tile_rows * lax.axis_size("lat")
-    t = jnp.stack(
-        [lax.rem(lon + j, LON) for j in range(LON)]
-        + [lax.rem(lon - j + LON, LON) for j in range(LON)]
-    )
+    i = jnp.arange(2 * LON + 1, dtype=jnp.int32)
+    t = lax.rem(jnp.where(i < LON, lon + i, lon - i + 2 * LON), LON)
+    t = jnp.where(i < 2 * LON, t, sub)
 
     above = lax.ppermute(x[:, tile_rows - 16 :], "lat", ring(8, 1))
     below = lax.ppermute(x[:, :16], "lat", ring(8, -1))
-
-    flag = (sub == 0).astype(jnp.int32).reshape(1)
+    sent, blocks = rows_to_send(t, x, initial_backdrop)
+    extra = {}
+    for j, block in zip((2, 1, 3, 0), blocks):
+        pairs = [(s * LON + a, s * LON + (a + j) % LON) for s in (0, SUB - 1) for a in range(LON)]
+        extra[j] = lax.ppermute(block, ("sub", "lon"), pairs) if j else block
+    extra = [extra[j] for j in (0, 3, 2, 1)]
+    sent = add_edges(t, x, above, below, sent)
+    s2, s1, s3, s0 = (to_next(v, j) for v, j in zip(sent, (2, 1, 3, 0)))
+    come = [s0, s3, s2, s1]
+
+    s0, variances = lax.optimization_barrier((s0, spectral_inverse_variances))
     first_row = lat * tile_rows + lon * ROWS
     offsets = jnp.arange(TILES + SPARE) - HALO
     f1 = coriolis_rows(total, first_row, offsets)
     f2 = coriolis_rows(total, first_row, offsets + CHUNK)
-    rows = weighting_rows(spectral_inverse_variances)
-    above, *tied = lax.optimization_barrier((above, f1, f2, flag, *rows))
-    f1, f2, flag, *rows = tied
-
-    sent = add_edges(t, x, above, below, rows_to_send(t, x))
-    s2, s1, s3, s0 = (to_next(v, j) for v, j in zip(sent, (2, 1, 3, 0)))
-    come = [s0, s3, s2, s1]
-    own = [lax.ppermute(v, "sub", ring(SUB, -1)) for v in come]
-    back = {}
-    for j in (2, 1, 3, 0):
-        block = lax.dynamic_slice(initial_backdrop, (0, ROWS * t[j], 0), (3, ROWS, 256))
-        back[j] = lax.ppermute(block, ("sub", "lon"), ring(LON, j)) if j else block
-    back = [back[j] for j in (0, 3, 2, 1)]
+    rows = weighting_rows(variances)
+    s3, *tied = lax.optimization_barrier((s3, *rows, *extra))
+    rows, extra = tied[:3], tied[3:]
+    own = [lax.ppermute(v, "sub", ring(SUB, -1)) for v in (s3, s2, s1)]
 
     m1 = model_call(False, f1, come)
-    o1 = weight_call(0, flag, m1, back, own, rows)
+    o1 = weight_call(0, t, m1, rows, x, own, extra, come)
     r1 = [to_lon(o1[j], j) if j else o1[j] for j in range(LON)]
     f2, *o1 = lax.optimization_barrier((f2, *o1))
     m2 = model_call(True, f2, come)
-    o2 = weight_call(1, flag, m2, back, own, rows)
+    o2 = weight_call(1, t, m2, rows, x, own, extra, come)
     r2 = [to_lon(o2[j], j) if j else o2[j] for j in range(LON)]
     return place(t, r2, tile_rows, place(t, r1, tile_rows))[None]
 

time: 132 us -> 138 us (1.045)
  the two profiles are of different devices: /device:TPU:24 before, /device:TPU:1 now
where the time goes in v4:
time: 138 us
  waiting for transfers between devices  53.6 us (39%)
  starting transfers between devices  44.2 us (32%)
  Pallas kernels  32.5 us (24%)
  local copies, waits for them, and re-layouts  3.51 us (3%)
  matrix products  2.76 us (2%)
    ppermute x4, waiting for transfers between devices, to_next(): return lax.ppermute(value, ('sub', 'lon'), pairs)  30.8 us
    ppermute x6, waiting for transfers between devices, to_lon(): return lax.ppermute(value, 'lon', ring(LON, j))  18.3 us
    pallas_call x2, Pallas kernels, model_call(): call(functools.partial(model_kernel, second), array(3, CHUNK, NLON), [sme...  17.6 us
    ppermute x6, starting transfers between devices, to_lon(): return lax.ppermute(value, 'lon', ring(LON, j))  13.4 us
    ppermute x4, starting transfers between devices, to_next(): return lax.ppermute(value, ('sub', 'lon'), pairs)  12.8 us
    ppermute x3, starting transfers between devices, shards(): own = [lax.ppermute(v, 'sub', ring(SUB, -1)) for v in (s3, s2, s1)]  11.1 us
    pallas_call x2, Pallas kernels, weight_call(): call(functools.partial(weight_kernel, half), [array(3, CHUNK, 256)] * 4,...  5.58 us
    ppermute x1, starting transfers between devices, shards(): below = lax.ppermute(x[:, :16], 'lat', ring(8, -1))  4.98 us
  transfers between devices with their start and end apart: 18, of which 6 were waited for; matrix products, arithmetic and copies ran while one was open for 2% of the time, Pallas kernels for 19%

profile of v4, /device:TPU:1, one launch (start us, length us, event | category | flops | bytes accessed | tf_op | source)
XLA Modules:
  0.0 137.6 jit_solution(10357915056858807912)
XLA Ops:
  0.0 0.8 fusion.6
  0.8 5.0 %collective-permute-start.1 = (f32[3,16,256]{2,1,0:T(8,128)S(1)}, f32[3,16,256]{2,1,0:T(8,128)S(1)}, u32[]{:S(2)}, u32[]{:S(2)}) collective-permute-start(f32[3,16,256]{2,1,0:T(8,128)S(1)} %get-tuple-element.65), channel_id=1, source_target_pairs={{0,28},{4,0},{8,4},{12,8},{16,12},{20,16},{24,20},{28,24},{1,29},{... | collective-permute-start | bytes 147464 | tf_op jit(solution)/shard_map/ppermute | solution.py:409
  6.3 3.7 %shard_map.46 = (f32[440,256]{1,0:T(8,128)}, f32[440,256]{1,0:T(8,128)}, f32[440,256]{1,0:T(8,128)}, f32[440,256]{1,0:T(8,128)}, f32[3,64,256]{2,1,0:T(8,128)}, ...) custom-call(s32[9]{0:T(128)} %compare_select_fusion.3.t_ref, f32[3,512,256]{2,1,0:T(8,128)} %bitcast.5, ...), custom_call_target="tpu_custom_call" | custom-call | bytes 1 | tf_op jit(solution)/shard_map/pallas_call | solution.py:207
  10.1 0.8 collective-permute-done.above
  11.5 2.6 %shard_map.47 = (f32[440,256]{1,0:T(8,128)}, f32[440,256]{1,0:T(8,128)}, f32[440,256]{1,0:T(8,128)}, f32[440,256]{1,0:T(8,128)}) custom-call(s32[9]{0:T(128)} %compare_select_fusion.3.t_ref, f32[3,512,256]{2,1,0:T(8,128)} %bitcast.6, f32[3,16,256]{2,1,0:T(8,128)} %copy-done.11, ...), custom_call_target="tpu_custom_call", output_to_operand_aliasing={{0}: (4, {}), {1}: (5, {}), {2}: (6, {}), {3}: (7, {})} | custom-call | bytes 1 | tf_op jit(solution)/shard_map/pallas_call | solution.py:246
  14.1 3.2 %collective-permute-start.2 = (f32[440,256]{1,0:T(8,128)}, f32[440,256]{1,0:T(8,128)S(1)}, u32[]{:S(2)}, u32[]{:S(2)}) collective-permute-start(f32[440,256]{1,0:T(8,128)} %get-tuple-element.39), channel_id=1, source_target_pairs={{0,32},{1,33},{2,34},{3,35},{32,64},{33,65},{34,66},{35,67},{64,96... | collective-permute-start | bytes 1351688 | tf_op jit(solution)/shard_map/ppermute | solution.py:389
  17.4 0.7 collective-permute-start.6
  18.0 0.7 collective-permute-start.7
  18.7 5.1 %collective-permute-start.3 = (f32[440,256]{1,0:T(8,128)}, f32[440,256]{1,0:T(8,128)S(1)}, u32[]{:S(2)}, u32[]{:S(2)}) collective-permute-start(f32[440,256]{1,0:T(8,128)} %get-tuple-element.40), channel_id=1, source_target_pairs={{0,35},{1,32},{2,33},{3,34},{32,67},{33,64},{34,65},{35,66},{64,99... | collective-permute-start | bytes 1351688 | tf_op jit(solution)/shard_map/ppermute | solution.py:389
  23.8 2.5 %collective-permute-start.4 = (f32[440,256]{1,0:T(8,128)}, f32[440,256]{1,0:T(8,128)S(1)}, u32[]{:S(2)}, u32[]{:S(2)}) collective-permute-start(f32[440,256]{1,0:T(8,128)} %get-tuple-element.41), channel_id=1, source_target_pairs={{0,34},{1,35},{2,32},{3,33},{32,66},{33,67},{34,64},{35,65},{64,98... | collective-permute-start | bytes 1351688 | tf_op jit(solution)/shard_map/ppermute | solution.py:389
  26.3 2.0 %collective-permute-start.5 = (f32[440,256]{1,0:T(8,128)}, f32[440,256]{1,0:T(8,128)S(1)}, u32[]{:S(2)}, u32[]{:S(2)}) collective-permute-start(f32[440,256]{1,0:T(8,128)} %get-tuple-element.42), channel_id=1, source_target_pairs={{0,33},{1,34},{2,35},{3,32},{32,65},{33,66},{34,67},{35,64},{64,97... | collective-permute-start | bytes 1351688 | tf_op jit(solution)/shard_map/ppermute | solution.py:389
  28.3 2.8 %fusion.7 = f32[3,1024]{1,0:T(4,128)S(1)} fusion(f32[3,513]{1,0:T(4,128)S(1)} %copy-done, f32[513,1024]{1,0:T(8,128)} %constant.47.clone), kind=kOutput, calls=%fused_computation.16 | convolution fusion | flops 18911232 | bytes 2119692 | tf_op jit(solution)/shard_map/dot_general | solution.py:308
  31.1 0.7 copy-done.3
  31.7 0.7 collective-permute-start.8
  33.1 0.7 copy-done.7
  33.8 30.8 %collective-permute-done.3.s3.refs_8_ = f32[440,256]{1,0:T(8,128)S(1)} collective-permute-done((f32[440,256]{1,0:T(8,128)}, f32[440,256]{1,0:T(8,128)S(1)}, u32[]{:S(2)}, u32[]{:S(2)}) %collective-permute-start.3) | collective-permute-done | bytes 450592 | tf_op jit(solution)/shard_map/ppermute | solution.py:389
  64.5 11.1 %collective-permute-start.9 = (f32[440,256]{1,0:T(8,128)S(1)}, f32[440,256]{1,0:T(8,128)}, u32[]{:S(2)}, u32[]{:S(2)}) collective-permute-start(f32[440,256]{1,0:T(8,128)S(1)} %collective-permute-done.3.s3.refs_8_), channel_id=1, source_target_pairs={{0,224},{32,0},{64,32},{96,64},{128,96},{160,128},{192,160},{224,1... | collective-permute-start | bytes 1351688 | tf_op jit(solution)/shard_map/ppermute | solution.py:428
  75.7 8.8 %shard_map.48.f_ref = f32[3,64,1024]{2,1,0:T(8,128)S(1)} custom-call(f32[114]{0:T(128)S(1)} %sine_multiply_fusion.f_ref, f32[440,256]{1,0:T(8,128)S(1)} %collective-permute-done.2.s0.refs_7_, f32[440,256]{1,0:T(8,128)S(1)} %collective-permute-done.3.s3.refs_8_, f32[440,256]{1,0:T(8,128)S(1)} %collective-permute-done.4.s2.refs_9_, ...), custom_call_target="tpu_custom_call" | custom-call | bytes 1 | tf_op jit(solution)/shard_map/pallas_call | solution.py:156
  84.6 3.8 %collective-permute-done.11.refs_2_ = f32[440,256]{1,0:T(8,128)} collective-permute-done((f32[440,256]{1,0:T(8,128)S(1)}, f32[440,256]{1,0:T(8,128)}, u32[]{:S(2)}, u32[]{:S(2)}) %collective-permute-start.11) | collective-permute-done | bytes 450592 | tf_op jit(solution)/shard_map/ppermute | solution.py:428
  88.4 2.8 %shard_map.49 = (f32[3,64,256]{2,1,0:T(8,128)S(1)}, f32[3,64,256]{2,1,0:T(8,128)S(1)}, f32[3,64,256]{2,1,0:T(8,128)S(1)}, f32[3,64,256]{2,1,0:T(8,128)S(1)}) custom-call(s32[9]{0:T(128)S(1)} %copy-done.9, f32[3,64,1024]{2,1,0:T(8,128)S(1)} %shard_map.48.f_ref, f32[3,256]{1,0:T(4,128)S(1)} %get-tuple-element.48.a_ref, f32[3,256]{1,0:T(4,128)S(1)} %get-tuple-element.49.b_ref, ...), custom_call_target="tpu_custom_call" | custom-call | bytes 1 | tf_op jit(solution)/shard_map/pallas_call | solution.py:364
  91.2 1.8 %collective-permute-start.15 = (f32[3,64,256]{2,1,0:T(8,128)S(1)}, f32[3,64,256]{2,1,0:T(8,128)S(1)}, u32[]{:S(2)}, u32[]{:S(2)}) collective-permute-start(f32[3,64,256]{2,1,0:T(8,128)S(1)} %get-tuple-element.57), channel_id=1, source_target_pairs={{0,1},{1,2},{2,3},{3,0},{4,5},{5,6},{6,7},{7,4},{8,9},{9,10},{10,1... | collective-permute-start | bytes 589832 | tf_op jit(solution)/shard_map/ppermute | solution.py:393
  93.1 4.1 %collective-permute-start.16 = (f32[3,64,256]{2,1,0:T(8,128)S(1)}, f32[3,64,256]{2,1,0:T(8,128)S(1)}, u32[]{:S(2)}, u32[]{:S(2)}) collective-permute-start(f32[3,64,256]{2,1,0:T(8,128)S(1)} %get-tuple-element.58), channel_id=1, source_target_pairs={{0,2},{1,3},{2,0},{3,1},{4,6},{5,7},{6,4},{7,5},{8,10},{9,11},{10,... | collective-permute-start | bytes 589832 | tf_op jit(solution)/shard_map/ppermute | solution.py:393
  97.2 3.6 %collective-permute-start.17 = (f32[3,64,256]{2,1,0:T(8,128)S(1)}, f32[3,64,256]{2,1,0:T(8,128)S(1)}, u32[]{:S(2)}, u32[]{:S(2)}) collective-permute-start(f32[3,64,256]{2,1,0:T(8,128)S(1)} %get-tuple-element.59), channel_id=1, source_target_pairs={{0,3},{1,0},{2,1},{3,2},{4,7},{5,4},{6,5},{7,6},{8,11},{9,8},{10,9... | collective-permute-start | bytes 589832 | tf_op jit(solution)/shard_map/ppermute | solution.py:393
  100.8 8.8 %shard_map.50.f_ref = f32[3,64,1024]{2,1,0:T(8,128)S(1)} custom-call(f32[114]{0:T(128)S(1)} %sine_multiply_fusion.1.f_ref, f32[440,256]{1,0:T(8,128)S(1)} %collective-permute-done.2.s0.refs_7_, f32[440,256]{1,0:T(8,128)S(1)} %collective-permute-done.3.s3.refs_8_, f32[440,256]{1,0:T(8,128)S(1)} %collective-permute-done.4.s2.refs_9_, ...), custom_call_target="tpu_custom_call" | custom-call | bytes 1 | tf_op jit(solution)/shard_map/pallas_call | solution.py:156
  109.6 2.8 %shard_map.51 = (f32[3,64,256]{2,1,0:T(8,128)S(1)}, f32[3,64,256]{2,1,0:T(8,128)S(1)}, f32[3,64,256]{2,1,0:T(8,128)S(1)}, f32[3,64,256]{2,1,0:T(8,128)S(1)}) custom-call(s32[9]{0:T(128)S(1)} %copy-done.9, f32[3,64,1024]{2,1,0:T(8,128)S(1)} %shard_map.50.f_ref, f32[3,256]{1,0:T(4,128)S(1)} %get-tuple-element.48.a_ref, f32[3,256]{1,0:T(4,128)S(1)} %get-tuple-element.49.b_ref, ...), custom_call_target="tpu_custom_call" | custom-call | bytes 1 | tf_op jit(solution)/shard_map/pallas_call | solution.py:364
  112.4 2.1 %collective-permute-start.13 = (f32[3,64,256]{2,1,0:T(8,128)S(1)}, f32[3,64,256]{2,1,0:T(8,128)S(1)}, u32[]{:S(2)}, u32[]{:S(2)}) collective-permute-start(f32[3,64,256]{2,1,0:T(8,128)S(1)} %get-tuple-element.63), channel_id=1, source_target_pairs={{0,2},{1,3},{2,0},{3,1},{4,6},{5,7},{6,4},{7,5},{8,10},{9,11},{10,... | collective-permute-start | bytes 589832 | tf_op jit(solution)/shard_map/ppermute | solution.py:393
  114.5 1.8 %collective-permute-start.14 = (f32[3,64,256]{2,1,0:T(8,128)S(1)}, f32[3,64,256]{2,1,0:T(8,128)S(1)}, u32[]{:S(2)}, u32[]{:S(2)}) collective-permute-start(f32[3,64,256]{2,1,0:T(8,128)S(1)} %get-tuple-element.64), channel_id=1, source_target_pairs={{0,3},{1,0},{2,1},{3,2},{4,7},{5,4},{6,5},{7,6},{8,11},{9,8},{10,9... | collective-permute-start | bytes 589832 | tf_op jit(solution)/shard_map/ppermute | solution.py:393
  116.3 1.4 %shard_map.52.refs_0_ = f32[3,512,256]{2,1,0:T(8,128)} custom-call(s32[9]{0:T(128)S(1)} %copy-done.9, f32[3,64,256]{2,1,0:T(8,128)S(1)} %get-tuple-element.56.o0, f32[3,64,256]{2,1,0:T(8,128)S(1)} %collective-permute-done.15.r1, f32[3,64,256]{2,1,0:T(8,128)S(1)} %collective-permute-done.16.r2, f32[3,64,256]{2,1,0:T(8,128)S(1)} %collective-permute-done.17.r3), custom_call_target="tpu_custom_call" | custom-call | bytes 1 | tf_op jit(solution)/shard_map/pallas_call | solution.py:274
  117.7 1.4 %collective-permute-done.12.r1 = f32[3,64,256]{2,1,0:T(8,128)S(1)} collective-permute-done((f32[3,64,256]{2,1,0:T(8,128)S(1)}, f32[3,64,256]{2,1,0:T(8,128)S(1)}, u32[]{:S(2)}, u32[]{:S(2)}) %collective-permute-start.12) | collective-permute-done | bytes 196640 | tf_op jit(solution)/shard_map/ppermute | solution.py:393
  119.2 11.5 %collective-permute-done.13.r2 = f32[3,64,256]{2,1,0:T(8,128)S(1)} collective-permute-done((f32[3,64,256]{2,1,0:T(8,128)S(1)}, f32[3,64,256]{2,1,0:T(8,128)S(1)}, u32[]{:S(2)}, u32[]{:S(2)}) %collective-permute-start.13) | collective-permute-done | bytes 196640 | tf_op jit(solution)/shard_map/ppermute | solution.py:393
  130.7 5.3 %collective-permute-done.14.r3 = f32[3,64,256]{2,1,0:T(8,128)S(1)} collective-permute-done((f32[3,64,256]{2,1,0:T(8,128)S(1)}, f32[3,64,256]{2,1,0:T(8,128)S(1)}, u32[]{:S(2)}, u32[]{:S(2)}) %collective-permute-start.14) | collective-permute-done | bytes 196640 | tf_op jit(solution)/shard_map/ppermute | solution.py:393
  136.0 1.4 %shard_map.53 = f32[3,512,256]{2,1,0:T(8,128)} custom-call(s32[9]{0:T(128)S(1)} %copy-done.9, f32[3,64,256]{2,1,0:T(8,128)S(1)} %get-tuple-element.61.o0, f32[3,64,256]{2,1,0:T(8,128)S(1)} %collective-permute-done.12.r1, f32[3,64,256]{2,1,0:T(8,128)S(1)} %collective-permute-done.13.r2, ...), custom_call_target="tpu_custom_call", output_to_operand_aliasing={{}: (5, {})} | custom-call | bytes 1 | tf_op jit(solution)/shard_map/pallas_call | solution.py:274
  (49 shorter events, 2.1 us)
Async XLA Ops:
  0.0 28.3 %copy-start = (f32[3,513]{1,0:T(4,128)S(1)}, f32[3,513]{1,0:T(4,128)}, u32[]{:S(2)}) copy-start(f32[3,513]{1,0:T(4,128)} %param.6) | copy-start | bytes 18472
  0.8 9.2 %collective-permute-start.1 = (f32[3,16,256]{2,1,0:T(8,128)S(1)}, f32[3,16,256]{2,1,0:T(8,128)S(1)}, u32[]{:S(2)}, u32[]{:S(2)}) collective-permute-start(f32[3,16,256]{2,1,0:T(8,128)S(1)} %get-tuple-element.65), channel_id=1, source_target_pairs={{0,28},{4,0},{8,4},{12,8},{16,12},{20,16},{24,20},{28,24},{1,29},{... | collective-permute-start | bytes 147464 | tf_op jit(solution)/shard_map/ppermute | solution.py:409
  5.8 5.0 %collective-permute-start = (f32[3,16,256]{2,1,0:T(8,128)S(1)}, f32[3,16,256]{2,1,0:T(8,128)S(1)}, u32[]{:S(2)}, u32[]{:S(2)}) collective-permute-start(f32[3,16,256]{2,1,0:T(8,128)S(1)} %get-tuple-element.66), channel_id=1, source_target_pairs={{0,4},{4,8},{8,12},{12,16},{16,20},{20,24},{24,28},{28,0},{1,5},{5... | collective-permute-start | bytes 147464 | tf_op jit(solution)/shard_map/ppermute | solution.py:408
  10.1 0.8 copy-start.10
  11.5 5.9 %copy-start.14 = (f32[3,64,256]{2,1,0:T(8,128)S(1)}, f32[3,64,256]{2,1,0:T(8,128)}, u32[]{:S(2)}) copy-start(f32[3,64,256]{2,1,0:T(8,128)} %get-tuple-element.45) | copy-start | bytes 589828
  11.5 6.5 %copy-start.13 = (f32[3,64,256]{2,1,0:T(8,128)S(1)}, f32[3,64,256]{2,1,0:T(8,128)}, u32[]{:S(2)}) copy-start(f32[3,64,256]{2,1,0:T(8,128)} %get-tuple-element.46) | copy-start | bytes 589828
  14.1 17.6 %copy-start.12 = (f32[3,64,256]{2,1,0:T(8,128)S(1)}, f32[3,64,256]{2,1,0:T(8,128)}, u32[]{:S(2)}) copy-start(f32[3,64,256]{2,1,0:T(8,128)} %get-tuple-element.47) | copy-start | bytes 589828
  14.1 12.1 %collective-permute-start.2 = (f32[440,256]{1,0:T(8,128)}, f32[440,256]{1,0:T(8,128)S(1)}, u32[]{:S(2)}, u32[]{:S(2)}) collective-permute-start(f32[440,256]{1,0:T(8,128)} %get-tuple-element.39), channel_id=1, source_target_pairs={{0,32},{1,33},{2,34},{3,35},{32,64},{33,65},{34,66},{35,67},{64,96... | collective-permute-start | bytes 1351688 | tf_op jit(solution)/shard_map/ppermute | solution.py:389
  17.4 13.7 %collective-permute-start.6 = (f32[3,64,256]{2,1,0:T(8,128)S(1)}, f32[3,64,256]{2,1,0:T(8,128)S(1)}, u32[]{:S(2)}, u32[]{:S(2)}) collective-permute-start(f32[3,64,256]{2,1,0:T(8,128)S(1)} %copy-done.14), channel_id=1, source_target_pairs={{0,3},{1,0},{2,1},{3,2},{224,227},{225,224},{226,225},{227,226},{4... | collective-permute-start | bytes 589832 | tf_op jit(solution)/shard_map/ppermute | solution.py:414
  18.0 14.4 %collective-permute-start.7 = (f32[3,64,256]{2,1,0:T(8,128)S(1)}, f32[3,64,256]{2,1,0:T(8,128)S(1)}, u32[]{:S(2)}, u32[]{:S(2)}) collective-permute-start(f32[3,64,256]{2,1,0:T(8,128)S(1)} %copy-done.13), channel_id=1, source_target_pairs={{0,2},{1,3},{2,0},{3,1},{224,226},{225,227},{226,224},{227,225},{4... | collective-permute-start | bytes 589832 | tf_op jit(solution)/shard_map/ppermute | solution.py:414
  18.7 45.8 %collective-permute-start.3 = (f32[440,256]{1,0:T(8,128)}, f32[440,256]{1,0:T(8,128)S(1)}, u32[]{:S(2)}, u32[]{:S(2)}) collective-permute-start(f32[440,256]{1,0:T(8,128)} %get-tuple-element.40), channel_id=1, source_target_pairs={{0,35},{1,32},{2,33},{3,34},{32,67},{33,64},{34,65},{35,66},{64,99... | collective-permute-start | bytes 1351688 | tf_op jit(solution)/shard_map/ppermute | solution.py:389
  23.8 51.8 %collective-permute-start.4 = (f32[440,256]{1,0:T(8,128)}, f32[440,256]{1,0:T(8,128)S(1)}, u32[]{:S(2)}, u32[]{:S(2)}) collective-permute-start(f32[440,256]{1,0:T(8,128)} %get-tuple-element.41), channel_id=1, source_target_pairs={{0,34},{1,35},{2,32},{3,33},{32,66},{33,67},{34,64},{35,65},{64,98... | collective-permute-start | bytes 1351688 | tf_op jit(solution)/shard_map/ppermute | solution.py:389
  26.3 49.3 %collective-permute-start.5 = (f32[440,256]{1,0:T(8,128)}, f32[440,256]{1,0:T(8,128)S(1)}, u32[]{:S(2)}, u32[]{:S(2)}) collective-permute-start(f32[440,256]{1,0:T(8,128)} %get-tuple-element.42), channel_id=1, source_target_pairs={{0,33},{1,34},{2,35},{3,32},{32,65},{33,66},{34,67},{35,64},{64,97... | collective-permute-start | bytes 1351688 | tf_op jit(solution)/shard_map/ppermute | solution.py:389
  31.0 57.3 %copy-start.1 = (f32[1,3,512,256]{3,2,1,0:T(8,128)S(1)}, f32[1,3,512,256]{3,2,1,0:T(8,128)}, u32[]{:S(2)}) copy-start(f32[1,3,512,256]{3,2,1,0:T(8,128)} %param.4) | copy-start | bytes 4718596
  31.0 57.3 %copy-start.9 = (s32[9]{0:T(128)S(1)}, s32[9]{0:T(128)}, u32[]{:S(2)}) copy-start(s32[9]{0:T(128)} %compare_select_fusion.3.t_ref) | copy-start | bytes 112
  31.1 0.7 copy-start.3
  31.7 1.4 collective-permute-start.8
  32.4 0.7 copy-start.5
  33.1 0.7 copy-start.7
  64.5 20.0 %collective-permute-start.9 = (f32[440,256]{1,0:T(8,128)S(1)}, f32[440,256]{1,0:T(8,128)}, u32[]{:S(2)}, u32[]{:S(2)}) collective-permute-start(f32[440,256]{1,0:T(8,128)S(1)} %collective-permute-done.3.s3.refs_8_), channel_id=1, source_target_pairs={{0,224},{32,0},{64,32},{96,64},{128,96},{160,128},{192,160},{224,1... | collective-permute-start | bytes 1351688 | tf_op jit(solution)/shard_map/ppermute | solution.py:428
  75.6 9.0 %collective-permute-start.10 = (f32[440,256]{1,0:T(8,128)S(1)}, f32[440,256]{1,0:T(8,128)}, u32[]{:S(2)}, u32[]{:S(2)}) collective-permute-start(f32[440,256]{1,0:T(8,128)S(1)} %collective-permute-done.4.s2.refs_9_), channel_id=1, source_target_pairs={{0,224},{32,0},{64,32},{96,64},{128,96},{160,128},{192,160},{224,1... | collective-permute-start | bytes 1351688 | tf_op jit(solution)/shard_map/ppermute | solution.py:428
  75.6 12.7 %collective-permute-start.11 = (f32[440,256]{1,0:T(8,128)S(1)}, f32[440,256]{1,0:T(8,128)}, u32[]{:S(2)}, u32[]{:S(2)}) collective-permute-start(f32[440,256]{1,0:T(8,128)S(1)} %collective-permute-done.5.s1.refs_10_), channel_id=1, source_target_pairs={{0,224},{32,0},{64,32},{96,64},{128,96},{160,128},{192,160},{224,1... | collective-permute-start | bytes 1351688 | tf_op jit(solution)/shard_map/ppermute | solution.py:428
  75.6 12.7 %copy-start.2 = (f32[3,64,256]{2,1,0:T(8,128)S(1)}, f32[3,64,256]{2,1,0:T(8,128)}, u32[]{:S(2)}) copy-start(f32[3,64,256]{2,1,0:T(8,128)} %get-tuple-element.52.refs_3_) | copy-start | bytes 589828
  75.7 12.7 %copy-start.4 = (f32[3,64,256]{2,1,0:T(8,128)S(1)}, f32[3,64,256]{2,1,0:T(8,128)}, u32[]{:S(2)}) copy-start(f32[3,64,256]{2,1,0:T(8,128)} %copy-done.3) | copy-start | bytes 589828
  75.7 12.7 %copy-start.6 = (f32[3,64,256]{2,1,0:T(8,128)S(1)}, f32[3,64,256]{2,1,0:T(8,128)}, u32[]{:S(2)}) copy-start(f32[3,64,256]{2,1,0:T(8,128)} %copy-done.5) | copy-start | bytes 589828
  75.7 12.7 %copy-start.8 = (f32[3,64,256]{2,1,0:T(8,128)S(1)}, f32[3,64,256]{2,1,0:T(8,128)}, u32[]{:S(2)}) copy-start(f32[3,64,256]{2,1,0:T(8,128)} %copy-done.7) | copy-start | bytes 589828
  91.2 23.3 %collective-permute-start.15 = (f32[3,64,256]{2,1,0:T(8,128)S(1)}, f32[3,64,256]{2,1,0:T(8,128)S(1)}, u32[]{:S(2)}, u32[]{:S(2)}) collective-permute-start(f32[3,64,256]{2,1,0:T(8,128)S(1)} %get-tuple-element.57), channel_id=1, source_target_pairs={{0,1},{1,2},{2,3},{3,0},{4,5},{5,6},{6,7},{7,4},{8,9},{9,10},{10,1... | collective-permute-start | bytes 589832 | tf_op jit(solution)/shard_map/ppermute | solution.py:393
  93.1 23.2 %collective-permute-start.16 = (f32[3,64,256]{2,1,0:T(8,128)S(1)}, f32[3,64,256]{2,1,0:T(8,128)S(1)}, u32[]{:S(2)}, u32[]{:S(2)}) collective-permute-start(f32[3,64,256]{2,1,0:T(8,128)S(1)} %get-tuple-element.58), channel_id=1, source_target_pairs={{0,2},{1,3},{2,0},{3,1},{4,6},{5,7},{6,4},{7,5},{8,10},{9,11},{10,... | collective-permute-start | bytes 589832 | tf_op jit(solution)/shard_map/ppermute | solution.py:393
  97.2 19.1 %collective-permute-start.17 = (f32[3,64,256]{2,1,0:T(8,128)S(1)}, f32[3,64,256]{2,1,0:T(8,128)S(1)}, u32[]{:S(2)}, u32[]{:S(2)}) collective-permute-start(f32[3,64,256]{2,1,0:T(8,128)S(1)} %get-tuple-element.59), channel_id=1, source_target_pairs={{0,3},{1,0},{2,1},{3,2},{4,7},{5,4},{6,5},{7,6},{8,11},{9,8},{10,9... | collective-permute-start | bytes 589832 | tf_op jit(solution)/shard_map/ppermute | solution.py:393
  112.4 6.8 %collective-permute-start.12 = (f32[3,64,256]{2,1,0:T(8,128)S(1)}, f32[3,64,256]{2,1,0:T(8,128)S(1)}, u32[]{:S(2)}, u32[]{:S(2)}) collective-permute-start(f32[3,64,256]{2,1,0:T(8,128)S(1)} %get-tuple-element.62), channel_id=1, source_target_pairs={{0,1},{1,2},{2,3},{3,0},{4,5},{5,6},{6,7},{7,4},{8,9},{9,10},{10,1... | collective-permute-start | bytes 589832 | tf_op jit(solution)/shard_map/ppermute | solution.py:393
  112.4 18.3 %collective-permute-start.13 = (f32[3,64,256]{2,1,0:T(8,128)S(1)}, f32[3,64,256]{2,1,0:T(8,128)S(1)}, u32[]{:S(2)}, u32[]{:S(2)}) collective-permute-start(f32[3,64,256]{2,1,0:T(8,128)S(1)} %get-tuple-element.63), channel_id=1, source_target_pairs={{0,2},{1,3},{2,0},{3,1},{4,6},{5,7},{6,4},{7,5},{8,10},{9,11},{10,... | collective-permute-start | bytes 589832 | tf_op jit(solution)/shard_map/ppermute | solution.py:393
  114.5 21.5 %collective-permute-start.14 = (f32[3,64,256]{2,1,0:T(8,128)S(1)}, f32[3,64,256]{2,1,0:T(8,128)S(1)}, u32[]{:S(2)}, u32[]{:S(2)}) collective-permute-start(f32[3,64,256]{2,1,0:T(8,128)S(1)} %get-tuple-element.64), channel_id=1, source_target_pairs={{0,3},{1,0},{2,1},{3,2},{4,7},{5,4},{6,5},{7,6},{8,11},{9,8},{10,9... | collective-permute-start | bytes 589832 | tf_op jit(solution)/shard_map/ppermute | solution.py:393
  (1 other events, 0.6 us)

commit v5 on v4

--- a/solution.py
+++ b/solution.py
@@ -124,19 +124,36 @@
     lax.fori_loop(0, -(-rows // GROUP), body, 0)
 
 
-def model_kernel(second, f_ref, s0, s3, s2, s1, out, *bufs):
+def half_of(chunk, t_ref):
+    swapped = jnp.where(t_ref[2 * LON] == SUB - 1, 1, 0)
+    return 1 - swapped if chunk else swapped
+
+
+def model_kernel(chunk, t_ref, f_ref, s0, s3, s2, s1, out, *bufs):
     x, b, c, y = bufs
-    for block, s in enumerate((s0, s3, s2, s1)):
-        for field in range(3):
-            row = ROWS * field
-            edge = 3 * ROWS + 2 * HALO * field
-            if second:
-                unpack_rows(x, s, field, row + CHUNK - HALO, 1, 0, block)
-                unpack_rows(x, s, field, row + CHUNK - HALO + 1, CHUNK + HALO - 1, 1, block)
-                unpack_rows(x, s, field, edge + HALO, HALO, CHUNK + HALO, block)
-            else:
-                unpack_rows(x, s, field, edge, HALO, 0, block)
-                unpack_rows(x, s, field, row, CHUNK + HALO, HALO, block)
+    half = half_of(chunk, t_ref)
+
+    def unpack(second):
+        for block, s in enumerate((s0, s3, s2, s1)):
+            for field in range(3):
+                row = ROWS * field
+                edge = 3 * ROWS + 2 * HALO * field
+                if second:
+                    unpack_rows(x, s, field, row + CHUNK - HALO, 1, 0, block)
+                    unpack_rows(x, s, field, row + CHUNK - HALO + 1, CHUNK + HALO - 1, 1, block)
+                    unpack_rows(x, s, field, edge + HALO, HALO, CHUNK + HALO, block)
+                else:
+                    unpack_rows(x, s, field, edge, HALO, 0, block)
+                    unpack_rows(x, s, field, row, CHUNK + HALO, HALO, block)
+
+    @pl.when(half == 0)
+    def _():
+        unpack(False)
+
+    @pl.when(half == 1)
+    def _():
+        unpack(True)
+
     done = 0
     for _ in range(STEPS):
         for kind, (src, base, dst) in enumerate(((x, x, b), (b, x, c), (c, x, y))):
@@ -152,15 +169,15 @@
                 )
 
 
-def model_call(second, f, pieces):
+def model_call(chunk, t, f, pieces):
     return call(
-        functools.partial(model_kernel, second),
+        functools.partial(model_kernel, chunk),
         array(3, CHUNK, NLON),
-        [smem_spec()] + [vmem_spec()] * 4,
+        [smem_spec()] * 2 + [vmem_spec()] * 4,
         vmem_spec(),
         [pltpu.VMEM((3, (TILES + SPARE) * 8, 128), F32)] * 4,
         10,
-    )(f, *pieces)
+    )(t, f, *pieces)
 
 
 def rows_kernel(t_ref, x, back, s2, s1, s3, s0, e2, e1, e3, e0, sem, sem_extra):
@@ -259,25 +276,29 @@
     )(t, x, above, below, *sent)
 
 
-def place_kernel(first, t_ref, o0, r1, r2, r3, *refs):
-    out, sem = refs[-2:]
-    pairs = [
-        (r, out.at[:, pl.ds(aligned(t_ref[LON + j] * ROWS + first), CHUNK), :])
-        for j, r in enumerate((o0, r1, r2, r3))
-    ]
-    for copy in start_all(sem, pairs):
+def place_kernel(chunk, t_ref, o0, r1, r2, r3, *refs):
+    out, buf, sem, sem_out = refs[-4:]
+    first = CHUNK * half_of(chunk, t_ref)
+    copies = start_all(sem, [(r, buf.at[j]) for j, r in enumerate((o0, r1, r2, r3))])
+    outs = []
+    for j, copy in enumerate(copies):
+        copy.wait()
+        where = out.at[:, pl.ds(aligned(t_ref[LON + j] * ROWS + first), CHUNK), :]
+        outs.append(pltpu.make_async_copy(buf.at[j], where, sem_out.at[j]))
+        outs[-1].start()
+    for copy in outs:
         copy.wait()
 
 
 def place(t, pieces, rows, begun=None):
     extra = [] if begun is None else [begun]
     return call(
-        functools.partial(place_kernel, CHUNK if extra else 0),
+        functools.partial(place_kernel, 1 if extra else 0),
         [array(3, rows, 256)],
         [smem_spec()] + [hbm_spec()] * (4 + len(extra)),
         [hbm_spec()],
-        [dma_sems(4)],
-        2,
+        [pltpu.VMEM((4, 3, CHUNK, 256), F32), dma_sems(4), dma_sems(4)],
+        3,
         input_output_aliases={5: 0} if extra else {},
     )(t, *pieces, *extra)[0]
 
@@ -319,34 +340,25 @@
     return y[:n] + y[n:] + jnp.dot(xh, low, preferred_element_type=F32)
 
 
-def weight_kernel(half, t_ref, f_ref, a_ref, b_ref, r_ref, x, *refs):
-    own, extra = refs[:3], refs[3:7]
-    come = refs[7:11] if half == 0 else None
-    outs = refs[-6:-2]
-    mine, sem = refs[-2:]
-    copy = pltpu.make_async_copy(
-        x.at[:, pl.ds(aligned(t_ref[0] * ROWS + CHUNK * half), CHUNK), :], mine, sem.at[0]
-    )
-    copy.start()
+def weight_kernel(chunk, t_ref, f_ref, a_ref, b_ref, r_ref, *refs):
+    own, other, outs = refs[:4], refs[4:8], refs[8:]
+    half = half_of(chunk, t_ref)
     first = t_ref[2 * LON] == 0
     last = t_ref[2 * LON] == SUB - 1
     for c in range(3):
         a = split(toeplitz(a_ref[c : c + 1, :], 256, 1))
         b = split(toeplitz(b_ref[c : c + 1, :], 256, -1))
         r = split(toeplitz(r_ref[c : c + 1, :], 512, -1))
-        if c == 0:
-            copy.wait()
         d = []
-        row = ROWS * c + CHUNK * half
+        rows = pl.ds(pl.multiple_of(ROWS * c + CHUNK * half, CHUNK), CHUNK)
         for block in range(4):
             f = f_ref[c, :, 256 * block : 256 * block + 256]
-            now = mine[c] if block == 0 else own[block - 1][row : row + CHUNK, :]
-            if half == 0:
-                if block:
-                    now = jnp.where(last, extra[block][c], now)
-                prev = jnp.where(first, come[block][row : row + CHUNK, :], f)
+            now = own[block][rows, :]
+            if chunk == 0:
+                prev = jnp.where(first, other[block][rows, :], f)
             else:
-                prev = jnp.where(first, extra[block][c], f)
+                now = jnp.where(last, other[block][c], now)
+                prev = jnp.where(first, other[block][c], f)
             d.append(now - prev)
         even, odd = d[0] + d[2], d[1] + d[3]
         x0 = dot3(even + odd, *a)
@@ -359,16 +371,16 @@
         outs[3][c] = q - w[:, 256:]
 
 
-def weight_call(half, t, f, rows, x, own, extra, come):
-    pieces = [*own, *extra, *(come if half == 0 else ())]
+def weight_call(chunk, t, f, rows, own, other):
+    pieces = [*own, *other]
     return call(
-        functools.partial(weight_kernel, half),
+        functools.partial(weight_kernel, chunk),
         [array(3, CHUNK, 256)] * 4,
-        [smem_spec()] + [vmem_spec()] * 4 + [hbm_spec()] + [vmem_spec()] * len(pieces),
+        [smem_spec()] + [vmem_spec()] * 4 + [vmem_spec()] * len(pieces),
         [vmem_spec()] * 4,
-        [pltpu.VMEM((3, CHUNK, 256), F32), dma_sems(1)],
+        [],
         10,
-    )(t, f, *rows, x, *pieces)
+    )(t, f, *rows, *pieces)
 
 
 def coriolis_rows(total, first, offsets):
@@ -408,31 +420,32 @@
     above = lax.ppermute(x[:, tile_rows - 16 :], "lat", ring(8, 1))
     below = lax.ppermute(x[:, :16], "lat", ring(8, -1))
     sent, blocks = rows_to_send(t, x, initial_backdrop)
+    sent = add_edges(t, x, above, below, sent)
+    s2, s1, s3, s0 = (to_next(v, j) for v, j in zip(sent, (2, 1, 3, 0)))
+    come = [s0, s3, s2, s1]
+
+    s0, variances, *blocks = lax.optimization_barrier((s0, spectral_inverse_variances, *blocks))
+    first_row = lat * tile_rows + lon * ROWS
+    offsets = jnp.arange(TILES + SPARE) - HALO
+    swapped = jnp.where(sub == SUB - 1, CHUNK, 0)
+    f1 = coriolis_rows(total, first_row + swapped, offsets)
+    f2 = coriolis_rows(total, first_row - swapped, offsets + CHUNK)
+    rows = weighting_rows(variances)
     extra = {}
     for j, block in zip((2, 1, 3, 0), blocks):
         pairs = [(s * LON + a, s * LON + (a + j) % LON) for s in (0, SUB - 1) for a in range(LON)]
         extra[j] = lax.ppermute(block, ("sub", "lon"), pairs) if j else block
     extra = [extra[j] for j in (0, 3, 2, 1)]
-    sent = add_edges(t, x, above, below, sent)
-    s2, s1, s3, s0 = (to_next(v, j) for v, j in zip(sent, (2, 1, 3, 0)))
-    come = [s0, s3, s2, s1]
-
-    s0, variances = lax.optimization_barrier((s0, spectral_inverse_variances))
-    first_row = lat * tile_rows + lon * ROWS
-    offsets = jnp.arange(TILES + SPARE) - HALO
-    f1 = coriolis_rows(total, first_row, offsets)
-    f2 = coriolis_rows(total, first_row, offsets + CHUNK)
-    rows = weighting_rows(variances)
-    s3, *tied = lax.optimization_barrier((s3, *rows, *extra))
-    rows, extra = tied[:3], tied[3:]
-    own = [lax.ppermute(v, "sub", ring(SUB, -1)) for v in (s3, s2, s1)]
-
-    m1 = model_call(False, f1, come)
-    o1 = weight_call(0, t, m1, rows, x, own, extra, come)
+    s3, *rows = lax.optimization_barrier((s3, *rows))
+    own = [sent[3]] + [lax.ppermute(v, "sub", ring(SUB, -1)) for v in (s3, s2, s1)]
+
+    m1 = model_call(0, t, f1, come)
+    o1 = weight_call(0, t, m1, rows, own, come)
     r1 = [to_lon(o1[j], j) if j else o1[j] for j in range(LON)]
-    f2, *o1 = lax.optimization_barrier((f2, *o1))
-    m2 = model_call(True, f2, come)
-    o2 = weight_call(1, t, m2, rows, x, own, extra, come)
+    f2, *tied = lax.optimization_barrier((f2, *o1, *extra))
+    o1, extra = tied[:LON], tied[LON:]
+    m2 = model_call(1, t, f2, come)
+    o2 = weight_call(1, t, m2, rows, own, extra)
     r2 = [to_lon(o2[j], j) if j else o2[j] for j in range(LON)]
     return place(t, r2, tile_rows, place(t, r1, tile_rows))[None]
 

time: 138 us -> 131 us (0.949)
  the two profiles are of different devices: /device:TPU:1 before, /device:TPU:24 now
where the time goes in v5:
time: 131 us; the launch traced here: 129 us
  waiting for transfers between devices  43.5 us (33%)
  starting transfers between devices  43.2 us (33%)
  Pallas kernels  34.9 us (27%)
  local copies, waits for them, and re-layouts  3.54 us (3%)
  matrix products  2.76 us (2%)
    ppermute x4, waiting for transfers between devices, to_next(): return lax.ppermute(value, ('sub', 'lon'), pairs)  35.8 us
    pallas_call x2, Pallas kernels, model_call(): call(functools.partial(model_kernel, chunk), array(3, CHUNK, NLON), [smem...  17.9 us
    ppermute x6, starting transfers between devices, to_lon(): return lax.ppermute(value, 'lon', ring(LON, j))  14.4 us
    ppermute x3, starting transfers between devices, shards(): extra[j] = lax.ppermute(block, ('sub', 'lon'), pairs) if j else block  11.7 us
    ppermute x4, starting transfers between devices, to_next(): return lax.ppermute(value, ('sub', 'lon'), pairs)  11.7 us
    ppermute x6, waiting for transfers between devices, to_lon(): return lax.ppermute(value, 'lon', ring(LON, j))  7.72 us
    pallas_call x2, Pallas kernels, weight_call(): call(functools.partial(weight_kernel, chunk), [array(3, CHUNK, 256)] * 4,...  5.5 us
    pallas_call x2, Pallas kernels, place(): call(functools.partial(place_kernel, 1 if extra else 0), [array(3, rows,...  5.1 us
  transfers between devices with their start and end apart: 18, of which 5 were waited for; matrix products, arithmetic and copies ran while one was open for 3% of the time, Pallas kernels for 23%

profile of v5, /device:TPU:24, one launch (start us, length us, event | category | flops | bytes accessed | tf_op | source)
XLA Modules:
  0.0 129.1 jit_solution(6133837096465351471)
XLA Ops:
  0.0 0.8 fusion.6
  0.8 0.8 collective-permute-start.1
  1.6 3.4 %collective-permute-start = (f32[3,16,256]{2,1,0:T(8,128)S(1)}, f32[3,16,256]{2,1,0:T(8,128)S(1)}, u32[]{:S(2)}, u32[]{:S(2)}) collective-permute-start(f32[3,16,256]{2,1,0:T(8,128)S(1)} %get-tuple-element.74), channel_id=1, source_target_pairs={{0,4},{4,8},{8,12},{12,16},{16,20},{20,24},{24,28},{28,0},{1,5},{5... | collective-permute-start | bytes 147464 | tf_op jit(solution)/shard_map/ppermute | solution.py:420
  5.6 4.0 %shard_map.46 = (f32[440,256]{1,0:T(8,128)}, f32[440,256]{1,0:T(8,128)}, f32[440,256]{1,0:T(8,128)}, f32[440,256]{1,0:T(8,128)}, f32[3,64,256]{2,1,0:T(8,128)}, ...) custom-call(s32[9]{0:T(128)} %compare_select_fusion.3.t_ref, f32[3,512,256]{2,1,0:T(8,128)} %bitcast.5, ...), custom_call_target="tpu_custom_call" | custom-call | bytes 1 | tf_op jit(solution)/shard_map/pallas_call | solution.py:224
  9.7 0.6 copy-done.8
  10.3 2.5 %shard_map.47 = (f32[440,256]{1,0:T(8,128)}, f32[440,256]{1,0:T(8,128)}, f32[440,256]{1,0:T(8,128)}, f32[440,256]{1,0:T(8,128)}) custom-call(s32[9]{0:T(128)} %compare_select_fusion.3.t_ref, f32[3,512,256]{2,1,0:T(8,128)} %bitcast.6, f32[3,16,256]{2,1,0:T(8,128)} %copy-done.9, ...), custom_call_target="tpu_custom_call", output_to_operand_aliasing={{0}: (4, {}), {1}: (5, {}), {2}: (6, {}), {3}: (7, {})} | custom-call | bytes 1 | tf_op jit(solution)/shard_map/pallas_call | solution.py:263
  12.8 8.1 %collective-permute-start.4 = (f32[440,256]{1,0:T(8,128)}, f32[440,256]{1,0:T(8,128)S(1)}, u32[]{:S(2)}, u32[]{:S(2)}) collective-permute-start(f32[440,256]{1,0:T(8,128)} %get-tuple-element.45), channel_id=1, source_target_pairs={{0,34},{1,35},{2,32},{3,33},{32,66},{33,67},{34,64},{35,65},{64,98... | collective-permute-start | bytes 1351688 | tf_op jit(solution)/shard_map/ppermute | solution.py:401
  20.9 3.6 %collective-permute-start.5 = (f32[440,256]{1,0:T(8,128)}, f32[440,256]{1,0:T(8,128)S(1)}, u32[]{:S(2)}, u32[]{:S(2)}) collective-permute-start(f32[440,256]{1,0:T(8,128)} %get-tuple-element.46), channel_id=1, source_target_pairs={{0,33},{1,34},{2,35},{3,32},{32,65},{33,66},{34,67},{35,64},{64,97... | collective-permute-start | bytes 1351688 | tf_op jit(solution)/shard_map/ppermute | solution.py:401
  24.5 2.8 %fusion.7 = f32[3,1024]{1,0:T(4,128)S(1)} fusion(f32[3,513]{1,0:T(4,128)S(1)} %copy-done, f32[513,1024]{1,0:T(8,128)} %constant.52.clone), kind=kOutput, calls=%fused_computation.16 | convolution fusion | flops 18911232 | bytes 2119692 | tf_op jit(solution)/shard_map/dot_general | solution.py:329
  27.3 14.1 %collective-permute-done.4.s2.refs_6_ = f32[440,256]{1,0:T(8,128)S(1)} collective-permute-done((f32[440,256]{1,0:T(8,128)}, f32[440,256]{1,0:T(8,128)S(1)}, u32[]{:S(2)}, u32[]{:S(2)}) %collective-permute-start.4) | collective-permute-done | bytes 450592 | tf_op jit(solution)/shard_map/ppermute | solution.py:401
  41.4 21.7 %collective-permute-done.3.s3.refs_5_ = f32[440,256]{1,0:T(8,128)S(1)} collective-permute-done((f32[440,256]{1,0:T(8,128)}, f32[440,256]{1,0:T(8,128)S(1)}, u32[]{:S(2)}, u32[]{:S(2)}) %collective-permute-start.3) | collective-permute-done | bytes 450592 | tf_op jit(solution)/shard_map/ppermute | solution.py:401
  63.3 1.0 collective-permute-start.6
  64.3 4.8 %collective-permute-start.9 = (f32[3,64,256]{2,1,0:T(8,128)}, f32[3,64,256]{2,1,0:T(8,128)}, u32[]{:S(2)}, u32[]{:S(2)}) collective-permute-start(f32[3,64,256]{2,1,0:T(8,128)} %get-tuple-element.61), channel_id=1, source_target_pairs={{0,3},{1,0},{2,1},{3,2},{224,227},{225,224},{226,225},{227,226},{4... | collective-permute-start | bytes 589832 | tf_op jit(solution)/shard_map/ppermute | solution.py:437
  69.2 4.9 %collective-permute-start.10 = (f32[3,64,256]{2,1,0:T(8,128)}, f32[3,64,256]{2,1,0:T(8,128)}, u32[]{:S(2)}, u32[]{:S(2)}) collective-permute-start(f32[3,64,256]{2,1,0:T(8,128)} %get-tuple-element.62), channel_id=1, source_target_pairs={{0,2},{1,3},{2,0},{3,1},{224,226},{225,227},{226,224},{227,225},{4... | collective-permute-start | bytes 589832 | tf_op jit(solution)/shard_map/ppermute | solution.py:437
  74.2 1.9 %collective-permute-start.11 = (f32[3,64,256]{2,1,0:T(8,128)}, f32[3,64,256]{2,1,0:T(8,128)}, u32[]{:S(2)}, u32[]{:S(2)}) collective-permute-start(f32[3,64,256]{2,1,0:T(8,128)} %get-tuple-element.63), channel_id=1, source_target_pairs={{0,1},{1,2},{2,3},{3,0},{224,225},{225,226},{226,227},{227,224},{4... | collective-permute-start | bytes 589832 | tf_op jit(solution)/shard_map/ppermute | solution.py:437
  76.1 8.8 %shard_map.48.f_ref = f32[3,64,1024]{2,1,0:T(8,128)S(1)} custom-call(s32[9]{0:T(128)S(1)} %copy-done.5, f32[114]{0:T(128)S(1)} %sine_multiply_fusion.f_ref, f32[440,256]{1,0:T(8,128)S(1)} %collective-permute-done.2.s0.refs_4_, f32[440,256]{1,0:T(8,128)S(1)} %collective-permute-done.3.s3.refs_5_, f32[440,256]{1,0:T(8,128)S(1)} %collective-permute-done.4.s2.refs_6_, ...), custom_call_target="tpu_custom_call" | custom-call | bytes 1 | tf_op jit(solution)/shard_map/pallas_call | solution.py:173
  85.0 2.9 %shard_map.49 = (f32[3,64,256]{2,1,0:T(8,128)S(1)}, f32[3,64,256]{2,1,0:T(8,128)}, f32[3,64,256]{2,1,0:T(8,128)S(1)}, f32[3,64,256]{2,1,0:T(8,128)S(1)}) custom-call(s32[9]{0:T(128)S(1)} %copy-done.5, f32[3,64,1024]{2,1,0:T(8,128)S(1)} %shard_map.48.f_ref, f32[3,256]{1,0:T(4,128)S(1)} %get-tuple-element.52.a_ref, f32[3,256]{1,0:T(4,128)S(1)} %get-tuple-element.53.b_ref, ...), custom_call_target="tpu_custom_call" | custom-call | bytes 1 | tf_op jit(solution)/shard_map/pallas_call | solution.py:376
  88.0 0.7 copy-done.3
  88.7 0.7 copy-done.6
  89.3 0.7 copy-done.7
  90.0 3.4 %collective-permute-start.15 = (f32[3,64,256]{2,1,0:T(8,128)}, f32[3,64,256]{2,1,0:T(8,128)}, u32[]{:S(2)}, u32[]{:S(2)}) collective-permute-start(f32[3,64,256]{2,1,0:T(8,128)} %get-tuple-element.57), channel_id=1, source_target_pairs={{0,1},{1,2},{2,3},{3,0},{4,5},{5,6},{6,7},{7,4},{8,9},{9,10},{10,1... | collective-permute-start | bytes 589832 | tf_op jit(solution)/shard_map/ppermute | solution.py:405
  93.5 3.1 %collective-permute-start.16 = (f32[3,64,256]{2,1,0:T(8,128)}, f32[3,64,256]{2,1,0:T(8,128)S(1)}, u32[]{:S(2)}, u32[]{:S(2)}) collective-permute-start(f32[3,64,256]{2,1,0:T(8,128)} %copy-done.7), channel_id=1, source_target_pairs={{0,2},{1,3},{2,0},{3,1},{4,6},{5,7},{6,4},{7,5},{8,10},{9,11},{10,... | collective-permute-start | bytes 589832 | tf_op jit(solution)/shard_map/ppermute | solution.py:405
  97.2 9.0 %shard_map.50.f_ref = f32[3,64,1024]{2,1,0:T(8,128)S(1)} custom-call(s32[9]{0:T(128)S(1)} %copy-done.5, f32[114]{0:T(128)S(1)} %sine_multiply_fusion.1.f_ref, f32[440,256]{1,0:T(8,128)S(1)} %collective-permute-done.2.s0.refs_4_, f32[440,256]{1,0:T(8,128)S(1)} %collective-permute-done.3.s3.refs_5_, f32[440,256]{1,0:T(8,128)S(1)} %collective-permute-done.4.s2.refs_6_, ...), custom_call_target="tpu_custom_call" | custom-call | bytes 1 | tf_op jit(solution)/shard_map/pallas_call | solution.py:173
  106.2 2.6 %shard_map.51 = (f32[3,64,256]{2,1,0:T(8,128)S(1)}, f32[3,64,256]{2,1,0:T(8,128)S(1)}, f32[3,64,256]{2,1,0:T(8,128)S(1)}, f32[3,64,256]{2,1,0:T(8,128)S(1)}) custom-call(s32[9]{0:T(128)S(1)} %copy-done.5, f32[3,64,1024]{2,1,0:T(8,128)S(1)} %shard_map.50.f_ref, f32[3,256]{1,0:T(4,128)S(1)} %get-tuple-element.52.a_ref, f32[3,256]{1,0:T(4,128)S(1)} %get-tuple-element.53.b_ref, ...), custom_call_target="tpu_custom_call" | custom-call | bytes 1 | tf_op jit(solution)/shard_map/pallas_call | solution.py:376
  108.8 2.5 %collective-permute-start.12 = (f32[3,64,256]{2,1,0:T(8,128)S(1)}, f32[3,64,256]{2,1,0:T(8,128)S(1)}, u32[]{:S(2)}, u32[]{:S(2)}) collective-permute-start(f32[3,64,256]{2,1,0:T(8,128)S(1)} %get-tuple-element.70), channel_id=1, source_target_pairs={{0,1},{1,2},{2,3},{3,0},{4,5},{5,6},{6,7},{7,4},{8,9},{9,10},{10,1... | collective-permute-start | bytes 589832 | tf_op jit(solution)/shard_map/ppermute | solution.py:405
  111.3 2.9 %collective-permute-start.13 = (f32[3,64,256]{2,1,0:T(8,128)S(1)}, f32[3,64,256]{2,1,0:T(8,128)S(1)}, u32[]{:S(2)}, u32[]{:S(2)}) collective-permute-start(f32[3,64,256]{2,1,0:T(8,128)S(1)} %get-tuple-element.71), channel_id=1, source_target_pairs={{0,2},{1,3},{2,0},{3,1},{4,6},{5,7},{6,4},{7,5},{8,10},{9,11},{10,... | collective-permute-start | bytes 589832 | tf_op jit(solution)/shard_map/ppermute | solution.py:405
  114.2 1.9 %collective-permute-start.14 = (f32[3,64,256]{2,1,0:T(8,128)S(1)}, f32[3,64,256]{2,1,0:T(8,128)S(1)}, u32[]{:S(2)}, u32[]{:S(2)}) collective-permute-start(f32[3,64,256]{2,1,0:T(8,128)S(1)} %get-tuple-element.72), channel_id=1, source_target_pairs={{0,3},{1,0},{2,1},{3,2},{4,7},{5,4},{6,5},{7,6},{8,11},{9,8},{10,9... | collective-permute-start | bytes 589832 | tf_op jit(solution)/shard_map/ppermute | solution.py:405
  116.1 1.7 %collective-permute-done.17.r3 = f32[3,64,256]{2,1,0:T(8,128)S(1)} collective-permute-done((f32[3,64,256]{2,1,0:T(8,128)}, f32[3,64,256]{2,1,0:T(8,128)S(1)}, u32[]{:S(2)}, u32[]{:S(2)}) %collective-permute-start.17) | collective-permute-done | bytes 196640 | tf_op jit(solution)/shard_map/ppermute | solution.py:405
  117.8 2.6 %shard_map.52.refs_0_ = f32[3,512,256]{2,1,0:T(8,128)} custom-call(s32[9]{0:T(128)S(1)} %copy-done.5, f32[3,64,256]{2,1,0:T(8,128)S(1)} %copy-done.4, f32[3,64,256]{2,1,0:T(8,128)} %collective-permute-done.15.r1, f32[3,64,256]{2,1,0:T(8,128)S(1)} %collective-permute-done.16.r2, f32[3,64,256]{2,1,0:T(8,128)S(1)} %collective-permute-done.17.r3), custom_call_target="tpu_custom_call" | custom-call | bytes 1 | tf_op jit(solution)/shard_map/pallas_call | solution.py:295
  120.4 1.5 %collective-permute-done.13.r2 = f32[3,64,256]{2,1,0:T(8,128)S(1)} collective-permute-done((f32[3,64,256]{2,1,0:T(8,128)S(1)}, f32[3,64,256]{2,1,0:T(8,128)S(1)}, u32[]{:S(2)}, u32[]{:S(2)}) %collective-permute-start.13) | collective-permute-done | bytes 196640 | tf_op jit(solution)/shard_map/ppermute | solution.py:405
  121.9 4.5 %collective-permute-done.14.r3 = f32[3,64,256]{2,1,0:T(8,128)S(1)} collective-permute-done((f32[3,64,256]{2,1,0:T(8,128)S(1)}, f32[3,64,256]{2,1,0:T(8,128)S(1)}, u32[]{:S(2)}, u32[]{:S(2)}) %collective-permute-start.14) | collective-permute-done | bytes 196640 | tf_op jit(solution)/shard_map/ppermute | solution.py:405
  126.4 2.5 %shard_map.53 = f32[3,512,256]{2,1,0:T(8,128)} custom-call(s32[9]{0:T(128)S(1)} %copy-done.5, f32[3,64,256]{2,1,0:T(8,128)S(1)} %get-tuple-element.69.o0, f32[3,64,256]{2,1,0:T(8,128)S(1)} %collective-permute-done.12.r1, f32[3,64,256]{2,1,0:T(8,128)S(1)} %collective-permute-done.13.r2, ...), custom_call_target="tpu_custom_call", output_to_operand_aliasing={{}: (5, {})} | custom-call | bytes 1 | tf_op jit(solution)/shard_map/pallas_call | solution.py:295
  (39 shorter events, 1.6 us)
Async XLA Ops:
  0.0 24.5 %copy-start = (f32[3,513]{1,0:T(4,128)S(1)}, f32[3,513]{1,0:T(4,128)}, u32[]{:S(2)}) copy-start(f32[3,513]{1,0:T(4,128)} %param.6) | copy-start | bytes 18472
  0.8 8.8 %collective-permute-start.1 = (f32[3,16,256]{2,1,0:T(8,128)S(1)}, f32[3,16,256]{2,1,0:T(8,128)S(1)}, u32[]{:S(2)}, u32[]{:S(2)}) collective-permute-start(f32[3,16,256]{2,1,0:T(8,128)S(1)} %get-tuple-element.73), channel_id=1, source_target_pairs={{0,28},{4,0},{8,4},{12,8},{16,12},{20,16},{24,20},{28,24},{1,29},{... | collective-permute-start | bytes 147464 | tf_op jit(solution)/shard_map/ppermute | solution.py:421
  1.6 8.0 %collective-permute-start = (f32[3,16,256]{2,1,0:T(8,128)S(1)}, f32[3,16,256]{2,1,0:T(8,128)S(1)}, u32[]{:S(2)}, u32[]{:S(2)}) collective-permute-start(f32[3,16,256]{2,1,0:T(8,128)S(1)} %get-tuple-element.74), channel_id=1, source_target_pairs={{0,4},{4,8},{8,12},{12,16},{16,20},{20,24},{24,28},{28,0},{1,5},{5... | collective-permute-start | bytes 147464 | tf_op jit(solution)/shard_map/ppermute | solution.py:420
  9.6 0.6 copy-start.8
  9.7 0.6 copy-start.9
  12.8 63.4 %copy-start.5 = (s32[9]{0:T(128)S(1)}, s32[9]{0:T(128)}, u32[]{:S(2)}) copy-start(s32[9]{0:T(128)} %compare_select_fusion.3.t_ref) | copy-start | bytes 112
  12.8 11.7 %collective-permute-start.2 = (f32[440,256]{1,0:T(8,128)}, f32[440,256]{1,0:T(8,128)S(1)}, u32[]{:S(2)}, u32[]{:S(2)}) collective-permute-start(f32[440,256]{1,0:T(8,128)} %get-tuple-element.43.refs_0_), channel_id=1, source_target_pairs={{0,32},{1,33},{2,34},{3,35},{32,64},{33,65},{34,66},{35,67},{64,96... | collective-permute-start | bytes 1351688 | tf_op jit(solution)/shard_map/ppermute | solution.py:401
  12.8 28.6 %collective-permute-start.4 = (f32[440,256]{1,0:T(8,128)}, f32[440,256]{1,0:T(8,128)S(1)}, u32[]{:S(2)}, u32[]{:S(2)}) collective-permute-start(f32[440,256]{1,0:T(8,128)} %get-tuple-element.45), channel_id=1, source_target_pairs={{0,34},{1,35},{2,32},{3,33},{32,66},{33,67},{34,64},{35,65},{64,98... | collective-permute-start | bytes 1351688 | tf_op jit(solution)/shard_map/ppermute | solution.py:401
  20.9 42.2 %collective-permute-start.3 = (f32[440,256]{1,0:T(8,128)}, f32[440,256]{1,0:T(8,128)S(1)}, u32[]{:S(2)}, u32[]{:S(2)}) collective-permute-start(f32[440,256]{1,0:T(8,128)} %get-tuple-element.44), channel_id=1, source_target_pairs={{0,35},{1,32},{2,33},{3,34},{32,67},{33,64},{34,65},{35,66},{64,99... | collective-permute-start | bytes 1351688 | tf_op jit(solution)/shard_map/ppermute | solution.py:401
  20.9 42.2 %collective-permute-start.5 = (f32[440,256]{1,0:T(8,128)}, f32[440,256]{1,0:T(8,128)S(1)}, u32[]{:S(2)}, u32[]{:S(2)}) collective-permute-start(f32[440,256]{1,0:T(8,128)} %get-tuple-element.46), channel_id=1, source_target_pairs={{0,33},{1,34},{2,35},{3,32},{32,65},{33,66},{34,67},{35,64},{64,97... | collective-permute-start | bytes 1351688 | tf_op jit(solution)/shard_map/ppermute | solution.py:401
  27.3 57.7 %copy-start.1 = (f32[440,256]{1,0:T(8,128)S(1)}, f32[440,256]{1,0:T(8,128)}, u32[]{:S(2)}) copy-start(f32[440,256]{1,0:T(8,128)} %get-tuple-element.43.refs_0_) | copy-start | bytes 1351684
  41.4 32.7 %collective-permute-start.7 = (f32[440,256]{1,0:T(8,128)S(1)}, f32[440,256]{1,0:T(8,128)S(1)}, u32[]{:S(2)}, u32[]{:S(2)}) collective-permute-start(f32[440,256]{1,0:T(8,128)S(1)} %collective-permute-done.4.s2.refs_6_), channel_id=1, source_target_pairs={{0,224},{32,0},{64,32},{96,64},{128,96},{160,128},{192,160},{224,1... | collective-permute-start | bytes 1351688 | tf_op jit(solution)/shard_map/ppermute | solution.py:440
  63.1 21.9 %collective-permute-start.8 = (f32[440,256]{1,0:T(8,128)S(1)}, f32[440,256]{1,0:T(8,128)S(1)}, u32[]{:S(2)}, u32[]{:S(2)}) collective-permute-start(f32[440,256]{1,0:T(8,128)S(1)} %collective-permute-done.5.s1.refs_7_), channel_id=1, source_target_pairs={{0,224},{32,0},{64,32},{96,64},{128,96},{160,128},{192,160},{224,1... | collective-permute-start | bytes 1351688 | tf_op jit(solution)/shard_map/ppermute | solution.py:440
  63.3 21.7 %collective-permute-start.6 = (f32[440,256]{1,0:T(8,128)S(1)}, f32[440,256]{1,0:T(8,128)}, u32[]{:S(2)}, u32[]{:S(2)}) collective-permute-start(f32[440,256]{1,0:T(8,128)S(1)} %collective-permute-done.3.s3.refs_5_), channel_id=1, source_target_pairs={{0,224},{32,0},{64,32},{96,64},{128,96},{160,128},{192,160},{224,1... | collective-permute-start | bytes 1351688 | tf_op jit(solution)/shard_map/ppermute | solution.py:440
  64.3 32.3 %collective-permute-start.9 = (f32[3,64,256]{2,1,0:T(8,128)}, f32[3,64,256]{2,1,0:T(8,128)}, u32[]{:S(2)}, u32[]{:S(2)}) collective-permute-start(f32[3,64,256]{2,1,0:T(8,128)} %get-tuple-element.61), channel_id=1, source_target_pairs={{0,3},{1,0},{2,1},{3,2},{224,227},{225,224},{226,225},{227,226},{4... | collective-permute-start | bytes 589832 | tf_op jit(solution)/shard_map/ppermute | solution.py:437
  69.2 28.0 %collective-permute-start.10 = (f32[3,64,256]{2,1,0:T(8,128)}, f32[3,64,256]{2,1,0:T(8,128)}, u32[]{:S(2)}, u32[]{:S(2)}) collective-permute-start(f32[3,64,256]{2,1,0:T(8,128)} %get-tuple-element.62), channel_id=1, source_target_pairs={{0,2},{1,3},{2,0},{3,1},{224,226},{225,227},{226,224},{227,225},{4... | collective-permute-start | bytes 589832 | tf_op jit(solution)/shard_map/ppermute | solution.py:437
  74.2 23.0 %collective-permute-start.11 = (f32[3,64,256]{2,1,0:T(8,128)}, f32[3,64,256]{2,1,0:T(8,128)}, u32[]{:S(2)}, u32[]{:S(2)}) collective-permute-start(f32[3,64,256]{2,1,0:T(8,128)} %get-tuple-element.63), channel_id=1, source_target_pairs={{0,1},{1,2},{2,3},{3,0},{224,225},{225,226},{226,227},{227,224},{4... | collective-permute-start | bytes 589832 | tf_op jit(solution)/shard_map/ppermute | solution.py:437
  88.0 0.7 copy-start.3
  88.7 0.7 copy-start.6
  89.3 0.7 copy-start.7
  90.0 16.2 %copy-start.2 = (f32[3,64,256]{2,1,0:T(8,128)S(1)}, f32[3,64,256]{2,1,0:T(8,128)}, u32[]{:S(2)}) copy-start(f32[3,64,256]{2,1,0:T(8,128)} %get-tuple-element.65.refs_4_) | copy-start | bytes 589828
  90.0 24.1 %collective-permute-start.15 = (f32[3,64,256]{2,1,0:T(8,128)}, f32[3,64,256]{2,1,0:T(8,128)}, u32[]{:S(2)}, u32[]{:S(2)}) collective-permute-start(f32[3,64,256]{2,1,0:T(8,128)} %get-tuple-element.57), channel_id=1, source_target_pairs={{0,1},{1,2},{2,3},{3,0},{4,5},{5,6},{6,7},{7,4},{8,9},{9,10},{10,1... | collective-permute-start | bytes 589832 | tf_op jit(solution)/shard_map/ppermute | solution.py:405
  93.5 22.6 %collective-permute-start.16 = (f32[3,64,256]{2,1,0:T(8,128)}, f32[3,64,256]{2,1,0:T(8,128)S(1)}, u32[]{:S(2)}, u32[]{:S(2)}) collective-permute-start(f32[3,64,256]{2,1,0:T(8,128)} %copy-done.7), channel_id=1, source_target_pairs={{0,2},{1,3},{2,0},{3,1},{4,6},{5,7},{6,4},{7,5},{8,10},{9,11},{10,... | collective-permute-start | bytes 589832 | tf_op jit(solution)/shard_map/ppermute | solution.py:405
  96.6 21.1 %collective-permute-start.17 = (f32[3,64,256]{2,1,0:T(8,128)}, f32[3,64,256]{2,1,0:T(8,128)S(1)}, u32[]{:S(2)}, u32[]{:S(2)}) collective-permute-start(f32[3,64,256]{2,1,0:T(8,128)} %copy-done.6), channel_id=1, source_target_pairs={{0,3},{1,0},{2,1},{3,2},{4,7},{5,4},{6,5},{7,6},{8,11},{9,8},{10,9... | collective-permute-start | bytes 589832 | tf_op jit(solution)/shard_map/ppermute | solution.py:405
  106.2 11.5 %copy-start.4 = (f32[3,64,256]{2,1,0:T(8,128)S(1)}, f32[3,64,256]{2,1,0:T(8,128)}, u32[]{:S(2)}) copy-start(f32[3,64,256]{2,1,0:T(8,128)} %copy-done.3) | copy-start | bytes 589828
  108.8 11.6 %collective-permute-start.12 = (f32[3,64,256]{2,1,0:T(8,128)S(1)}, f32[3,64,256]{2,1,0:T(8,128)S(1)}, u32[]{:S(2)}, u32[]{:S(2)}) collective-permute-start(f32[3,64,256]{2,1,0:T(8,128)S(1)} %get-tuple-element.70), channel_id=1, source_target_pairs={{0,1},{1,2},{2,3},{3,0},{4,5},{5,6},{6,7},{7,4},{8,9},{9,10},{10,1... | collective-permute-start | bytes 589832 | tf_op jit(solution)/shard_map/ppermute | solution.py:405
  111.3 10.6 %collective-permute-start.13 = (f32[3,64,256]{2,1,0:T(8,128)S(1)}, f32[3,64,256]{2,1,0:T(8,128)S(1)}, u32[]{:S(2)}, u32[]{:S(2)}) collective-permute-start(f32[3,64,256]{2,1,0:T(8,128)S(1)} %get-tuple-element.71), channel_id=1, source_target_pairs={{0,2},{1,3},{2,0},{3,1},{4,6},{5,7},{6,4},{7,5},{8,10},{9,11},{10,... | collective-permute-start | bytes 589832 | tf_op jit(solution)/shard_map/ppermute | solution.py:405
  114.2 12.2 %collective-permute-start.14 = (f32[3,64,256]{2,1,0:T(8,128)S(1)}, f32[3,64,256]{2,1,0:T(8,128)S(1)}, u32[]{:S(2)}, u32[]{:S(2)}) collective-permute-start(f32[3,64,256]{2,1,0:T(8,128)S(1)} %get-tuple-element.72), channel_id=1, source_target_pairs={{0,3},{1,0},{2,1},{3,2},{4,7},{5,4},{6,5},{7,6},{8,11},{9,8},{10,9... | collective-permute-start | bytes 589832 | tf_op jit(solution)/shard_map/ppermute | solution.py:405

commit v6 on v5

--- a/solution.py
+++ b/solution.py
@@ -20,8 +20,8 @@
 CHUNK = ROWS // 2
 SENT = 440
 TILES = CHUNK + 2 * HALO
-GROUP = 16
-SPARE = 2 * GROUP
+GROUP = 40
+SPARE = 16
 F32 = jnp.float32
 BF16 = jnp.bfloat16
 
@@ -180,56 +180,82 @@
     )(t, f, *pieces)
 
 
-def rows_kernel(t_ref, x, back, s2, s1, s3, s0, e2, e1, e3, e0, sem, sem_extra):
-    order = ((2, s2, e2), (1, s1, e1), (3, s3, e3), (0, s0, e0))
-    at = [aligned(t_ref[j] * ROWS) for j, _, _ in order]
-    pairs = []
-    for row, (_, s, _) in zip(at, order):
-        for c in range(3):
-            pairs.append((x.at[c, pl.ds(row, ROWS), :], s.at[pl.ds(ROWS * c, ROWS), :]))
-    copies = start_all(sem, pairs)
+def extra_kernel(t_ref, x, back, e2, e1, e3, e0, buf, sem, sem_out):
+    order = ((2, e2), (1, e1), (3, e3), (0, e0))
+    at = [aligned(t_ref[j] * ROWS) for j, _ in order]
+
+    def move(src, first):
+        pairs = [
+            (src.at[:, pl.ds(aligned(row + first), CHUNK), :], buf.at[n])
+            for n, row in enumerate(at)
+        ]
+        for copy in start_all(sem, pairs):
+            copy.wait()
+        for copy in start_all(sem_out, [(buf.at[n], e) for n, (_, e) in enumerate(order)]):
+            copy.wait()
 
     @pl.when(t_ref[2 * LON] == 0)
     def _():
-        pairs = [
-            (back.at[:, pl.ds(aligned(row + CHUNK), CHUNK), :], e)
-            for row, (_, _, e) in zip(at, order)
-        ]
-        for copy in start_all(sem_extra, pairs):
-            copy.wait()
+        move(back, CHUNK)
 
     @pl.when(t_ref[2 * LON] == SUB - 1)
     def _():
-        pairs = [(x.at[:, pl.ds(row, CHUNK), :], e) for row, (_, _, e) in zip(at, order)]
-        for copy in start_all(sem_extra, pairs):
-            copy.wait()
-
-    for copy in copies:
-        copy.wait()
-
-    @pl.when(t_ref[2 * LON] == SUB - 1)
-    def _():
-        pairs = []
-        for row, (_, s, _) in zip(at, order):
-            for c in range(3):
-                pairs.append((back.at[c, pl.ds(row, CHUNK), :], s.at[pl.ds(ROWS * c, CHUNK), :]))
-        for copy in start_all(sem, pairs):
-            copy.wait()
-
-    for _, s, _ in order:
-        s[3 * ROWS :, :] = jnp.zeros((SENT - 3 * ROWS, 256), F32)
-
-
-def rows_to_send(t, x, back):
-    out = call(
-        rows_kernel,
-        [array(SENT, 256)] * 4 + [array(3, CHUNK, 256)] * 4,
+        move(x, 0)
+
+
+def extra_rows(t, x, back):
+    return call(
+        extra_kernel,
+        [array(3, CHUNK, 256)] * 4,
         [smem_spec(), hbm_spec(), hbm_spec()],
-        [vmem_spec()] * 8,
-        [dma_sems(12), dma_sems(4)],
+        [hbm_spec()] * 4,
+        [pltpu.VMEM((4, 3, CHUNK, 256), F32), dma_sems(4), dma_sems(4)],
         60,
     )(t, x, back)
-    return out[:4], out[4:]
+
+
+def rows_kernel(t_ref, x, back, s2, s1, s3, s0, buf, sem, sem_out):
+    order = ((2, s2), (1, s1), (3, s3), (0, s0))
+    at = [aligned(t_ref[j] * ROWS) for j, _ in order]
+    last = t_ref[2 * LON] == SUB - 1
+
+    def move(parts):
+        pairs = []
+        for n, row in enumerate(at):
+            for src, first, count in parts:
+                for c in range(3):
+                    dst = buf.at[n, pl.ds(ROWS * c + first, count), :]
+                    pairs.append((src.at[c, pl.ds(aligned(row + first), count), :], dst))
+        copies = start_all(sem, pairs)
+        each = 3 * len(parts)
+        outs = []
+        for n, (_, s) in enumerate(order):
+            for copy in copies[each * n : each * n + each]:
+                copy.wait()
+            buf[n, 3 * ROWS :, :] = jnp.zeros((SENT - 3 * ROWS, 256), F32)
+            outs.append(pltpu.make_async_copy(buf.at[n], s, sem_out.at[n]))
+            outs[-1].start()
+        for copy in outs:
+            copy.wait()
+
+    @pl.when(last)
+    def _():
+        move(((back, 0, CHUNK), (x, CHUNK, CHUNK)))
+
+    @pl.when(jnp.logical_not(last))
+    def _():
+        move(((x, 0, ROWS),))
+
+
+def rows_to_send(t, x, back):
+    return call(
+        rows_kernel,
+        [array(SENT, 256)] * 4,
+        [smem_spec(), hbm_spec(), hbm_spec()],
+        [hbm_spec()] * 4,
+        [pltpu.VMEM((4, SENT, 256), F32), dma_sems(24), dma_sems(4)],
+        60,
+    )(t, x, back)
 
 
 def edges_kernel(t_ref, x, above, below, *refs):
@@ -276,9 +302,8 @@
     )(t, x, above, below, *sent)
 
 
-def place_kernel(chunk, t_ref, o0, r1, r2, r3, *refs):
-    out, buf, sem, sem_out = refs[-4:]
-    first = CHUNK * half_of(chunk, t_ref)
+def place_first_kernel(t_ref, o0, r1, r2, r3, out, buf, sem, sem_out):
+    first = CHUNK * half_of(0, t_ref)
     copies = start_all(sem, [(r, buf.at[j]) for j, r in enumerate((o0, r1, r2, r3))])
     outs = []
     for j, copy in enumerate(copies):
@@ -290,17 +315,37 @@
         copy.wait()
 
 
-def place(t, pieces, rows, begun=None):
-    extra = [] if begun is None else [begun]
-    return call(
-        functools.partial(place_kernel, 1 if extra else 0),
+def place_first(t, pieces, rows):
+    return call(
+        place_first_kernel,
         [array(3, rows, 256)],
-        [smem_spec()] + [hbm_spec()] * (4 + len(extra)),
+        [smem_spec()] + [hbm_spec()] * 4,
         [hbm_spec()],
         [pltpu.VMEM((4, 3, CHUNK, 256), F32), dma_sems(4), dma_sems(4)],
-        3,
-        input_output_aliases={5: 0} if extra else {},
-    )(t, *pieces, *extra)[0]
+        4,
+    )(t, *pieces)[0]
+
+
+def place_second_kernel(t_ref, o0, r1, r2, r3, begun, out, sem):
+    first = CHUNK * half_of(1, t_ref)
+    pairs = [
+        (r, out.at[:, pl.ds(aligned(t_ref[LON + j] * ROWS + first), CHUNK), :])
+        for j, r in enumerate((o0, r1, r2, r3))
+    ]
+    for copy in start_all(sem, pairs):
+        copy.wait()
+
+
+def place_second(t, pieces, begun):
+    return call(
+        place_second_kernel,
+        [array(*begun.shape)],
+        [smem_spec()] + [vmem_spec()] * 4 + [hbm_spec()],
+        [hbm_spec()],
+        [dma_sems(4)],
+        4,
+        input_output_aliases={5: 0},
+    )(t, *pieces, begun)[0]
 
 
 def cosine_table():
@@ -419,24 +464,26 @@
 
     above = lax.ppermute(x[:, tile_rows - 16 :], "lat", ring(8, 1))
     below = lax.ppermute(x[:, :16], "lat", ring(8, -1))
-    sent, blocks = rows_to_send(t, x, initial_backdrop)
+    sent = rows_to_send(t, x, initial_backdrop)
     sent = add_edges(t, x, above, below, sent)
     s2, s1, s3, s0 = (to_next(v, j) for v, j in zip(sent, (2, 1, 3, 0)))
     come = [s0, s3, s2, s1]
 
-    s0, variances, *blocks = lax.optimization_barrier((s0, spectral_inverse_variances, *blocks))
+    s0, variances, later = lax.optimization_barrier((s0, spectral_inverse_variances, t))
+    blocks = extra_rows(later, x, initial_backdrop)
     first_row = lat * tile_rows + lon * ROWS
     offsets = jnp.arange(TILES + SPARE) - HALO
     swapped = jnp.where(sub == SUB - 1, CHUNK, 0)
     f1 = coriolis_rows(total, first_row + swapped, offsets)
     f2 = coriolis_rows(total, first_row - swapped, offsets + CHUNK)
     rows = weighting_rows(variances)
+    s3, *tied = lax.optimization_barrier((s3, *rows, *blocks))
+    rows, blocks = tied[:3], tied[3:]
     extra = {}
     for j, block in zip((2, 1, 3, 0), blocks):
         pairs = [(s * LON + a, s * LON + (a + j) % LON) for s in (0, SUB - 1) for a in range(LON)]
         extra[j] = lax.ppermute(block, ("sub", "lon"), pairs) if j else block
     extra = [extra[j] for j in (0, 3, 2, 1)]
-    s3, *rows = lax.optimization_barrier((s3, *rows))
     own = [sent[3]] + [lax.ppermute(v, "sub", ring(SUB, -1)) for v in (s3, s2, s1)]
 
     m1 = model_call(0, t, f1, come)
@@ -447,7 +494,7 @@
     m2 = model_call(1, t, f2, come)
     o2 = weight_call(1, t, m2, rows, own, extra)
     r2 = [to_lon(o2[j], j) if j else o2[j] for j in range(LON)]
-    return place(t, r2, tile_rows, place(t, r1, tile_rows))[None]
+    return place_second(t, r2, place_first(t, r1, tile_rows))[None]
 
 
 def solution(mesh):

time: 131 us -> 126 us (0.962)
  Pallas kernels: 34.9 us -> 32.2 us
  waiting for transfers between devices: 43.5 us -> 41.9 us
    pallas_call x2, Pallas kernels: 17.9 us -> 14 us  [model_call(): call(functools.partial(model_kernel, chunk), array(3, CHUNK, NLON), [smem...]
    ppermute x4, waiting for transfers between devices: 35.8 us -> 32.6 us  [to_next(): return lax.ppermute(value, ('sub', 'lon'), pairs)]
    ppermute x6, waiting for transfers between devices: 7.72 us -> 9.31 us  [to_lon(): return lax.ppermute(value, 'lon', ring(LON, j))]
    pallas_call x3 -> x4, Pallas kernels: 9.09 us -> 10.1 us  [the longest x1 3.2 us: rows_to_send(): call(rows_kernel, [array(SENT, 256)] * 4, [smem_spec(), hbm_spec(), hbm_s...]
  transfers between devices with their start and end apart: 18 -> 18, of which waited for: 5 -> 6; matrix products, arithmetic and copies ran while one was open for 3% -> 3% of each run, Pallas kernels for 23% -> 23%
where the time goes in v6:
time: 126 us; the launch traced here: 124 us
  starting transfers between devices  42.8 us (34%)
  waiting for transfers between devices  41.9 us (33%)
  Pallas kernels  32.2 us (26%)
  local copies, waits for them, and re-layouts  3.51 us (3%)
  matrix products  2.76 us (2%)
    ppermute x4, waiting for transfers between devices, to_next(): return lax.ppermute(value, ('sub', 'lon'), pairs)  32.6 us
    ppermute x6, starting transfers between devices, to_lon(): return lax.ppermute(value, 'lon', ring(LON, j))  14.4 us
    pallas_call x2, Pallas kernels, model_call(): call(functools.partial(model_kernel, chunk), array(3, CHUNK, NLON), [smem...  14 us
    ppermute x4, starting transfers between devices, to_next(): return lax.ppermute(value, ('sub', 'lon'), pairs)  12 us
    ppermute x3, starting transfers between devices, shards(): extra[j] = lax.ppermute(block, ('sub', 'lon'), pairs) if j else block  10.7 us
    ppermute x6, waiting for transfers between devices, to_lon(): return lax.ppermute(value, 'lon', ring(LON, j))  9.31 us
    pallas_call x2, Pallas kernels, weight_call(): call(functools.partial(weight_kernel, chunk), [array(3, CHUNK, 256)] * 4,...  5.49 us
    ppermute x1, starting transfers between devices, shards(): above = lax.ppermute(x[:, tile_rows - 16:], 'lat', ring(8, 1))  3.39 us
  transfers between devices with their start and end apart: 18, of which 6 were waited for; matrix products, arithmetic and copies ran while one was open for 3% of the time, Pallas kernels for 23%

profile of v6, /device:TPU:24, one launch (start us, length us, event | category | flops | bytes accessed | tf_op | source)
XLA Modules:
  0.0 124.2 jit_solution(8894103764301939769)
XLA Ops:
  0.0 0.8 fusion.6
  0.8 0.8 collective-permute-start.1
  1.6 3.4 %collective-permute-start = (f32[3,16,256]{2,1,0:T(8,128)S(1)}, f32[3,16,256]{2,1,0:T(8,128)S(1)}, u32[]{:S(2)}, u32[]{:S(2)}) collective-permute-start(f32[3,16,256]{2,1,0:T(8,128)S(1)} %get-tuple-element.76), channel_id=1, source_target_pairs={{0,4},{4,8},{8,12},{12,16},{16,20},{20,24},{24,28},{28,0},{1,5},{5... | collective-permute-start | bytes 147464 | tf_op jit(solution)/shard_map/ppermute | solution.py:465
  5.6 3.2 %shard_map.46 = (f32[440,256]{1,0:T(8,128)}, f32[440,256]{1,0:T(8,128)}, f32[440,256]{1,0:T(8,128)}, f32[440,256]{1,0:T(8,128)}) custom-call(s32[9]{0:T(128)} %compare_select_fusion.3.t_ref, f32[3,512,256]{2,1,0:T(8,128)} %bitcast.5, f32[3,512,256]{2,1,0:T(8,128)} %back.3), custom_call_target="tpu_custom_call" | custom-call | bytes 1 | tf_op jit(solution)/shard_map/pallas_call | solution.py:251
  9.4 2.5 %shard_map.47 = (f32[440,256]{1,0:T(8,128)}, f32[440,256]{1,0:T(8,128)}, f32[440,256]{1,0:T(8,128)}, f32[440,256]{1,0:T(8,128)}) custom-call(s32[9]{0:T(128)} %compare_select_fusion.3.t_ref, f32[3,512,256]{2,1,0:T(8,128)} %bitcast.6, f32[3,16,256]{2,1,0:T(8,128)} %copy-done.9, ...), custom_call_target="tpu_custom_call", output_to_operand_aliasing={{0}: (4, {}), {1}: (5, {}), {2}: (6, {}), {3}: (7, {})} | custom-call | bytes 1 | tf_op jit(solution)/shard_map/pallas_call | solution.py:289
  12.0 8.4 %collective-permute-start.4 = (f32[440,256]{1,0:T(8,128)}, f32[440,256]{1,0:T(8,128)S(1)}, u32[]{:S(2)}, u32[]{:S(2)}) collective-permute-start(f32[440,256]{1,0:T(8,128)} %get-tuple-element.46), channel_id=1, source_target_pairs={{0,34},{1,35},{2,32},{3,33},{32,66},{33,67},{34,64},{35,65},{64,98... | collective-permute-start | bytes 1351688 | tf_op jit(solution)/shard_map/ppermute | solution.py:446
  20.4 3.6 %collective-permute-start.5 = (f32[440,256]{1,0:T(8,128)}, f32[440,256]{1,0:T(8,128)S(1)}, u32[]{:S(2)}, u32[]{:S(2)}) collective-permute-start(f32[440,256]{1,0:T(8,128)} %get-tuple-element.47), channel_id=1, source_target_pairs={{0,33},{1,34},{2,35},{3,32},{32,65},{33,66},{34,67},{35,64},{64,97... | collective-permute-start | bytes 1351688 | tf_op jit(solution)/shard_map/ppermute | solution.py:446
  23.9 2.8 %fusion.7 = f32[3,1024]{1,0:T(4,128)S(1)} fusion(f32[3,513]{1,0:T(4,128)S(1)} %copy-done, f32[513,1024]{1,0:T(8,128)} %constant.52.clone), kind=kOutput, calls=%fused_computation.16 | convolution fusion | flops 18911232 | bytes 2119692 | tf_op jit(solution)/shard_map/dot_general | solution.py:374
  26.7 14.4 %collective-permute-done.4.s2.refs_6_ = f32[440,256]{1,0:T(8,128)S(1)} collective-permute-done((f32[440,256]{1,0:T(8,128)}, f32[440,256]{1,0:T(8,128)S(1)}, u32[]{:S(2)}, u32[]{:S(2)}) %collective-permute-start.4) | collective-permute-done | bytes 450592 | tf_op jit(solution)/shard_map/ppermute | solution.py:446
  41.1 2.9 %shard_map.49 = (f32[3,64,256]{2,1,0:T(8,128)}, f32[3,64,256]{2,1,0:T(8,128)}, f32[3,64,256]{2,1,0:T(8,128)}, f32[3,64,256]{2,1,0:T(8,128)}) custom-call(s32[9]{0:T(128)} %compare_select_fusion.3.t_ref, f32[3,512,256]{2,1,0:T(8,128)} %bitcast.7, f32[3,512,256]{2,1,0:T(8,128)} %back.3), custom_call_target="tpu_custom_call" | custom-call | bytes 1 | tf_op jit(solution)/shard_map/pallas_call | solution.py:207
  44.1 18.2 %collective-permute-done.3.s3.refs_5_ = f32[440,256]{1,0:T(8,128)S(1)} collective-permute-done((f32[440,256]{1,0:T(8,128)}, f32[440,256]{1,0:T(8,128)S(1)}, u32[]{:S(2)}, u32[]{:S(2)}) %collective-permute-start.3) | collective-permute-done | bytes 450592 | tf_op jit(solution)/shard_map/ppermute | solution.py:446
  62.5 1.4 %collective-permute-start.6 = (f32[440,256]{1,0:T(8,128)S(1)}, f32[440,256]{1,0:T(8,128)}, u32[]{:S(2)}, u32[]{:S(2)}) collective-permute-start(f32[440,256]{1,0:T(8,128)S(1)} %collective-permute-done.3.s3.refs_5_), channel_id=1, source_target_pairs={{0,224},{32,0},{64,32},{96,64},{128,96},{160,128},{192,160},{224,1... | collective-permute-start | bytes 1351688 | tf_op jit(solution)/shard_map/ppermute | solution.py:487
  63.9 4.5 %collective-permute-start.9 = (f32[3,64,256]{2,1,0:T(8,128)}, f32[3,64,256]{2,1,0:T(8,128)}, u32[]{:S(2)}, u32[]{:S(2)}) collective-permute-start(f32[3,64,256]{2,1,0:T(8,128)} %get-tuple-element.63), channel_id=1, source_target_pairs={{0,3},{1,0},{2,1},{3,2},{224,227},{225,224},{226,225},{227,226},{4... | collective-permute-start | bytes 589832 | tf_op jit(solution)/shard_map/ppermute | solution.py:485
  68.3 3.7 %collective-permute-start.10 = (f32[3,64,256]{2,1,0:T(8,128)}, f32[3,64,256]{2,1,0:T(8,128)}, u32[]{:S(2)}, u32[]{:S(2)}) collective-permute-start(f32[3,64,256]{2,1,0:T(8,128)} %get-tuple-element.64), channel_id=1, source_target_pairs={{0,2},{1,3},{2,0},{3,1},{224,226},{225,227},{226,224},{227,225},{4... | collective-permute-start | bytes 589832 | tf_op jit(solution)/shard_map/ppermute | solution.py:485
  72.1 2.5 %collective-permute-start.11 = (f32[3,64,256]{2,1,0:T(8,128)}, f32[3,64,256]{2,1,0:T(8,128)}, u32[]{:S(2)}, u32[]{:S(2)}) collective-permute-start(f32[3,64,256]{2,1,0:T(8,128)} %get-tuple-element.65), channel_id=1, source_target_pairs={{0,1},{1,2},{2,3},{3,0},{224,225},{225,226},{226,227},{227,224},{4... | collective-permute-start | bytes 589832 | tf_op jit(solution)/shard_map/ppermute | solution.py:485
  74.6 7.0 %shard_map.48.f_ref = f32[3,64,1024]{2,1,0:T(8,128)S(1)} custom-call(s32[9]{0:T(128)S(1)} %copy-done.5, f32[98]{0:T(128)S(1)} %sine_multiply_fusion.f_ref, f32[440,256]{1,0:T(8,128)S(1)} %collective-permute-done.2.s0.refs_4_, f32[440,256]{1,0:T(8,128)S(1)} %collective-permute-done.3.s3.refs_5_, f32[440,256]{1,0:T(8,128)S(1)} %collective-permute-done.4.s2.refs_6_, ...), custom_call_target="tpu_custom_call" | custom-call | bytes 1 | tf_op jit(solution)/shard_map/pallas_call | solution.py:173
  81.7 2.9 %shard_map.50 = (f32[3,64,256]{2,1,0:T(8,128)S(1)}, f32[3,64,256]{2,1,0:T(8,128)}, f32[3,64,256]{2,1,0:T(8,128)S(1)}, f32[3,64,256]{2,1,0:T(8,128)S(1)}) custom-call(s32[9]{0:T(128)S(1)} %copy-done.5, f32[3,64,1024]{2,1,0:T(8,128)S(1)} %shard_map.48.f_ref, f32[3,256]{1,0:T(4,128)S(1)} %get-tuple-element.54.a_ref, f32[3,256]{1,0:T(4,128)S(1)} %get-tuple-element.55.b_ref, ...), custom_call_target="tpu_custom_call" | custom-call | bytes 1 | tf_op jit(solution)/shard_map/pallas_call | solution.py:421
  86.0 0.7 copy-done.7
  86.6 4.1 %collective-permute-start.15 = (f32[3,64,256]{2,1,0:T(8,128)}, f32[3,64,256]{2,1,0:T(8,128)}, u32[]{:S(2)}, u32[]{:S(2)}) collective-permute-start(f32[3,64,256]{2,1,0:T(8,128)} %get-tuple-element.59), channel_id=1, source_target_pairs={{0,1},{1,2},{2,3},{3,0},{4,5},{5,6},{6,7},{7,4},{8,9},{9,10},{10,1... | collective-permute-start | bytes 589832 | tf_op jit(solution)/shard_map/ppermute | solution.py:450
  90.8 1.9 %collective-permute-start.16 = (f32[3,64,256]{2,1,0:T(8,128)}, f32[3,64,256]{2,1,0:T(8,128)S(1)}, u32[]{:S(2)}, u32[]{:S(2)}) collective-permute-start(f32[3,64,256]{2,1,0:T(8,128)} %copy-done.7), channel_id=1, source_target_pairs={{0,2},{1,3},{2,0},{3,1},{4,6},{5,7},{6,4},{7,5},{8,10},{9,11},{10,... | collective-permute-start | bytes 589832 | tf_op jit(solution)/shard_map/ppermute | solution.py:450
  92.7 2.1 %collective-permute-start.17 = (f32[3,64,256]{2,1,0:T(8,128)}, f32[3,64,256]{2,1,0:T(8,128)S(1)}, u32[]{:S(2)}, u32[]{:S(2)}) collective-permute-start(f32[3,64,256]{2,1,0:T(8,128)} %copy-done.6), channel_id=1, source_target_pairs={{0,3},{1,0},{2,1},{3,2},{4,7},{5,4},{6,5},{7,6},{8,11},{9,8},{10,9... | collective-permute-start | bytes 589832 | tf_op jit(solution)/shard_map/ppermute | solution.py:450
  94.8 7.0 %shard_map.51.f_ref = f32[3,64,1024]{2,1,0:T(8,128)S(1)} custom-call(s32[9]{0:T(128)S(1)} %copy-done.5, f32[98]{0:T(128)S(1)} %sine_multiply_fusion.1.f_ref, f32[440,256]{1,0:T(8,128)S(1)} %collective-permute-done.2.s0.refs_4_, f32[440,256]{1,0:T(8,128)S(1)} %collective-permute-done.3.s3.refs_5_, f32[440,256]{1,0:T(8,128)S(1)} %collective-permute-done.4.s2.refs_6_, ...), custom_call_target="tpu_custom_call" | custom-call | bytes 1 | tf_op jit(solution)/shard_map/pallas_call | solution.py:173
  101.9 2.5 %shard_map.52 = (f32[3,64,256]{2,1,0:T(8,128)S(1)}, f32[3,64,256]{2,1,0:T(8,128)S(1)}, f32[3,64,256]{2,1,0:T(8,128)S(1)}, f32[3,64,256]{2,1,0:T(8,128)S(1)}) custom-call(s32[9]{0:T(128)S(1)} %copy-done.5, f32[3,64,1024]{2,1,0:T(8,128)S(1)} %shard_map.51.f_ref, f32[3,256]{1,0:T(4,128)S(1)} %get-tuple-element.54.a_ref, f32[3,256]{1,0:T(4,128)S(1)} %get-tuple-element.55.b_ref, ...), custom_call_target="tpu_custom_call" | custom-call | bytes 1 | tf_op jit(solution)/shard_map/pallas_call | solution.py:421
  104.5 0.9 collective-permute-start.12
  105.3 4.1 %collective-permute-start.13 = (f32[3,64,256]{2,1,0:T(8,128)S(1)}, f32[3,64,256]{2,1,0:T(8,128)S(1)}, u32[]{:S(2)}, u32[]{:S(2)}) collective-permute-start(f32[3,64,256]{2,1,0:T(8,128)S(1)} %get-tuple-element.73), channel_id=1, source_target_pairs={{0,2},{1,3},{2,0},{3,1},{4,6},{5,7},{6,4},{7,5},{8,10},{9,11},{10,... | collective-permute-start | bytes 589832 | tf_op jit(solution)/shard_map/ppermute | solution.py:450
  109.5 1.2 collective-permute-start.14
  110.7 0.9 collective-permute-done.16.r2
  111.6 2.7 %collective-permute-done.17.r3 = f32[3,64,256]{2,1,0:T(8,128)S(1)} collective-permute-done((f32[3,64,256]{2,1,0:T(8,128)}, f32[3,64,256]{2,1,0:T(8,128)S(1)}, u32[]{:S(2)}, u32[]{:S(2)}) %collective-permute-start.17) | collective-permute-done | bytes 196640 | tf_op jit(solution)/shard_map/ppermute | solution.py:450
  114.2 2.6 %shard_map.53.begun = f32[3,512,256]{2,1,0:T(8,128)} custom-call(s32[9]{0:T(128)S(1)} %copy-done.5, f32[3,64,256]{2,1,0:T(8,128)S(1)} %copy-done.4, f32[3,64,256]{2,1,0:T(8,128)} %collective-permute-done.15.r1, f32[3,64,256]{2,1,0:T(8,128)S(1)} %collective-permute-done.16.r2, f32[3,64,256]{2,1,0:T(8,128)S(1)} %collective-permute-done.17.r3), custom_call_target="tpu_custom_call" | custom-call | bytes 1 | tf_op jit(solution)/shard_map/pallas_call | solution.py:319
  116.9 2.1 %collective-permute-done.13.r2 = f32[3,64,256]{2,1,0:T(8,128)S(1)} collective-permute-done((f32[3,64,256]{2,1,0:T(8,128)S(1)}, f32[3,64,256]{2,1,0:T(8,128)S(1)}, u32[]{:S(2)}, u32[]{:S(2)}) %collective-permute-start.13) | collective-permute-done | bytes 196640 | tf_op jit(solution)/shard_map/ppermute | solution.py:450
  119.0 3.7 %collective-permute-done.14.r3 = f32[3,64,256]{2,1,0:T(8,128)S(1)} collective-permute-done((f32[3,64,256]{2,1,0:T(8,128)S(1)}, f32[3,64,256]{2,1,0:T(8,128)S(1)}, u32[]{:S(2)}, u32[]{:S(2)}) %collective-permute-start.14) | collective-permute-done | bytes 196640 | tf_op jit(solution)/shard_map/ppermute | solution.py:450
  122.6 1.5 %shard_map.54 = f32[3,512,256]{2,1,0:T(8,128)} custom-call(s32[9]{0:T(128)S(1)} %copy-done.5, f32[3,64,256]{2,1,0:T(8,128)S(1)} %get-tuple-element.71.o0, f32[3,64,256]{2,1,0:T(8,128)S(1)} %collective-permute-done.12.r1, f32[3,64,256]{2,1,0:T(8,128)S(1)} %collective-permute-done.13.r2, ...), custom_call_target="tpu_custom_call", output_to_operand_aliasing={{}: (5, {})} | custom-call | bytes 1 | tf_op jit(solution)/shard_map/pallas_call | solution.py:340
  (40 shorter events, 2.9 us)
Async XLA Ops:
  0.0 23.9 %copy-start = (f32[3,513]{1,0:T(4,128)S(1)}, f32[3,513]{1,0:T(4,128)}, u32[]{:S(2)}) copy-start(f32[3,513]{1,0:T(4,128)} %param.6) | copy-start | bytes 18472
  0.8 8.0 %collective-permute-start.1 = (f32[3,16,256]{2,1,0:T(8,128)S(1)}, f32[3,16,256]{2,1,0:T(8,128)S(1)}, u32[]{:S(2)}, u32[]{:S(2)}) collective-permute-start(f32[3,16,256]{2,1,0:T(8,128)S(1)} %get-tuple-element.75), channel_id=1, source_target_pairs={{0,28},{4,0},{8,4},{12,8},{16,12},{20,16},{24,20},{28,24},{1,29},{... | collective-permute-start | bytes 147464 | tf_op jit(solution)/shard_map/ppermute | solution.py:466
  1.6 7.2 %collective-permute-start = (f32[3,16,256]{2,1,0:T(8,128)S(1)}, f32[3,16,256]{2,1,0:T(8,128)S(1)}, u32[]{:S(2)}, u32[]{:S(2)}) collective-permute-start(f32[3,16,256]{2,1,0:T(8,128)S(1)} %get-tuple-element.76), channel_id=1, source_target_pairs={{0,4},{4,8},{8,12},{12,16},{16,20},{20,24},{24,28},{28,0},{1,5},{5... | collective-permute-start | bytes 147464 | tf_op jit(solution)/shard_map/ppermute | solution.py:465
  8.8 0.6 copy-start.8
  8.8 0.6 copy-start.9
  12.0 12.0 %collective-permute-start.2 = (f32[440,256]{1,0:T(8,128)}, f32[440,256]{1,0:T(8,128)S(1)}, u32[]{:S(2)}, u32[]{:S(2)}) collective-permute-start(f32[440,256]{1,0:T(8,128)} %get-tuple-element.44.refs_0_), channel_id=1, source_target_pairs={{0,32},{1,33},{2,34},{3,35},{32,64},{33,65},{34,66},{35,67},{64,96... | collective-permute-start | bytes 1351688 | tf_op jit(solution)/shard_map/ppermute | solution.py:446
  12.0 29.1 %collective-permute-start.4 = (f32[440,256]{1,0:T(8,128)}, f32[440,256]{1,0:T(8,128)S(1)}, u32[]{:S(2)}, u32[]{:S(2)}) collective-permute-start(f32[440,256]{1,0:T(8,128)} %get-tuple-element.46), channel_id=1, source_target_pairs={{0,34},{1,35},{2,32},{3,33},{32,66},{33,67},{34,64},{35,65},{64,98... | collective-permute-start | bytes 1351688 | tf_op jit(solution)/shard_map/ppermute | solution.py:446
  20.4 41.9 %collective-permute-start.3 = (f32[440,256]{1,0:T(8,128)}, f32[440,256]{1,0:T(8,128)S(1)}, u32[]{:S(2)}, u32[]{:S(2)}) collective-permute-start(f32[440,256]{1,0:T(8,128)} %get-tuple-element.45), channel_id=1, source_target_pairs={{0,35},{1,32},{2,33},{3,34},{32,67},{33,64},{34,65},{35,66},{64,99... | collective-permute-start | bytes 1351688 | tf_op jit(solution)/shard_map/ppermute | solution.py:446
  20.4 41.9 %collective-permute-start.5 = (f32[440,256]{1,0:T(8,128)}, f32[440,256]{1,0:T(8,128)S(1)}, u32[]{:S(2)}, u32[]{:S(2)}) collective-permute-start(f32[440,256]{1,0:T(8,128)} %get-tuple-element.47), channel_id=1, source_target_pairs={{0,33},{1,34},{2,35},{3,32},{32,65},{33,66},{34,67},{35,64},{64,97... | collective-permute-start | bytes 1351688 | tf_op jit(solution)/shard_map/ppermute | solution.py:446
  41.1 31.0 %collective-permute-start.7 = (f32[440,256]{1,0:T(8,128)S(1)}, f32[440,256]{1,0:T(8,128)S(1)}, u32[]{:S(2)}, u32[]{:S(2)}) collective-permute-start(f32[440,256]{1,0:T(8,128)S(1)} %collective-permute-done.4.s2.refs_6_), channel_id=1, source_target_pairs={{0,224},{32,0},{64,32},{96,64},{128,96},{160,128},{192,160},{224,1... | collective-permute-start | bytes 1351688 | tf_op jit(solution)/shard_map/ppermute | solution.py:487
  41.1 33.5 %copy-start.5 = (s32[9]{0:T(128)S(1)}, s32[9]{0:T(128)}, u32[]{:S(2)}) copy-start(s32[9]{0:T(128)} %compare_select_fusion.3.t_ref) | copy-start | bytes 112
  44.0 37.6 %copy-start.1 = (f32[440,256]{1,0:T(8,128)S(1)}, f32[440,256]{1,0:T(8,128)}, u32[]{:S(2)}) copy-start(f32[440,256]{1,0:T(8,128)} %get-tuple-element.44.refs_0_) | copy-start | bytes 1351684
  62.3 19.4 %collective-permute-start.8 = (f32[440,256]{1,0:T(8,128)S(1)}, f32[440,256]{1,0:T(8,128)S(1)}, u32[]{:S(2)}, u32[]{:S(2)}) collective-permute-start(f32[440,256]{1,0:T(8,128)S(1)} %collective-permute-done.5.s1.refs_7_), channel_id=1, source_target_pairs={{0,224},{32,0},{64,32},{96,64},{128,96},{160,128},{192,160},{224,1... | collective-permute-start | bytes 1351688 | tf_op jit(solution)/shard_map/ppermute | solution.py:487
  62.5 19.2 %collective-permute-start.6 = (f32[440,256]{1,0:T(8,128)S(1)}, f32[440,256]{1,0:T(8,128)}, u32[]{:S(2)}, u32[]{:S(2)}) collective-permute-start(f32[440,256]{1,0:T(8,128)S(1)} %collective-permute-done.3.s3.refs_5_), channel_id=1, source_target_pairs={{0,224},{32,0},{64,32},{96,64},{128,96},{160,128},{192,160},{224,1... | collective-permute-start | bytes 1351688 | tf_op jit(solution)/shard_map/ppermute | solution.py:487
  63.9 28.9 %collective-permute-start.9 = (f32[3,64,256]{2,1,0:T(8,128)}, f32[3,64,256]{2,1,0:T(8,128)}, u32[]{:S(2)}, u32[]{:S(2)}) collective-permute-start(f32[3,64,256]{2,1,0:T(8,128)} %get-tuple-element.63), channel_id=1, source_target_pairs={{0,3},{1,0},{2,1},{3,2},{224,227},{225,224},{226,225},{227,226},{4... | collective-permute-start | bytes 589832 | tf_op jit(solution)/shard_map/ppermute | solution.py:485
  68.3 26.5 %collective-permute-start.10 = (f32[3,64,256]{2,1,0:T(8,128)}, f32[3,64,256]{2,1,0:T(8,128)}, u32[]{:S(2)}, u32[]{:S(2)}) collective-permute-start(f32[3,64,256]{2,1,0:T(8,128)} %get-tuple-element.64), channel_id=1, source_target_pairs={{0,2},{1,3},{2,0},{3,1},{224,226},{225,227},{226,224},{227,225},{4... | collective-permute-start | bytes 589832 | tf_op jit(solution)/shard_map/ppermute | solution.py:485
  72.1 22.8 %collective-permute-start.11 = (f32[3,64,256]{2,1,0:T(8,128)}, f32[3,64,256]{2,1,0:T(8,128)}, u32[]{:S(2)}, u32[]{:S(2)}) collective-permute-start(f32[3,64,256]{2,1,0:T(8,128)} %get-tuple-element.65), channel_id=1, source_target_pairs={{0,1},{1,2},{2,3},{3,0},{224,225},{225,226},{226,227},{227,224},{4... | collective-permute-start | bytes 589832 | tf_op jit(solution)/shard_map/ppermute | solution.py:485
  84.6 0.7 copy-start.3
  85.3 0.7 copy-start.6
  86.0 0.7 copy-start.7
  86.6 15.2 %copy-start.2 = (f32[3,64,256]{2,1,0:T(8,128)S(1)}, f32[3,64,256]{2,1,0:T(8,128)}, u32[]{:S(2)}) copy-start(f32[3,64,256]{2,1,0:T(8,128)} %get-tuple-element.67.refs_4_) | copy-start | bytes 589828
  86.6 22.8 %collective-permute-start.15 = (f32[3,64,256]{2,1,0:T(8,128)}, f32[3,64,256]{2,1,0:T(8,128)}, u32[]{:S(2)}, u32[]{:S(2)}) collective-permute-start(f32[3,64,256]{2,1,0:T(8,128)} %get-tuple-element.59), channel_id=1, source_target_pairs={{0,1},{1,2},{2,3},{3,0},{4,5},{5,6},{6,7},{7,4},{8,9},{9,10},{10,1... | collective-permute-start | bytes 589832 | tf_op jit(solution)/shard_map/ppermute | solution.py:450
  90.8 20.8 %collective-permute-start.16 = (f32[3,64,256]{2,1,0:T(8,128)}, f32[3,64,256]{2,1,0:T(8,128)S(1)}, u32[]{:S(2)}, u32[]{:S(2)}) collective-permute-start(f32[3,64,256]{2,1,0:T(8,128)} %copy-done.7), channel_id=1, source_target_pairs={{0,2},{1,3},{2,0},{3,1},{4,6},{5,7},{6,4},{7,5},{8,10},{9,11},{10,... | collective-permute-start | bytes 589832 | tf_op jit(solution)/shard_map/ppermute | solution.py:450
  92.7 21.5 %collective-permute-start.17 = (f32[3,64,256]{2,1,0:T(8,128)}, f32[3,64,256]{2,1,0:T(8,128)S(1)}, u32[]{:S(2)}, u32[]{:S(2)}) collective-permute-start(f32[3,64,256]{2,1,0:T(8,128)} %copy-done.6), channel_id=1, source_target_pairs={{0,3},{1,0},{2,1},{3,2},{4,7},{5,4},{6,5},{7,6},{8,11},{9,8},{10,9... | collective-permute-start | bytes 589832 | tf_op jit(solution)/shard_map/ppermute | solution.py:450
  101.9 12.4 %copy-start.4 = (f32[3,64,256]{2,1,0:T(8,128)S(1)}, f32[3,64,256]{2,1,0:T(8,128)}, u32[]{:S(2)}) copy-start(f32[3,64,256]{2,1,0:T(8,128)} %copy-done.3) | copy-start | bytes 589828
  104.5 12.4 %collective-permute-start.12 = (f32[3,64,256]{2,1,0:T(8,128)S(1)}, f32[3,64,256]{2,1,0:T(8,128)S(1)}, u32[]{:S(2)}, u32[]{:S(2)}) collective-permute-start(f32[3,64,256]{2,1,0:T(8,128)S(1)} %get-tuple-element.72), channel_id=1, source_target_pairs={{0,1},{1,2},{2,3},{3,0},{4,5},{5,6},{6,7},{7,4},{8,9},{9,10},{10,1... | collective-permute-start | bytes 589832 | tf_op jit(solution)/shard_map/ppermute | solution.py:450
  105.3 13.6 %collective-permute-start.13 = (f32[3,64,256]{2,1,0:T(8,128)S(1)}, f32[3,64,256]{2,1,0:T(8,128)S(1)}, u32[]{:S(2)}, u32[]{:S(2)}) collective-permute-start(f32[3,64,256]{2,1,0:T(8,128)S(1)} %get-tuple-element.73), channel_id=1, source_target_pairs={{0,2},{1,3},{2,0},{3,1},{4,6},{5,7},{6,4},{7,5},{8,10},{9,11},{10,... | collective-permute-start | bytes 589832 | tf_op jit(solution)/shard_map/ppermute | solution.py:450
  109.5 13.2 %collective-permute-start.14 = (f32[3,64,256]{2,1,0:T(8,128)S(1)}, f32[3,64,256]{2,1,0:T(8,128)S(1)}, u32[]{:S(2)}, u32[]{:S(2)}) collective-permute-start(f32[3,64,256]{2,1,0:T(8,128)S(1)} %get-tuple-element.74), channel_id=1, source_target_pairs={{0,3},{1,0},{2,1},{3,2},{4,7},{5,4},{6,5},{7,6},{8,11},{9,8},{10,9... | collective-permute-start | bytes 589832 | tf_op jit(solution)/shard_map/ppermute | solution.py:450

commit v7 on v6

--- a/solution.py
+++ b/solution.py
@@ -129,7 +129,7 @@
     return 1 - swapped if chunk else swapped
 
 
-def model_kernel(chunk, t_ref, f_ref, s0, s3, s2, s1, out, *bufs):
+def model_kernel(chunk, t_ref, f_ref, s2, s1, s3, s0, out, *bufs):
     x, b, c, y = bufs
     half = half_of(chunk, t_ref)
 
@@ -302,7 +302,7 @@
     )(t, x, above, below, *sent)
 
 
-def place_first_kernel(t_ref, o0, r1, r2, r3, out, buf, sem, sem_out):
+def place_first_kernel(t_ref, r2, r1, r3, o0, out, buf, sem, sem_out):
     first = CHUNK * half_of(0, t_ref)
     copies = start_all(sem, [(r, buf.at[j]) for j, r in enumerate((o0, r1, r2, r3))])
     outs = []
@@ -326,7 +326,7 @@
     )(t, *pieces)[0]
 
 
-def place_second_kernel(t_ref, o0, r1, r2, r3, begun, out, sem):
+def place_second_kernel(t_ref, r2, r1, r3, o0, begun, out, sem):
     first = CHUNK * half_of(1, t_ref)
     pairs = [
         (r, out.at[:, pl.ds(aligned(t_ref[LON + j] * ROWS + first), CHUNK), :])
@@ -486,14 +486,14 @@
     extra = [extra[j] for j in (0, 3, 2, 1)]
     own = [sent[3]] + [lax.ppermute(v, "sub", ring(SUB, -1)) for v in (s3, s2, s1)]
 
-    m1 = model_call(0, t, f1, come)
+    m1 = model_call(0, t, f1, [come[n] for n in (2, 3, 1, 0)])
     o1 = weight_call(0, t, m1, rows, own, come)
-    r1 = [to_lon(o1[j], j) if j else o1[j] for j in range(LON)]
+    r1 = [to_lon(o1[j], j) if j else o1[j] for j in (2, 1, 3, 0)]
     f2, *tied = lax.optimization_barrier((f2, *o1, *extra))
     o1, extra = tied[:LON], tied[LON:]
-    m2 = model_call(1, t, f2, come)
+    m2 = model_call(1, t, f2, [come[n] for n in (2, 3, 1, 0)])
     o2 = weight_call(1, t, m2, rows, own, extra)
-    r2 = [to_lon(o2[j], j) if j else o2[j] for j in range(LON)]
+    r2 = [to_lon(o2[j], j) if j else o2[j] for j in (2, 1, 3, 0)]
     return place_second(t, r2, place_first(t, r1, tile_rows))[None]
 
 

time: 126 us -> 126 us (level)
  waiting for transfers between devices: 41.9 us -> 39 us
  starting transfers between devices: 42.8 us -> 45.1 us
    ppermute x6, waiting for transfers between devices: 9.31 us -> 7.71 us  [to_lon(): return lax.ppermute(value, 'lon', ring(LON, j))]
    ppermute x4, waiting for transfers between devices: 32.6 us -> 31.3 us  [to_next(): return lax.ppermute(value, ('sub', 'lon'), pairs)]
where the time goes in v7:
time: 126 us; the launch traced here: 124 us
  starting transfers between devices  45.1 us (36%)
  waiting for transfers between devices  39 us (31%)
  Pallas kernels  32.2 us (26%)
  local copies, waits for them, and re-layouts  3.51 us (3%)
  matrix products  2.76 us (2%)
    ppermute x4, waiting for transfers between devices, to_next(): return lax.ppermute(value, ('sub', 'lon'), pairs)  31.3 us
    ppermute x6, starting transfers between devices, to_lon(): return lax.ppermute(value, 'lon', ring(LON, j))  14.4 us
    pallas_call x2, Pallas kernels, model_call(): call(functools.partial(model_kernel, chunk), array(3, CHUNK, NLON), [smem...  14 us
    ppermute x4, starting transfers between devices, to_next(): return lax.ppermute(value, ('sub', 'lon'), pairs)  13.2 us
    ppermute x3, starting transfers between devices, shards(): extra[j] = lax.ppermute(block, ('sub', 'lon'), pairs) if j else block  11.7 us
    ppermute x6, waiting for transfers between devices, to_lon(): return lax.ppermute(value, 'lon', ring(LON, j))  7.71 us
    pallas_call x2, Pallas kernels, weight_call(): call(functools.partial(weight_kernel, chunk), [array(3, CHUNK, 256)] * 4,...  5.48 us
    ppermute x1, starting transfers between devices, shards(): above = lax.ppermute(x[:, tile_rows - 16:], 'lat', ring(8, 1))  3.39 us
  transfers between devices with their start and end apart: 18, of which 6 were waited for; matrix products, arithmetic and copies ran while one was open for 3% of the time, Pallas kernels for 23%

profile of v7, /device:TPU:24, one launch (start us, length us, event | category | flops | bytes accessed | tf_op | source)
XLA Modules:
  0.0 123.5 jit_solution(15427851318089697059)
XLA Ops:
  0.0 0.8 fusion.6
  0.8 0.8 collective-permute-start.1
  1.6 3.4 %collective-permute-start = (f32[3,16,256]{2,1,0:T(8,128)S(1)}, f32[3,16,256]{2,1,0:T(8,128)S(1)}, u32[]{:S(2)}, u32[]{:S(2)}) collective-permute-start(f32[3,16,256]{2,1,0:T(8,128)S(1)} %get-tuple-element.76), channel_id=1, source_target_pairs={{0,4},{4,8},{8,12},{12,16},{16,20},{20,24},{24,28},{28,0},{1,5},{5... | collective-permute-start | bytes 147464 | tf_op jit(solution)/shard_map/ppermute | solution.py:465
  5.6 3.2 %shard_map.46 = (f32[440,256]{1,0:T(8,128)}, f32[440,256]{1,0:T(8,128)}, f32[440,256]{1,0:T(8,128)}, f32[440,256]{1,0:T(8,128)}) custom-call(s32[9]{0:T(128)} %compare_select_fusion.3.t_ref, f32[3,512,256]{2,1,0:T(8,128)} %bitcast.5, f32[3,512,256]{2,1,0:T(8,128)} %back.3), custom_call_target="tpu_custom_call" | custom-call | bytes 1 | tf_op jit(solution)/shard_map/pallas_call | solution.py:251
  9.4 2.5 %shard_map.47 = (f32[440,256]{1,0:T(8,128)}, f32[440,256]{1,0:T(8,128)}, f32[440,256]{1,0:T(8,128)}, f32[440,256]{1,0:T(8,128)}) custom-call(s32[9]{0:T(128)} %compare_select_fusion.3.t_ref, f32[3,512,256]{2,1,0:T(8,128)} %bitcast.6, f32[3,16,256]{2,1,0:T(8,128)} %copy-done.9, ...), custom_call_target="tpu_custom_call", output_to_operand_aliasing={{0}: (4, {}), {1}: (5, {}), {2}: (6, {}), {3}: (7, {})} | custom-call | bytes 1 | tf_op jit(solution)/shard_map/pallas_call | solution.py:289
  12.0 8.4 %collective-permute-start.2 = (f32[440,256]{1,0:T(8,128)}, f32[440,256]{1,0:T(8,128)S(1)}, u32[]{:S(2)}, u32[]{:S(2)}) collective-permute-start(f32[440,256]{1,0:T(8,128)} %get-tuple-element.44), channel_id=1, source_target_pairs={{0,34},{1,35},{2,32},{3,33},{32,66},{33,67},{34,64},{35,65},{64,98... | collective-permute-start | bytes 1351688 | tf_op jit(solution)/shard_map/ppermute | solution.py:446
  20.4 1.0 collective-permute-start.3
  21.4 3.8 %collective-permute-start.4 = (f32[440,256]{1,0:T(8,128)}, f32[440,256]{1,0:T(8,128)S(1)}, u32[]{:S(2)}, u32[]{:S(2)}) collective-permute-start(f32[440,256]{1,0:T(8,128)} %get-tuple-element.46), channel_id=1, source_target_pairs={{0,35},{1,32},{2,33},{3,34},{32,67},{33,64},{34,65},{35,66},{64,99... | collective-permute-start | bytes 1351688 | tf_op jit(solution)/shard_map/ppermute | solution.py:446
  25.2 2.8 %fusion.7 = f32[3,1024]{1,0:T(4,128)S(1)} fusion(f32[3,513]{1,0:T(4,128)S(1)} %copy-done, f32[513,1024]{1,0:T(8,128)} %constant.52.clone), kind=kOutput, calls=%fused_computation.16 | convolution fusion | flops 18911232 | bytes 2119692 | tf_op jit(solution)/shard_map/dot_general | solution.py:374
  27.9 14.5 %collective-permute-done.2.s2.refs_6_ = f32[440,256]{1,0:T(8,128)S(1)} collective-permute-done((f32[440,256]{1,0:T(8,128)}, f32[440,256]{1,0:T(8,128)S(1)}, u32[]{:S(2)}, u32[]{:S(2)}) %collective-permute-start.2) | collective-permute-done | bytes 450592 | tf_op jit(solution)/shard_map/ppermute | solution.py:446
  42.5 2.9 %shard_map.49 = (f32[3,64,256]{2,1,0:T(8,128)}, f32[3,64,256]{2,1,0:T(8,128)}, f32[3,64,256]{2,1,0:T(8,128)}, f32[3,64,256]{2,1,0:T(8,128)}) custom-call(s32[9]{0:T(128)} %compare_select_fusion.3.t_ref, f32[3,512,256]{2,1,0:T(8,128)} %bitcast.7, f32[3,512,256]{2,1,0:T(8,128)} %back.3), custom_call_target="tpu_custom_call" | custom-call | bytes 1 | tf_op jit(solution)/shard_map/pallas_call | solution.py:207
  45.4 16.7 %collective-permute-done.4.s3.refs_5_ = f32[440,256]{1,0:T(8,128)S(1)} collective-permute-done((f32[440,256]{1,0:T(8,128)}, f32[440,256]{1,0:T(8,128)S(1)}, u32[]{:S(2)}, u32[]{:S(2)}) %collective-permute-start.4) | collective-permute-done | bytes 450592 | tf_op jit(solution)/shard_map/ppermute | solution.py:446
  62.5 1.3 %collective-permute-start.6 = (f32[440,256]{1,0:T(8,128)S(1)}, f32[440,256]{1,0:T(8,128)}, u32[]{:S(2)}, u32[]{:S(2)}) collective-permute-start(f32[440,256]{1,0:T(8,128)S(1)} %collective-permute-done.4.s3.refs_5_), channel_id=1, source_target_pairs={{0,224},{32,0},{64,32},{96,64},{128,96},{160,128},{192,160},{224,1... | collective-permute-start | bytes 1351688 | tf_op jit(solution)/shard_map/ppermute | solution.py:487
  63.8 5.5 %collective-permute-start.9 = (f32[3,64,256]{2,1,0:T(8,128)}, f32[3,64,256]{2,1,0:T(8,128)}, u32[]{:S(2)}, u32[]{:S(2)}) collective-permute-start(f32[3,64,256]{2,1,0:T(8,128)} %get-tuple-element.63), channel_id=1, source_target_pairs={{0,3},{1,0},{2,1},{3,2},{224,227},{225,224},{226,225},{227,226},{4... | collective-permute-start | bytes 589832 | tf_op jit(solution)/shard_map/ppermute | solution.py:485
  69.3 2.4 %collective-permute-start.10 = (f32[3,64,256]{2,1,0:T(8,128)}, f32[3,64,256]{2,1,0:T(8,128)}, u32[]{:S(2)}, u32[]{:S(2)}) collective-permute-start(f32[3,64,256]{2,1,0:T(8,128)} %get-tuple-element.64), channel_id=1, source_target_pairs={{0,2},{1,3},{2,0},{3,1},{224,226},{225,227},{226,224},{227,225},{4... | collective-permute-start | bytes 589832 | tf_op jit(solution)/shard_map/ppermute | solution.py:485
  71.7 3.8 %collective-permute-start.11 = (f32[3,64,256]{2,1,0:T(8,128)}, f32[3,64,256]{2,1,0:T(8,128)}, u32[]{:S(2)}, u32[]{:S(2)}) collective-permute-start(f32[3,64,256]{2,1,0:T(8,128)} %get-tuple-element.65), channel_id=1, source_target_pairs={{0,1},{1,2},{2,3},{3,0},{224,225},{225,226},{226,227},{227,224},{4... | collective-permute-start | bytes 589832 | tf_op jit(solution)/shard_map/ppermute | solution.py:485
  75.5 7.0 %shard_map.48.f_ref = f32[3,64,1024]{2,1,0:T(8,128)S(1)} custom-call(s32[9]{0:T(128)S(1)} %copy-done.5, f32[98]{0:T(128)S(1)} %sine_multiply_fusion.f_ref, f32[440,256]{1,0:T(8,128)S(1)} %collective-permute-done.2.s2.refs_6_, f32[440,256]{1,0:T(8,128)S(1)} %collective-permute-done.3.s1.refs_7_, f32[440,256]{1,0:T(8,128)S(1)} %collective-permute-done.4.s3.refs_5_, ...), custom_call_target="tpu_custom_call" | custom-call | bytes 1 | tf_op jit(solution)/shard_map/pallas_call | solution.py:173
  82.6 2.9 %shard_map.50 = (f32[3,64,256]{2,1,0:T(8,128)S(1)}, f32[3,64,256]{2,1,0:T(8,128)}, f32[3,64,256]{2,1,0:T(8,128)S(1)}, f32[3,64,256]{2,1,0:T(8,128)S(1)}) custom-call(s32[9]{0:T(128)S(1)} %copy-done.5, f32[3,64,1024]{2,1,0:T(8,128)S(1)} %shard_map.48.f_ref, f32[3,256]{1,0:T(4,128)S(1)} %get-tuple-element.54.a_ref, f32[3,256]{1,0:T(4,128)S(1)} %get-tuple-element.55.b_ref, ...), custom_call_target="tpu_custom_call" | custom-call | bytes 1 | tf_op jit(solution)/shard_map/pallas_call | solution.py:421
  86.9 0.7 copy-done.7
  87.6 4.1 %collective-permute-start.16 = (f32[3,64,256]{2,1,0:T(8,128)}, f32[3,64,256]{2,1,0:T(8,128)}, u32[]{:S(2)}, u32[]{:S(2)}) collective-permute-start(f32[3,64,256]{2,1,0:T(8,128)} %get-tuple-element.59), channel_id=1, source_target_pairs={{0,1},{1,2},{2,3},{3,0},{4,5},{5,6},{6,7},{7,4},{8,9},{9,10},{10,1... | collective-permute-start | bytes 589832 | tf_op jit(solution)/shard_map/ppermute | solution.py:450
  92.4 3.1 %collective-permute-start.17 = (f32[3,64,256]{2,1,0:T(8,128)}, f32[3,64,256]{2,1,0:T(8,128)S(1)}, u32[]{:S(2)}, u32[]{:S(2)}) collective-permute-start(f32[3,64,256]{2,1,0:T(8,128)} %copy-done.6), channel_id=1, source_target_pairs={{0,3},{1,0},{2,1},{3,2},{4,7},{5,4},{6,5},{7,6},{8,11},{9,8},{10,9... | collective-permute-start | bytes 589832 | tf_op jit(solution)/shard_map/ppermute | solution.py:450
  95.4 7.0 %shard_map.51.f_ref = f32[3,64,1024]{2,1,0:T(8,128)S(1)} custom-call(s32[9]{0:T(128)S(1)} %copy-done.5, f32[98]{0:T(128)S(1)} %sine_multiply_fusion.1.f_ref, f32[440,256]{1,0:T(8,128)S(1)} %collective-permute-done.2.s2.refs_6_, f32[440,256]{1,0:T(8,128)S(1)} %collective-permute-done.3.s1.refs_7_, f32[440,256]{1,0:T(8,128)S(1)} %collective-permute-done.4.s3.refs_5_, ...), custom_call_target="tpu_custom_call" | custom-call | bytes 1 | tf_op jit(solution)/shard_map/pallas_call | solution.py:173
  102.5 2.5 %shard_map.52 = (f32[3,64,256]{2,1,0:T(8,128)S(1)}, f32[3,64,256]{2,1,0:T(8,128)S(1)}, f32[3,64,256]{2,1,0:T(8,128)S(1)}, f32[3,64,256]{2,1,0:T(8,128)S(1)}) custom-call(s32[9]{0:T(128)S(1)} %copy-done.5, f32[3,64,1024]{2,1,0:T(8,128)S(1)} %shard_map.51.f_ref, f32[3,256]{1,0:T(4,128)S(1)} %get-tuple-element.54.a_ref, f32[3,256]{1,0:T(4,128)S(1)} %get-tuple-element.55.b_ref, ...), custom_call_target="tpu_custom_call" | custom-call | bytes 1 | tf_op jit(solution)/shard_map/pallas_call | solution.py:421
  105.0 2.4 %collective-permute-start.12 = (f32[3,64,256]{2,1,0:T(8,128)S(1)}, f32[3,64,256]{2,1,0:T(8,128)S(1)}, u32[]{:S(2)}, u32[]{:S(2)}) collective-permute-start(f32[3,64,256]{2,1,0:T(8,128)S(1)} %get-tuple-element.71), channel_id=1, source_target_pairs={{0,2},{1,3},{2,0},{3,1},{4,6},{5,7},{6,4},{7,5},{8,10},{9,11},{10,... | collective-permute-start | bytes 589832 | tf_op jit(solution)/shard_map/ppermute | solution.py:450
  107.5 2.9 %collective-permute-start.13 = (f32[3,64,256]{2,1,0:T(8,128)S(1)}, f32[3,64,256]{2,1,0:T(8,128)S(1)}, u32[]{:S(2)}, u32[]{:S(2)}) collective-permute-start(f32[3,64,256]{2,1,0:T(8,128)S(1)} %get-tuple-element.72), channel_id=1, source_target_pairs={{0,1},{1,2},{2,3},{3,0},{4,5},{5,6},{6,7},{7,4},{8,9},{9,10},{10,1... | collective-permute-start | bytes 589832 | tf_op jit(solution)/shard_map/ppermute | solution.py:450
  110.4 1.2 collective-permute-start.14
  111.6 3.6 %collective-permute-done.17.r3 = f32[3,64,256]{2,1,0:T(8,128)S(1)} collective-permute-done((f32[3,64,256]{2,1,0:T(8,128)}, f32[3,64,256]{2,1,0:T(8,128)S(1)}, u32[]{:S(2)}, u32[]{:S(2)}) %collective-permute-start.17) | collective-permute-done | bytes 196640 | tf_op jit(solution)/shard_map/ppermute | solution.py:450
  115.2 2.6 %shard_map.53.begun = f32[3,512,256]{2,1,0:T(8,128)} custom-call(s32[9]{0:T(128)S(1)} %copy-done.5, f32[3,64,256]{2,1,0:T(8,128)S(1)} %collective-permute-done.15.r2, f32[3,64,256]{2,1,0:T(8,128)} %collective-permute-done.16.r1, f32[3,64,256]{2,1,0:T(8,128)S(1)} %collective-permute-done.17.r3, f32[3,64,256]{2,1,0:T(8,128)S(1)} %copy-done.4), custom_call_target="tpu_custom_call" | custom-call | bytes 1 | tf_op jit(solution)/shard_map/pallas_call | solution.py:319
  117.8 1.2 collective-permute-done.12.r2
  119.1 1.6 %collective-permute-done.13.r1 = f32[3,64,256]{2,1,0:T(8,128)S(1)} collective-permute-done((f32[3,64,256]{2,1,0:T(8,128)S(1)}, f32[3,64,256]{2,1,0:T(8,128)S(1)}, u32[]{:S(2)}, u32[]{:S(2)}) %collective-permute-start.13) | collective-permute-done | bytes 196640 | tf_op jit(solution)/shard_map/ppermute | solution.py:450
  120.6 1.3 %collective-permute-done.14.r3 = f32[3,64,256]{2,1,0:T(8,128)S(1)} collective-permute-done((f32[3,64,256]{2,1,0:T(8,128)S(1)}, f32[3,64,256]{2,1,0:T(8,128)S(1)}, u32[]{:S(2)}, u32[]{:S(2)}) %collective-permute-start.14) | collective-permute-done | bytes 196640 | tf_op jit(solution)/shard_map/ppermute | solution.py:450
  121.9 1.5 %shard_map.54 = f32[3,512,256]{2,1,0:T(8,128)} custom-call(s32[9]{0:T(128)S(1)} %copy-done.5, f32[3,64,256]{2,1,0:T(8,128)S(1)} %collective-permute-done.12.r2, f32[3,64,256]{2,1,0:T(8,128)S(1)} %collective-permute-done.13.r1, f32[3,64,256]{2,1,0:T(8,128)S(1)} %collective-permute-done.14.r3, ...), custom_call_target="tpu_custom_call", output_to_operand_aliasing={{}: (5, {})} | custom-call | bytes 1 | tf_op jit(solution)/shard_map/pallas_call | solution.py:340
  (40 shorter events, 3.7 us)
Async XLA Ops:
  0.0 25.2 %copy-start = (f32[3,513]{1,0:T(4,128)S(1)}, f32[3,513]{1,0:T(4,128)}, u32[]{:S(2)}) copy-start(f32[3,513]{1,0:T(4,128)} %param.6) | copy-start | bytes 18472
  0.8 8.0 %collective-permute-start.1 = (f32[3,16,256]{2,1,0:T(8,128)S(1)}, f32[3,16,256]{2,1,0:T(8,128)S(1)}, u32[]{:S(2)}, u32[]{:S(2)}) collective-permute-start(f32[3,16,256]{2,1,0:T(8,128)S(1)} %get-tuple-element.75), channel_id=1, source_target_pairs={{0,28},{4,0},{8,4},{12,8},{16,12},{20,16},{24,20},{28,24},{1,29},{... | collective-permute-start | bytes 147464 | tf_op jit(solution)/shard_map/ppermute | solution.py:466
  1.6 7.2 %collective-permute-start = (f32[3,16,256]{2,1,0:T(8,128)S(1)}, f32[3,16,256]{2,1,0:T(8,128)S(1)}, u32[]{:S(2)}, u32[]{:S(2)}) collective-permute-start(f32[3,16,256]{2,1,0:T(8,128)S(1)} %get-tuple-element.76), channel_id=1, source_target_pairs={{0,4},{4,8},{8,12},{12,16},{16,20},{20,24},{24,28},{28,0},{1,5},{5... | collective-permute-start | bytes 147464 | tf_op jit(solution)/shard_map/ppermute | solution.py:465
  8.8 0.6 copy-start.8
  8.8 0.6 copy-start.9
  12.0 13.2 %collective-permute-start.5 = (f32[440,256]{1,0:T(8,128)}, f32[440,256]{1,0:T(8,128)S(1)}, u32[]{:S(2)}, u32[]{:S(2)}) collective-permute-start(f32[440,256]{1,0:T(8,128)} %get-tuple-element.47.refs_0_), channel_id=1, source_target_pairs={{0,32},{1,33},{2,34},{3,35},{32,64},{33,65},{34,66},{35,67},{64,96... | collective-permute-start | bytes 1351688 | tf_op jit(solution)/shard_map/ppermute | solution.py:446
  12.0 30.5 %collective-permute-start.2 = (f32[440,256]{1,0:T(8,128)}, f32[440,256]{1,0:T(8,128)S(1)}, u32[]{:S(2)}, u32[]{:S(2)}) collective-permute-start(f32[440,256]{1,0:T(8,128)} %get-tuple-element.44), channel_id=1, source_target_pairs={{0,34},{1,35},{2,32},{3,33},{32,66},{33,67},{34,64},{35,65},{64,98... | collective-permute-start | bytes 1351688 | tf_op jit(solution)/shard_map/ppermute | solution.py:446
  20.4 41.8 %collective-permute-start.3 = (f32[440,256]{1,0:T(8,128)}, f32[440,256]{1,0:T(8,128)S(1)}, u32[]{:S(2)}, u32[]{:S(2)}) collective-permute-start(f32[440,256]{1,0:T(8,128)} %get-tuple-element.45), channel_id=1, source_target_pairs={{0,33},{1,34},{2,35},{3,32},{32,65},{33,66},{34,67},{35,64},{64,97... | collective-permute-start | bytes 1351688 | tf_op jit(solution)/shard_map/ppermute | solution.py:446
  21.4 40.8 %collective-permute-start.4 = (f32[440,256]{1,0:T(8,128)}, f32[440,256]{1,0:T(8,128)S(1)}, u32[]{:S(2)}, u32[]{:S(2)}) collective-permute-start(f32[440,256]{1,0:T(8,128)} %get-tuple-element.46), channel_id=1, source_target_pairs={{0,35},{1,32},{2,33},{3,34},{32,67},{33,64},{34,65},{35,66},{64,99... | collective-permute-start | bytes 1351688 | tf_op jit(solution)/shard_map/ppermute | solution.py:446
  42.5 29.2 %collective-permute-start.7 = (f32[440,256]{1,0:T(8,128)S(1)}, f32[440,256]{1,0:T(8,128)S(1)}, u32[]{:S(2)}, u32[]{:S(2)}) collective-permute-start(f32[440,256]{1,0:T(8,128)S(1)} %collective-permute-done.2.s2.refs_6_), channel_id=1, source_target_pairs={{0,224},{32,0},{64,32},{96,64},{128,96},{160,128},{192,160},{224,1... | collective-permute-start | bytes 1351688 | tf_op jit(solution)/shard_map/ppermute | solution.py:487
  42.5 33.0 %copy-start.5 = (s32[9]{0:T(128)S(1)}, s32[9]{0:T(128)}, u32[]{:S(2)}) copy-start(s32[9]{0:T(128)} %compare_select_fusion.3.t_ref) | copy-start | bytes 112
  45.4 37.2 %copy-start.1 = (f32[440,256]{1,0:T(8,128)S(1)}, f32[440,256]{1,0:T(8,128)}, u32[]{:S(2)}) copy-start(f32[440,256]{1,0:T(8,128)} %get-tuple-element.47.refs_0_) | copy-start | bytes 1351684
  62.1 20.4 %collective-permute-start.8 = (f32[440,256]{1,0:T(8,128)S(1)}, f32[440,256]{1,0:T(8,128)S(1)}, u32[]{:S(2)}, u32[]{:S(2)}) collective-permute-start(f32[440,256]{1,0:T(8,128)S(1)} %collective-permute-done.3.s1.refs_7_), channel_id=1, source_target_pairs={{0,224},{32,0},{64,32},{96,64},{128,96},{160,128},{192,160},{224,1... | collective-permute-start | bytes 1351688 | tf_op jit(solution)/shard_map/ppermute | solution.py:487
  62.5 20.1 %collective-permute-start.6 = (f32[440,256]{1,0:T(8,128)S(1)}, f32[440,256]{1,0:T(8,128)}, u32[]{:S(2)}, u32[]{:S(2)}) collective-permute-start(f32[440,256]{1,0:T(8,128)S(1)} %collective-permute-done.4.s3.refs_5_), channel_id=1, source_target_pairs={{0,224},{32,0},{64,32},{96,64},{128,96},{160,128},{192,160},{224,1... | collective-permute-start | bytes 1351688 | tf_op jit(solution)/shard_map/ppermute | solution.py:487
  63.8 28.6 %collective-permute-start.9 = (f32[3,64,256]{2,1,0:T(8,128)}, f32[3,64,256]{2,1,0:T(8,128)}, u32[]{:S(2)}, u32[]{:S(2)}) collective-permute-start(f32[3,64,256]{2,1,0:T(8,128)} %get-tuple-element.63), channel_id=1, source_target_pairs={{0,3},{1,0},{2,1},{3,2},{224,227},{225,224},{226,225},{227,226},{4... | collective-permute-start | bytes 589832 | tf_op jit(solution)/shard_map/ppermute | solution.py:485
  69.3 26.2 %collective-permute-start.10 = (f32[3,64,256]{2,1,0:T(8,128)}, f32[3,64,256]{2,1,0:T(8,128)}, u32[]{:S(2)}, u32[]{:S(2)}) collective-permute-start(f32[3,64,256]{2,1,0:T(8,128)} %get-tuple-element.64), channel_id=1, source_target_pairs={{0,2},{1,3},{2,0},{3,1},{224,226},{225,227},{226,224},{227,225},{4... | collective-permute-start | bytes 589832 | tf_op jit(solution)/shard_map/ppermute | solution.py:485
  71.7 23.7 %collective-permute-start.11 = (f32[3,64,256]{2,1,0:T(8,128)}, f32[3,64,256]{2,1,0:T(8,128)}, u32[]{:S(2)}, u32[]{:S(2)}) collective-permute-start(f32[3,64,256]{2,1,0:T(8,128)} %get-tuple-element.65), channel_id=1, source_target_pairs={{0,1},{1,2},{2,3},{3,0},{224,225},{225,226},{226,227},{227,224},{4... | collective-permute-start | bytes 589832 | tf_op jit(solution)/shard_map/ppermute | solution.py:485
  85.5 0.7 copy-start.3
  86.2 0.7 copy-start.6
  86.9 0.7 copy-start.7
  87.6 14.9 %copy-start.2 = (f32[3,64,256]{2,1,0:T(8,128)S(1)}, f32[3,64,256]{2,1,0:T(8,128)}, u32[]{:S(2)}) copy-start(f32[3,64,256]{2,1,0:T(8,128)} %get-tuple-element.67.refs_4_) | copy-start | bytes 589828
  87.6 22.8 %collective-permute-start.16 = (f32[3,64,256]{2,1,0:T(8,128)}, f32[3,64,256]{2,1,0:T(8,128)}, u32[]{:S(2)}, u32[]{:S(2)}) collective-permute-start(f32[3,64,256]{2,1,0:T(8,128)} %get-tuple-element.59), channel_id=1, source_target_pairs={{0,1},{1,2},{2,3},{3,0},{4,5},{5,6},{6,7},{7,4},{8,9},{9,10},{10,1... | collective-permute-start | bytes 589832 | tf_op jit(solution)/shard_map/ppermute | solution.py:450
  91.7 19.9 %collective-permute-start.15 = (f32[3,64,256]{2,1,0:T(8,128)}, f32[3,64,256]{2,1,0:T(8,128)S(1)}, u32[]{:S(2)}, u32[]{:S(2)}) collective-permute-start(f32[3,64,256]{2,1,0:T(8,128)} %copy-done.7), channel_id=1, source_target_pairs={{0,2},{1,3},{2,0},{3,1},{4,6},{5,7},{6,4},{7,5},{8,10},{9,11},{10,... | collective-permute-start | bytes 589832 | tf_op jit(solution)/shard_map/ppermute | solution.py:450
  92.4 22.9 %collective-permute-start.17 = (f32[3,64,256]{2,1,0:T(8,128)}, f32[3,64,256]{2,1,0:T(8,128)S(1)}, u32[]{:S(2)}, u32[]{:S(2)}) collective-permute-start(f32[3,64,256]{2,1,0:T(8,128)} %copy-done.6), channel_id=1, source_target_pairs={{0,3},{1,0},{2,1},{3,2},{4,7},{5,4},{6,5},{7,6},{8,11},{9,8},{10,9... | collective-permute-start | bytes 589832 | tf_op jit(solution)/shard_map/ppermute | solution.py:450
  102.5 12.8 %copy-start.4 = (f32[3,64,256]{2,1,0:T(8,128)S(1)}, f32[3,64,256]{2,1,0:T(8,128)}, u32[]{:S(2)}) copy-start(f32[3,64,256]{2,1,0:T(8,128)} %copy-done.3) | copy-start | bytes 589828
  105.0 14.0 %collective-permute-start.12 = (f32[3,64,256]{2,1,0:T(8,128)S(1)}, f32[3,64,256]{2,1,0:T(8,128)S(1)}, u32[]{:S(2)}, u32[]{:S(2)}) collective-permute-start(f32[3,64,256]{2,1,0:T(8,128)S(1)} %get-tuple-element.71), channel_id=1, source_target_pairs={{0,2},{1,3},{2,0},{3,1},{4,6},{5,7},{6,4},{7,5},{8,10},{9,11},{10,... | collective-permute-start | bytes 589832 | tf_op jit(solution)/shard_map/ppermute | solution.py:450
  107.5 13.2 %collective-permute-start.13 = (f32[3,64,256]{2,1,0:T(8,128)S(1)}, f32[3,64,256]{2,1,0:T(8,128)S(1)}, u32[]{:S(2)}, u32[]{:S(2)}) collective-permute-start(f32[3,64,256]{2,1,0:T(8,128)S(1)} %get-tuple-element.72), channel_id=1, source_target_pairs={{0,1},{1,2},{2,3},{3,0},{4,5},{5,6},{6,7},{7,4},{8,9},{9,10},{10,1... | collective-permute-start | bytes 589832 | tf_op jit(solution)/shard_map/ppermute | solution.py:450
  110.4 11.5 %collective-permute-start.14 = (f32[3,64,256]{2,1,0:T(8,128)S(1)}, f32[3,64,256]{2,1,0:T(8,128)S(1)}, u32[]{:S(2)}, u32[]{:S(2)}) collective-permute-start(f32[3,64,256]{2,1,0:T(8,128)S(1)} %get-tuple-element.73), channel_id=1, source_target_pairs={{0,3},{1,0},{2,1},{3,2},{4,7},{5,4},{6,5},{7,6},{8,11},{9,8},{10,9... | collective-permute-start | bytes 589832 | tf_op jit(solution)/shard_map/ppermute | solution.py:450

commit v8 on v6

--- a/solution.py
+++ b/solution.py
@@ -20,7 +20,7 @@
 CHUNK = ROWS // 2
 SENT = 440
 TILES = CHUNK + 2 * HALO
-GROUP = 40
+LOOPS = 1
 SPARE = 16
 F32 = jnp.float32
 BF16 = jnp.bfloat16
@@ -83,6 +83,7 @@
 
 
 def stage(src, base, dst, f_ref, lo, rows, kind):
+    group = rows // LOOPS
     lane = lax.broadcasted_iota(jnp.int32, (8, 128), 1)
     is_first = lane == 0
     is_last = lane == 127
@@ -95,16 +96,16 @@
         return up, down
 
     def body(g, carry):
-        row = lo + g * GROUP
+        row = lo + g * group
 
         def load(ref, c, k):
             return ref[c, pl.ds(pl.multiple_of((row + k) * 8, 8), 8), :]
 
-        d = [load(src, 0, k) for k in range(-1, GROUP + 1)]
-        u = [load(src, 1, k) for k in range(-1, GROUP + 1)]
-        v = [load(src, 2, k) for k in range(-1, GROUP + 1)]
-        flux = [d[k] * v[k] for k in range(GROUP + 2)]
-        for k in range(1, GROUP + 1):
+        d = [load(src, 0, k) for k in range(-1, group + 1)]
+        u = [load(src, 1, k) for k in range(-1, group + 1)]
+        v = [load(src, 2, k) for k in range(-1, group + 1)]
+        flux = [d[k] * v[k] for k in range(group + 2)]
+        for k in range(1, group + 1):
             f = f_ref[row + k - 1]
             d_up, d_down = neighbours(d[k])
             u_up, u_down = neighbours(u[k])
@@ -121,7 +122,7 @@
                 dst[c, pl.ds(pl.multiple_of((row + k - 1) * 8, 8), 8), :] = new
         return carry
 
-    lax.fori_loop(0, -(-rows // GROUP), body, 0)
+    lax.fori_loop(0, LOOPS, body, 0)
 
 
 def half_of(chunk, t_ref):

time: 126 us -> 124 us (0.984)
  Pallas kernels: 32.2 us -> 28.5 us
  waiting for transfers between devices: 41.9 us -> 43.8 us
    pallas_call x2, Pallas kernels: 14 us -> 10.4 us  [model_call(): call(functools.partial(model_kernel, chunk), array(3, CHUNK, NLON), [smem...]
    ppermute x6, waiting for transfers between devices: 9.31 us -> 11.2 us  [to_lon(): return lax.ppermute(value, 'lon', ring(LON, j))]
  transfers between devices with their start and end apart: 18 -> 18, of which waited for: 6 -> 5; matrix products, arithmetic and copies ran while one was open for 3% -> 3% of each run, Pallas kernels for 23% -> 20%
where the time goes in v8:
time: 124 us; the launch traced here: 122 us
  waiting for transfers between devices  43.8 us (35%)
  starting transfers between devices  42.8 us (35%)
  Pallas kernels  28.5 us (23%)
  local copies, waits for them, and re-layouts  3.51 us (3%)
  matrix products  2.76 us (2%)
    ppermute x4, waiting for transfers between devices, to_next(): return lax.ppermute(value, ('sub', 'lon'), pairs)  32.6 us
    ppermute x6, starting transfers between devices, to_lon(): return lax.ppermute(value, 'lon', ring(LON, j))  14.4 us
    ppermute x4, starting transfers between devices, to_next(): return lax.ppermute(value, ('sub', 'lon'), pairs)  12 us
    ppermute x6, waiting for transfers between devices, to_lon(): return lax.ppermute(value, 'lon', ring(LON, j))  11.2 us
    ppermute x3, starting transfers between devices, shards(): extra[j] = lax.ppermute(block, ('sub', 'lon'), pairs) if j else block  10.7 us
    pallas_call x2, Pallas kernels, model_call(): call(functools.partial(model_kernel, chunk), array(3, CHUNK, NLON), [smem...  10.4 us
    pallas_call x2, Pallas kernels, weight_call(): call(functools.partial(weight_kernel, chunk), [array(3, CHUNK, 256)] * 4,...  5.49 us
    ppermute x1, starting transfers between devices, shards(): above = lax.ppermute(x[:, tile_rows - 16:], 'lat', ring(8, 1))  3.39 us
  transfers between devices with their start and end apart: 18, of which 5 were waited for; matrix products, arithmetic and copies ran while one was open for 3% of the time, Pallas kernels for 20%

profile of v8, /device:TPU:24, one launch (start us, length us, event | category | flops | bytes accessed | tf_op | source)
XLA Modules:
  0.0 122.5 jit_solution(9795194012428627065)
XLA Ops:
  0.0 0.8 fusion.6
  0.8 0.8 collective-permute-start.1
  1.6 3.4 %collective-permute-start = (f32[3,16,256]{2,1,0:T(8,128)S(1)}, f32[3,16,256]{2,1,0:T(8,128)S(1)}, u32[]{:S(2)}, u32[]{:S(2)}) collective-permute-start(f32[3,16,256]{2,1,0:T(8,128)S(1)} %get-tuple-element.76), channel_id=1, source_target_pairs={{0,4},{4,8},{8,12},{12,16},{16,20},{20,24},{24,28},{28,0},{1,5},{5... | collective-permute-start | bytes 147464 | tf_op jit(solution)/shard_map/ppermute | solution.py:466
  5.6 3.2 %shard_map.46 = (f32[440,256]{1,0:T(8,128)}, f32[440,256]{1,0:T(8,128)}, f32[440,256]{1,0:T(8,128)}, f32[440,256]{1,0:T(8,128)}) custom-call(s32[9]{0:T(128)} %compare_select_fusion.3.t_ref, f32[3,512,256]{2,1,0:T(8,128)} %bitcast.5, f32[3,512,256]{2,1,0:T(8,128)} %back.3), custom_call_target="tpu_custom_call" | custom-call | bytes 1 | tf_op jit(solution)/shard_map/pallas_call | solution.py:252
  9.4 2.5 %shard_map.47 = (f32[440,256]{1,0:T(8,128)}, f32[440,256]{1,0:T(8,128)}, f32[440,256]{1,0:T(8,128)}, f32[440,256]{1,0:T(8,128)}) custom-call(s32[9]{0:T(128)} %compare_select_fusion.3.t_ref, f32[3,512,256]{2,1,0:T(8,128)} %bitcast.6, f32[3,16,256]{2,1,0:T(8,128)} %copy-done.9, ...), custom_call_target="tpu_custom_call", output_to_operand_aliasing={{0}: (4, {}), {1}: (5, {}), {2}: (6, {}), {3}: (7, {})} | custom-call | bytes 1 | tf_op jit(solution)/shard_map/pallas_call | solution.py:290
  12.0 8.4 %collective-permute-start.4 = (f32[440,256]{1,0:T(8,128)}, f32[440,256]{1,0:T(8,128)S(1)}, u32[]{:S(2)}, u32[]{:S(2)}) collective-permute-start(f32[440,256]{1,0:T(8,128)} %get-tuple-element.46), channel_id=1, source_target_pairs={{0,34},{1,35},{2,32},{3,33},{32,66},{33,67},{34,64},{35,65},{64,98... | collective-permute-start | bytes 1351688 | tf_op jit(solution)/shard_map/ppermute | solution.py:447
  20.4 3.6 %collective-permute-start.5 = (f32[440,256]{1,0:T(8,128)}, f32[440,256]{1,0:T(8,128)S(1)}, u32[]{:S(2)}, u32[]{:S(2)}) collective-permute-start(f32[440,256]{1,0:T(8,128)} %get-tuple-element.47), channel_id=1, source_target_pairs={{0,33},{1,34},{2,35},{3,32},{32,65},{33,66},{34,67},{35,64},{64,97... | collective-permute-start | bytes 1351688 | tf_op jit(solution)/shard_map/ppermute | solution.py:447
  23.9 2.8 %fusion.7 = f32[3,1024]{1,0:T(4,128)S(1)} fusion(f32[3,513]{1,0:T(4,128)S(1)} %copy-done, f32[513,1024]{1,0:T(8,128)} %constant.52.clone), kind=kOutput, calls=%fused_computation.16 | convolution fusion | flops 18911232 | bytes 2119692 | tf_op jit(solution)/shard_map/dot_general | solution.py:375
  26.7 14.4 %collective-permute-done.4.s2.refs_6_ = f32[440,256]{1,0:T(8,128)S(1)} collective-permute-done((f32[440,256]{1,0:T(8,128)}, f32[440,256]{1,0:T(8,128)S(1)}, u32[]{:S(2)}, u32[]{:S(2)}) %collective-permute-start.4) | collective-permute-done | bytes 450592 | tf_op jit(solution)/shard_map/ppermute | solution.py:447
  41.1 2.9 %shard_map.49 = (f32[3,64,256]{2,1,0:T(8,128)}, f32[3,64,256]{2,1,0:T(8,128)}, f32[3,64,256]{2,1,0:T(8,128)}, f32[3,64,256]{2,1,0:T(8,128)}) custom-call(s32[9]{0:T(128)} %compare_select_fusion.3.t_ref, f32[3,512,256]{2,1,0:T(8,128)} %bitcast.7, f32[3,512,256]{2,1,0:T(8,128)} %back.3), custom_call_target="tpu_custom_call" | custom-call | bytes 1 | tf_op jit(solution)/shard_map/pallas_call | solution.py:208
  44.1 18.2 %collective-permute-done.3.s3.refs_5_ = f32[440,256]{1,0:T(8,128)S(1)} collective-permute-done((f32[440,256]{1,0:T(8,128)}, f32[440,256]{1,0:T(8,128)S(1)}, u32[]{:S(2)}, u32[]{:S(2)}) %collective-permute-start.3) | collective-permute-done | bytes 450592 | tf_op jit(solution)/shard_map/ppermute | solution.py:447
  62.5 1.4 %collective-permute-start.6 = (f32[440,256]{1,0:T(8,128)S(1)}, f32[440,256]{1,0:T(8,128)}, u32[]{:S(2)}, u32[]{:S(2)}) collective-permute-start(f32[440,256]{1,0:T(8,128)S(1)} %collective-permute-done.3.s3.refs_5_), channel_id=1, source_target_pairs={{0,224},{32,0},{64,32},{96,64},{128,96},{160,128},{192,160},{224,1... | collective-permute-start | bytes 1351688 | tf_op jit(solution)/shard_map/ppermute | solution.py:488
  63.9 4.5 %collective-permute-start.9 = (f32[3,64,256]{2,1,0:T(8,128)}, f32[3,64,256]{2,1,0:T(8,128)}, u32[]{:S(2)}, u32[]{:S(2)}) collective-permute-start(f32[3,64,256]{2,1,0:T(8,128)} %get-tuple-element.63), channel_id=1, source_target_pairs={{0,3},{1,0},{2,1},{3,2},{224,227},{225,224},{226,225},{227,226},{4... | collective-permute-start | bytes 589832 | tf_op jit(solution)/shard_map/ppermute | solution.py:486
  68.3 3.7 %collective-permute-start.10 = (f32[3,64,256]{2,1,0:T(8,128)}, f32[3,64,256]{2,1,0:T(8,128)}, u32[]{:S(2)}, u32[]{:S(2)}) collective-permute-start(f32[3,64,256]{2,1,0:T(8,128)} %get-tuple-element.64), channel_id=1, source_target_pairs={{0,2},{1,3},{2,0},{3,1},{224,226},{225,227},{226,224},{227,225},{4... | collective-permute-start | bytes 589832 | tf_op jit(solution)/shard_map/ppermute | solution.py:486
  72.1 2.5 %collective-permute-start.11 = (f32[3,64,256]{2,1,0:T(8,128)}, f32[3,64,256]{2,1,0:T(8,128)}, u32[]{:S(2)}, u32[]{:S(2)}) collective-permute-start(f32[3,64,256]{2,1,0:T(8,128)} %get-tuple-element.65), channel_id=1, source_target_pairs={{0,1},{1,2},{2,3},{3,0},{224,225},{225,226},{226,227},{227,224},{4... | collective-permute-start | bytes 589832 | tf_op jit(solution)/shard_map/ppermute | solution.py:486
  74.6 5.2 %shard_map.48.f_ref = f32[3,64,1024]{2,1,0:T(8,128)S(1)} custom-call(s32[9]{0:T(128)S(1)} %copy-done.5, f32[98]{0:T(128)S(1)} %sine_multiply_fusion.f_ref, f32[440,256]{1,0:T(8,128)S(1)} %collective-permute-done.2.s0.refs_4_, f32[440,256]{1,0:T(8,128)S(1)} %collective-permute-done.3.s3.refs_5_, f32[440,256]{1,0:T(8,128)S(1)} %collective-permute-done.4.s2.refs_6_, ...), custom_call_target="tpu_custom_call" | custom-call | bytes 1 | tf_op jit(solution)/shard_map/pallas_call | solution.py:174
  79.8 2.9 %shard_map.50 = (f32[3,64,256]{2,1,0:T(8,128)S(1)}, f32[3,64,256]{2,1,0:T(8,128)}, f32[3,64,256]{2,1,0:T(8,128)S(1)}, f32[3,64,256]{2,1,0:T(8,128)S(1)}) custom-call(s32[9]{0:T(128)S(1)} %copy-done.5, f32[3,64,1024]{2,1,0:T(8,128)S(1)} %shard_map.48.f_ref, f32[3,256]{1,0:T(4,128)S(1)} %get-tuple-element.54.a_ref, f32[3,256]{1,0:T(4,128)S(1)} %get-tuple-element.55.b_ref, ...), custom_call_target="tpu_custom_call" | custom-call | bytes 1 | tf_op jit(solution)/shard_map/pallas_call | solution.py:422
  82.8 0.7 copy-done.3
  83.5 0.7 copy-done.6
  84.1 0.7 copy-done.7
  84.8 4.1 %collective-permute-start.15 = (f32[3,64,256]{2,1,0:T(8,128)}, f32[3,64,256]{2,1,0:T(8,128)}, u32[]{:S(2)}, u32[]{:S(2)}) collective-permute-start(f32[3,64,256]{2,1,0:T(8,128)} %get-tuple-element.59), channel_id=1, source_target_pairs={{0,1},{1,2},{2,3},{3,0},{4,5},{5,6},{6,7},{7,4},{8,9},{9,10},{10,1... | collective-permute-start | bytes 589832 | tf_op jit(solution)/shard_map/ppermute | solution.py:451
  89.0 1.9 %collective-permute-start.16 = (f32[3,64,256]{2,1,0:T(8,128)}, f32[3,64,256]{2,1,0:T(8,128)S(1)}, u32[]{:S(2)}, u32[]{:S(2)}) collective-permute-start(f32[3,64,256]{2,1,0:T(8,128)} %copy-done.7), channel_id=1, source_target_pairs={{0,2},{1,3},{2,0},{3,1},{4,6},{5,7},{6,4},{7,5},{8,10},{9,11},{10,... | collective-permute-start | bytes 589832 | tf_op jit(solution)/shard_map/ppermute | solution.py:451
  90.9 2.1 %collective-permute-start.17 = (f32[3,64,256]{2,1,0:T(8,128)}, f32[3,64,256]{2,1,0:T(8,128)S(1)}, u32[]{:S(2)}, u32[]{:S(2)}) collective-permute-start(f32[3,64,256]{2,1,0:T(8,128)} %copy-done.6), channel_id=1, source_target_pairs={{0,3},{1,0},{2,1},{3,2},{4,7},{5,4},{6,5},{7,6},{8,11},{9,8},{10,9... | collective-permute-start | bytes 589832 | tf_op jit(solution)/shard_map/ppermute | solution.py:451
  93.0 5.2 %shard_map.51.f_ref = f32[3,64,1024]{2,1,0:T(8,128)S(1)} custom-call(s32[9]{0:T(128)S(1)} %copy-done.5, f32[98]{0:T(128)S(1)} %sine_multiply_fusion.1.f_ref, f32[440,256]{1,0:T(8,128)S(1)} %collective-permute-done.2.s0.refs_4_, f32[440,256]{1,0:T(8,128)S(1)} %collective-permute-done.3.s3.refs_5_, f32[440,256]{1,0:T(8,128)S(1)} %collective-permute-done.4.s2.refs_6_, ...), custom_call_target="tpu_custom_call" | custom-call | bytes 1 | tf_op jit(solution)/shard_map/pallas_call | solution.py:174
  98.2 2.5 %shard_map.52 = (f32[3,64,256]{2,1,0:T(8,128)S(1)}, f32[3,64,256]{2,1,0:T(8,128)S(1)}, f32[3,64,256]{2,1,0:T(8,128)S(1)}, f32[3,64,256]{2,1,0:T(8,128)S(1)}) custom-call(s32[9]{0:T(128)S(1)} %copy-done.5, f32[3,64,1024]{2,1,0:T(8,128)S(1)} %shard_map.51.f_ref, f32[3,256]{1,0:T(4,128)S(1)} %get-tuple-element.54.a_ref, f32[3,256]{1,0:T(4,128)S(1)} %get-tuple-element.55.b_ref, ...), custom_call_target="tpu_custom_call" | custom-call | bytes 1 | tf_op jit(solution)/shard_map/pallas_call | solution.py:422
  100.8 0.9 collective-permute-start.12
  101.7 4.1 %collective-permute-start.13 = (f32[3,64,256]{2,1,0:T(8,128)S(1)}, f32[3,64,256]{2,1,0:T(8,128)S(1)}, u32[]{:S(2)}, u32[]{:S(2)}) collective-permute-start(f32[3,64,256]{2,1,0:T(8,128)S(1)} %get-tuple-element.73), channel_id=1, source_target_pairs={{0,2},{1,3},{2,0},{3,1},{4,6},{5,7},{6,4},{7,5},{8,10},{9,11},{10,... | collective-permute-start | bytes 589832 | tf_op jit(solution)/shard_map/ppermute | solution.py:451
  105.8 1.2 %collective-permute-start.14 = (f32[3,64,256]{2,1,0:T(8,128)S(1)}, f32[3,64,256]{2,1,0:T(8,128)S(1)}, u32[]{:S(2)}, u32[]{:S(2)}) collective-permute-start(f32[3,64,256]{2,1,0:T(8,128)S(1)} %get-tuple-element.74), channel_id=1, source_target_pairs={{0,3},{1,0},{2,1},{3,2},{4,7},{5,4},{6,5},{7,6},{8,11},{9,8},{10,9... | collective-permute-start | bytes 589832 | tf_op jit(solution)/shard_map/ppermute | solution.py:451
  107.0 2.0 %collective-permute-done.16.r2 = f32[3,64,256]{2,1,0:T(8,128)S(1)} collective-permute-done((f32[3,64,256]{2,1,0:T(8,128)}, f32[3,64,256]{2,1,0:T(8,128)S(1)}, u32[]{:S(2)}, u32[]{:S(2)}) %collective-permute-start.16) | collective-permute-done | bytes 196640 | tf_op jit(solution)/shard_map/ppermute | solution.py:451
  109.1 9.1 %collective-permute-done.17.r3 = f32[3,64,256]{2,1,0:T(8,128)S(1)} collective-permute-done((f32[3,64,256]{2,1,0:T(8,128)}, f32[3,64,256]{2,1,0:T(8,128)S(1)}, u32[]{:S(2)}, u32[]{:S(2)}) %collective-permute-start.17) | collective-permute-done | bytes 196640 | tf_op jit(solution)/shard_map/ppermute | solution.py:451
  118.1 2.6 %shard_map.53.begun = f32[3,512,256]{2,1,0:T(8,128)} custom-call(s32[9]{0:T(128)S(1)} %copy-done.5, f32[3,64,256]{2,1,0:T(8,128)S(1)} %copy-done.4, f32[3,64,256]{2,1,0:T(8,128)} %collective-permute-done.15.r1, f32[3,64,256]{2,1,0:T(8,128)S(1)} %collective-permute-done.16.r2, f32[3,64,256]{2,1,0:T(8,128)S(1)} %collective-permute-done.17.r3), custom_call_target="tpu_custom_call" | custom-call | bytes 1 | tf_op jit(solution)/shard_map/pallas_call | solution.py:320
  120.9 1.5 %shard_map.54 = f32[3,512,256]{2,1,0:T(8,128)} custom-call(s32[9]{0:T(128)S(1)} %copy-done.5, f32[3,64,256]{2,1,0:T(8,128)S(1)} %get-tuple-element.71.o0, f32[3,64,256]{2,1,0:T(8,128)S(1)} %collective-permute-done.12.r1, f32[3,64,256]{2,1,0:T(8,128)S(1)} %collective-permute-done.13.r2, ...), custom_call_target="tpu_custom_call", output_to_operand_aliasing={{}: (5, {})} | custom-call | bytes 1 | tf_op jit(solution)/shard_map/pallas_call | solution.py:341
  (40 shorter events, 1.7 us)
Async XLA Ops:
  0.0 23.9 %copy-start = (f32[3,513]{1,0:T(4,128)S(1)}, f32[3,513]{1,0:T(4,128)}, u32[]{:S(2)}) copy-start(f32[3,513]{1,0:T(4,128)} %param.6) | copy-start | bytes 18472
  0.8 8.0 %collective-permute-start.1 = (f32[3,16,256]{2,1,0:T(8,128)S(1)}, f32[3,16,256]{2,1,0:T(8,128)S(1)}, u32[]{:S(2)}, u32[]{:S(2)}) collective-permute-start(f32[3,16,256]{2,1,0:T(8,128)S(1)} %get-tuple-element.75), channel_id=1, source_target_pairs={{0,28},{4,0},{8,4},{12,8},{16,12},{20,16},{24,20},{28,24},{1,29},{... | collective-permute-start | bytes 147464 | tf_op jit(solution)/shard_map/ppermute | solution.py:467
  1.6 7.2 %collective-permute-start = (f32[3,16,256]{2,1,0:T(8,128)S(1)}, f32[3,16,256]{2,1,0:T(8,128)S(1)}, u32[]{:S(2)}, u32[]{:S(2)}) collective-permute-start(f32[3,16,256]{2,1,0:T(8,128)S(1)} %get-tuple-element.76), channel_id=1, source_target_pairs={{0,4},{4,8},{8,12},{12,16},{16,20},{20,24},{24,28},{28,0},{1,5},{5... | collective-permute-start | bytes 147464 | tf_op jit(solution)/shard_map/ppermute | solution.py:466
  8.8 0.6 copy-start.8
  8.8 0.6 copy-start.9
  12.0 12.0 %collective-permute-start.2 = (f32[440,256]{1,0:T(8,128)}, f32[440,256]{1,0:T(8,128)S(1)}, u32[]{:S(2)}, u32[]{:S(2)}) collective-permute-start(f32[440,256]{1,0:T(8,128)} %get-tuple-element.44.refs_0_), channel_id=1, source_target_pairs={{0,32},{1,33},{2,34},{3,35},{32,64},{33,65},{34,66},{35,67},{64,96... | collective-permute-start | bytes 1351688 | tf_op jit(solution)/shard_map/ppermute | solution.py:447
  12.0 29.1 %collective-permute-start.4 = (f32[440,256]{1,0:T(8,128)}, f32[440,256]{1,0:T(8,128)S(1)}, u32[]{:S(2)}, u32[]{:S(2)}) collective-permute-start(f32[440,256]{1,0:T(8,128)} %get-tuple-element.46), channel_id=1, source_target_pairs={{0,34},{1,35},{2,32},{3,33},{32,66},{33,67},{34,64},{35,65},{64,98... | collective-permute-start | bytes 1351688 | tf_op jit(solution)/shard_map/ppermute | solution.py:447
  20.4 41.9 %collective-permute-start.3 = (f32[440,256]{1,0:T(8,128)}, f32[440,256]{1,0:T(8,128)S(1)}, u32[]{:S(2)}, u32[]{:S(2)}) collective-permute-start(f32[440,256]{1,0:T(8,128)} %get-tuple-element.45), channel_id=1, source_target_pairs={{0,35},{1,32},{2,33},{3,34},{32,67},{33,64},{34,65},{35,66},{64,99... | collective-permute-start | bytes 1351688 | tf_op jit(solution)/shard_map/ppermute | solution.py:447
  20.4 41.9 %collective-permute-start.5 = (f32[440,256]{1,0:T(8,128)}, f32[440,256]{1,0:T(8,128)S(1)}, u32[]{:S(2)}, u32[]{:S(2)}) collective-permute-start(f32[440,256]{1,0:T(8,128)} %get-tuple-element.47), channel_id=1, source_target_pairs={{0,33},{1,34},{2,35},{3,32},{32,65},{33,66},{34,67},{35,64},{64,97... | collective-permute-start | bytes 1351688 | tf_op jit(solution)/shard_map/ppermute | solution.py:447
  41.1 31.0 %collective-permute-start.7 = (f32[440,256]{1,0:T(8,128)S(1)}, f32[440,256]{1,0:T(8,128)S(1)}, u32[]{:S(2)}, u32[]{:S(2)}) collective-permute-start(f32[440,256]{1,0:T(8,128)S(1)} %collective-permute-done.4.s2.refs_6_), channel_id=1, source_target_pairs={{0,224},{32,0},{64,32},{96,64},{128,96},{160,128},{192,160},{224,1... | collective-permute-start | bytes 1351688 | tf_op jit(solution)/shard_map/ppermute | solution.py:488
  41.1 33.5 %copy-start.5 = (s32[9]{0:T(128)S(1)}, s32[9]{0:T(128)}, u32[]{:S(2)}) copy-start(s32[9]{0:T(128)} %compare_select_fusion.3.t_ref) | copy-start | bytes 112
  44.0 35.8 %copy-start.1 = (f32[440,256]{1,0:T(8,128)S(1)}, f32[440,256]{1,0:T(8,128)}, u32[]{:S(2)}) copy-start(f32[440,256]{1,0:T(8,128)} %get-tuple-element.44.refs_0_) | copy-start | bytes 1351684
  62.3 17.5 %collective-permute-start.8 = (f32[440,256]{1,0:T(8,128)S(1)}, f32[440,256]{1,0:T(8,128)S(1)}, u32[]{:S(2)}, u32[]{:S(2)}) collective-permute-start(f32[440,256]{1,0:T(8,128)S(1)} %collective-permute-done.5.s1.refs_7_), channel_id=1, source_target_pairs={{0,224},{32,0},{64,32},{96,64},{128,96},{160,128},{192,160},{224,1... | collective-permute-start | bytes 1351688 | tf_op jit(solution)/shard_map/ppermute | solution.py:488
  62.5 17.3 %collective-permute-start.6 = (f32[440,256]{1,0:T(8,128)S(1)}, f32[440,256]{1,0:T(8,128)}, u32[]{:S(2)}, u32[]{:S(2)}) collective-permute-start(f32[440,256]{1,0:T(8,128)S(1)} %collective-permute-done.3.s3.refs_5_), channel_id=1, source_target_pairs={{0,224},{32,0},{64,32},{96,64},{128,96},{160,128},{192,160},{224,1... | collective-permute-start | bytes 1351688 | tf_op jit(solution)/shard_map/ppermute | solution.py:488
  63.9 27.1 %collective-permute-start.9 = (f32[3,64,256]{2,1,0:T(8,128)}, f32[3,64,256]{2,1,0:T(8,128)}, u32[]{:S(2)}, u32[]{:S(2)}) collective-permute-start(f32[3,64,256]{2,1,0:T(8,128)} %get-tuple-element.63), channel_id=1, source_target_pairs={{0,3},{1,0},{2,1},{3,2},{224,227},{225,224},{226,225},{227,226},{4... | collective-permute-start | bytes 589832 | tf_op jit(solution)/shard_map/ppermute | solution.py:486
  68.3 24.7 %collective-permute-start.10 = (f32[3,64,256]{2,1,0:T(8,128)}, f32[3,64,256]{2,1,0:T(8,128)}, u32[]{:S(2)}, u32[]{:S(2)}) collective-permute-start(f32[3,64,256]{2,1,0:T(8,128)} %get-tuple-element.64), channel_id=1, source_target_pairs={{0,2},{1,3},{2,0},{3,1},{224,226},{225,227},{226,224},{227,225},{4... | collective-permute-start | bytes 589832 | tf_op jit(solution)/shard_map/ppermute | solution.py:486
  72.1 20.9 %collective-permute-start.11 = (f32[3,64,256]{2,1,0:T(8,128)}, f32[3,64,256]{2,1,0:T(8,128)}, u32[]{:S(2)}, u32[]{:S(2)}) collective-permute-start(f32[3,64,256]{2,1,0:T(8,128)} %get-tuple-element.65), channel_id=1, source_target_pairs={{0,1},{1,2},{2,3},{3,0},{224,225},{225,226},{226,227},{227,224},{4... | collective-permute-start | bytes 589832 | tf_op jit(solution)/shard_map/ppermute | solution.py:486
  82.8 0.7 copy-start.3
  83.5 0.7 copy-start.6
  84.1 0.7 copy-start.7
  84.8 13.4 %copy-start.2 = (f32[3,64,256]{2,1,0:T(8,128)S(1)}, f32[3,64,256]{2,1,0:T(8,128)}, u32[]{:S(2)}) copy-start(f32[3,64,256]{2,1,0:T(8,128)} %get-tuple-element.67.refs_4_) | copy-start | bytes 589828
  84.8 21.0 %collective-permute-start.15 = (f32[3,64,256]{2,1,0:T(8,128)}, f32[3,64,256]{2,1,0:T(8,128)}, u32[]{:S(2)}, u32[]{:S(2)}) collective-permute-start(f32[3,64,256]{2,1,0:T(8,128)} %get-tuple-element.59), channel_id=1, source_target_pairs={{0,1},{1,2},{2,3},{3,0},{4,5},{5,6},{6,7},{7,4},{8,9},{9,10},{10,1... | collective-permute-start | bytes 589832 | tf_op jit(solution)/shard_map/ppermute | solution.py:451
  89.0 20.1 %collective-permute-start.16 = (f32[3,64,256]{2,1,0:T(8,128)}, f32[3,64,256]{2,1,0:T(8,128)S(1)}, u32[]{:S(2)}, u32[]{:S(2)}) collective-permute-start(f32[3,64,256]{2,1,0:T(8,128)} %copy-done.7), channel_id=1, source_target_pairs={{0,2},{1,3},{2,0},{3,1},{4,6},{5,7},{6,4},{7,5},{8,10},{9,11},{10,... | collective-permute-start | bytes 589832 | tf_op jit(solution)/shard_map/ppermute | solution.py:451
  90.9 27.2 %collective-permute-start.17 = (f32[3,64,256]{2,1,0:T(8,128)}, f32[3,64,256]{2,1,0:T(8,128)S(1)}, u32[]{:S(2)}, u32[]{:S(2)}) collective-permute-start(f32[3,64,256]{2,1,0:T(8,128)} %copy-done.6), channel_id=1, source_target_pairs={{0,3},{1,0},{2,1},{3,2},{4,7},{5,4},{6,5},{7,6},{8,11},{9,8},{10,9... | collective-permute-start | bytes 589832 | tf_op jit(solution)/shard_map/ppermute | solution.py:451
  98.2 19.9 %copy-start.4 = (f32[3,64,256]{2,1,0:T(8,128)S(1)}, f32[3,64,256]{2,1,0:T(8,128)}, u32[]{:S(2)}) copy-start(f32[3,64,256]{2,1,0:T(8,128)} %copy-done.3) | copy-start | bytes 589828
  100.8 19.9 %collective-permute-start.12 = (f32[3,64,256]{2,1,0:T(8,128)S(1)}, f32[3,64,256]{2,1,0:T(8,128)S(1)}, u32[]{:S(2)}, u32[]{:S(2)}) collective-permute-start(f32[3,64,256]{2,1,0:T(8,128)S(1)} %get-tuple-element.72), channel_id=1, source_target_pairs={{0,1},{1,2},{2,3},{3,0},{4,5},{5,6},{6,7},{7,4},{8,9},{9,10},{10,1... | collective-permute-start | bytes 589832 | tf_op jit(solution)/shard_map/ppermute | solution.py:451
  101.7 19.0 %collective-permute-start.13 = (f32[3,64,256]{2,1,0:T(8,128)S(1)}, f32[3,64,256]{2,1,0:T(8,128)S(1)}, u32[]{:S(2)}, u32[]{:S(2)}) collective-permute-start(f32[3,64,256]{2,1,0:T(8,128)S(1)} %get-tuple-element.73), channel_id=1, source_target_pairs={{0,2},{1,3},{2,0},{3,1},{4,6},{5,7},{6,4},{7,5},{8,10},{9,11},{10,... | collective-permute-start | bytes 589832 | tf_op jit(solution)/shard_map/ppermute | solution.py:451
  105.8 15.1 %collective-permute-start.14 = (f32[3,64,256]{2,1,0:T(8,128)S(1)}, f32[3,64,256]{2,1,0:T(8,128)S(1)}, u32[]{:S(2)}, u32[]{:S(2)}) collective-permute-start(f32[3,64,256]{2,1,0:T(8,128)S(1)} %get-tuple-element.74), channel_id=1, source_target_pairs={{0,3},{1,0},{2,1},{3,2},{4,7},{5,4},{6,5},{7,6},{8,11},{9,8},{10,9... | collective-permute-start | bytes 589832 | tf_op jit(solution)/shard_map/ppermute | solution.py:451

commit v9 on v8

--- a/solution.py
+++ b/solution.py
@@ -303,7 +303,7 @@
     )(t, x, above, below, *sent)
 
 
-def place_first_kernel(t_ref, o0, r1, r2, r3, out, buf, sem, sem_out):
+def place_first_kernel(t_ref, r2, r1, r3, o0, out, buf, sem, sem_out):
     first = CHUNK * half_of(0, t_ref)
     copies = start_all(sem, [(r, buf.at[j]) for j, r in enumerate((o0, r1, r2, r3))])
     outs = []
@@ -327,7 +327,7 @@
     )(t, *pieces)[0]
 
 
-def place_second_kernel(t_ref, o0, r1, r2, r3, begun, out, sem):
+def place_second_kernel(t_ref, r2, r1, r3, o0, begun, out, sem):
     first = CHUNK * half_of(1, t_ref)
     pairs = [
         (r, out.at[:, pl.ds(aligned(t_ref[LON + j] * ROWS + first), CHUNK), :])
@@ -489,12 +489,12 @@
 
     m1 = model_call(0, t, f1, come)
     o1 = weight_call(0, t, m1, rows, own, come)
-    r1 = [to_lon(o1[j], j) if j else o1[j] for j in range(LON)]
+    r1 = [to_lon(o1[j], j) if j else o1[j] for j in (2, 1, 3, 0)]
     f2, *tied = lax.optimization_barrier((f2, *o1, *extra))
     o1, extra = tied[:LON], tied[LON:]
     m2 = model_call(1, t, f2, come)
     o2 = weight_call(1, t, m2, rows, own, extra)
-    r2 = [to_lon(o2[j], j) if j else o2[j] for j in range(LON)]
+    r2 = [to_lon(o2[j], j) if j else o2[j] for j in (2, 1, 3, 0)]
     return place_second(t, r2, place_first(t, r1, tile_rows))[None]
 
 

time: 124 us -> 124 us (level)
  no operation moved by 1% of the time
where the time goes in v9:
time: 124 us; the launch traced here: 122 us
  waiting for transfers between devices  43.8 us (35%)
  starting transfers between devices  42.8 us (35%)
  Pallas kernels  28.5 us (23%)
  local copies, waits for them, and re-layouts  3.51 us (3%)
  matrix products  2.76 us (2%)
    ppermute x4, waiting for transfers between devices, to_next(): return lax.ppermute(value, ('sub', 'lon'), pairs)  32.6 us
    ppermute x6, starting transfers between devices, to_lon(): return lax.ppermute(value, 'lon', ring(LON, j))  14.4 us
    ppermute x4, starting transfers between devices, to_next(): return lax.ppermute(value, ('sub', 'lon'), pairs)  12 us
    ppermute x6, waiting for transfers between devices, to_lon(): return lax.ppermute(value, 'lon', ring(LON, j))  11.2 us
    ppermute x3, starting transfers between devices, shards(): extra[j] = lax.ppermute(block, ('sub', 'lon'), pairs) if j else block  10.7 us
    pallas_call x2, Pallas kernels, model_call(): call(functools.partial(model_kernel, chunk), array(3, CHUNK, NLON), [smem...  10.4 us
    pallas_call x2, Pallas kernels, weight_call(): call(functools.partial(weight_kernel, chunk), [array(3, CHUNK, 256)] * 4,...  5.49 us
    ppermute x1, starting transfers between devices, shards(): above = lax.ppermute(x[:, tile_rows - 16:], 'lat', ring(8, 1))  3.39 us
  transfers between devices with their start and end apart: 18, of which 5 were waited for; matrix products, arithmetic and copies ran while one was open for 3% of the time, Pallas kernels for 20%

profile of v9, /device:TPU:24, one launch (start us, length us, event | category | flops | bytes accessed | tf_op | source)
XLA Modules:
  0.0 122.5 jit_solution(17777913204824942877)
XLA Ops:
  0.0 0.8 fusion.6
  0.8 0.8 collective-permute-start.1
  1.6 3.4 %collective-permute-start = (f32[3,16,256]{2,1,0:T(8,128)S(1)}, f32[3,16,256]{2,1,0:T(8,128)S(1)}, u32[]{:S(2)}, u32[]{:S(2)}) collective-permute-start(f32[3,16,256]{2,1,0:T(8,128)S(1)} %get-tuple-element.76), channel_id=1, source_target_pairs={{0,4},{4,8},{8,12},{12,16},{16,20},{20,24},{24,28},{28,0},{1,5},{5... | collective-permute-start | bytes 147464 | tf_op jit(solution)/shard_map/ppermute | solution.py:466
  5.6 3.2 %shard_map.46 = (f32[440,256]{1,0:T(8,128)}, f32[440,256]{1,0:T(8,128)}, f32[440,256]{1,0:T(8,128)}, f32[440,256]{1,0:T(8,128)}) custom-call(s32[9]{0:T(128)} %compare_select_fusion.3.t_ref, f32[3,512,256]{2,1,0:T(8,128)} %bitcast.5, f32[3,512,256]{2,1,0:T(8,128)} %back.3), custom_call_target="tpu_custom_call" | custom-call | bytes 1 | tf_op jit(solution)/shard_map/pallas_call | solution.py:252
  9.4 2.5 %shard_map.47 = (f32[440,256]{1,0:T(8,128)}, f32[440,256]{1,0:T(8,128)}, f32[440,256]{1,0:T(8,128)}, f32[440,256]{1,0:T(8,128)}) custom-call(s32[9]{0:T(128)} %compare_select_fusion.3.t_ref, f32[3,512,256]{2,1,0:T(8,128)} %bitcast.6, f32[3,16,256]{2,1,0:T(8,128)} %copy-done.9, ...), custom_call_target="tpu_custom_call", output_to_operand_aliasing={{0}: (4, {}), {1}: (5, {}), {2}: (6, {}), {3}: (7, {})} | custom-call | bytes 1 | tf_op jit(solution)/shard_map/pallas_call | solution.py:290
  12.0 8.4 %collective-permute-start.4 = (f32[440,256]{1,0:T(8,128)}, f32[440,256]{1,0:T(8,128)S(1)}, u32[]{:S(2)}, u32[]{:S(2)}) collective-permute-start(f32[440,256]{1,0:T(8,128)} %get-tuple-element.46), channel_id=1, source_target_pairs={{0,34},{1,35},{2,32},{3,33},{32,66},{33,67},{34,64},{35,65},{64,98... | collective-permute-start | bytes 1351688 | tf_op jit(solution)/shard_map/ppermute | solution.py:447
  20.4 3.6 %collective-permute-start.5 = (f32[440,256]{1,0:T(8,128)}, f32[440,256]{1,0:T(8,128)S(1)}, u32[]{:S(2)}, u32[]{:S(2)}) collective-permute-start(f32[440,256]{1,0:T(8,128)} %get-tuple-element.47), channel_id=1, source_target_pairs={{0,33},{1,34},{2,35},{3,32},{32,65},{33,66},{34,67},{35,64},{64,97... | collective-permute-start | bytes 1351688 | tf_op jit(solution)/shard_map/ppermute | solution.py:447
  23.9 2.8 %fusion.7 = f32[3,1024]{1,0:T(4,128)S(1)} fusion(f32[3,513]{1,0:T(4,128)S(1)} %copy-done, f32[513,1024]{1,0:T(8,128)} %constant.52.clone), kind=kOutput, calls=%fused_computation.16 | convolution fusion | flops 18911232 | bytes 2119692 | tf_op jit(solution)/shard_map/dot_general | solution.py:375
  26.7 14.4 %collective-permute-done.4.s2.refs_6_ = f32[440,256]{1,0:T(8,128)S(1)} collective-permute-done((f32[440,256]{1,0:T(8,128)}, f32[440,256]{1,0:T(8,128)S(1)}, u32[]{:S(2)}, u32[]{:S(2)}) %collective-permute-start.4) | collective-permute-done | bytes 450592 | tf_op jit(solution)/shard_map/ppermute | solution.py:447
  41.1 2.9 %shard_map.49 = (f32[3,64,256]{2,1,0:T(8,128)}, f32[3,64,256]{2,1,0:T(8,128)}, f32[3,64,256]{2,1,0:T(8,128)}, f32[3,64,256]{2,1,0:T(8,128)}) custom-call(s32[9]{0:T(128)} %compare_select_fusion.3.t_ref, f32[3,512,256]{2,1,0:T(8,128)} %bitcast.7, f32[3,512,256]{2,1,0:T(8,128)} %back.3), custom_call_target="tpu_custom_call" | custom-call | bytes 1 | tf_op jit(solution)/shard_map/pallas_call | solution.py:208
  44.1 18.2 %collective-permute-done.3.s3.refs_5_ = f32[440,256]{1,0:T(8,128)S(1)} collective-permute-done((f32[440,256]{1,0:T(8,128)}, f32[440,256]{1,0:T(8,128)S(1)}, u32[]{:S(2)}, u32[]{:S(2)}) %collective-permute-start.3) | collective-permute-done | bytes 450592 | tf_op jit(solution)/shard_map/ppermute | solution.py:447
  62.5 1.4 %collective-permute-start.6 = (f32[440,256]{1,0:T(8,128)S(1)}, f32[440,256]{1,0:T(8,128)}, u32[]{:S(2)}, u32[]{:S(2)}) collective-permute-start(f32[440,256]{1,0:T(8,128)S(1)} %collective-permute-done.3.s3.refs_5_), channel_id=1, source_target_pairs={{0,224},{32,0},{64,32},{96,64},{128,96},{160,128},{192,160},{224,1... | collective-permute-start | bytes 1351688 | tf_op jit(solution)/shard_map/ppermute | solution.py:488
  63.9 4.5 %collective-permute-start.9 = (f32[3,64,256]{2,1,0:T(8,128)}, f32[3,64,256]{2,1,0:T(8,128)}, u32[]{:S(2)}, u32[]{:S(2)}) collective-permute-start(f32[3,64,256]{2,1,0:T(8,128)} %get-tuple-element.63), channel_id=1, source_target_pairs={{0,3},{1,0},{2,1},{3,2},{224,227},{225,224},{226,225},{227,226},{4... | collective-permute-start | bytes 589832 | tf_op jit(solution)/shard_map/ppermute | solution.py:486
  68.3 3.7 %collective-permute-start.10 = (f32[3,64,256]{2,1,0:T(8,128)}, f32[3,64,256]{2,1,0:T(8,128)}, u32[]{:S(2)}, u32[]{:S(2)}) collective-permute-start(f32[3,64,256]{2,1,0:T(8,128)} %get-tuple-element.64), channel_id=1, source_target_pairs={{0,2},{1,3},{2,0},{3,1},{224,226},{225,227},{226,224},{227,225},{4... | collective-permute-start | bytes 589832 | tf_op jit(solution)/shard_map/ppermute | solution.py:486
  72.1 2.5 %collective-permute-start.11 = (f32[3,64,256]{2,1,0:T(8,128)}, f32[3,64,256]{2,1,0:T(8,128)}, u32[]{:S(2)}, u32[]{:S(2)}) collective-permute-start(f32[3,64,256]{2,1,0:T(8,128)} %get-tuple-element.65), channel_id=1, source_target_pairs={{0,1},{1,2},{2,3},{3,0},{224,225},{225,226},{226,227},{227,224},{4... | collective-permute-start | bytes 589832 | tf_op jit(solution)/shard_map/ppermute | solution.py:486
  74.6 5.2 %shard_map.48.f_ref = f32[3,64,1024]{2,1,0:T(8,128)S(1)} custom-call(s32[9]{0:T(128)S(1)} %copy-done.5, f32[98]{0:T(128)S(1)} %sine_multiply_fusion.f_ref, f32[440,256]{1,0:T(8,128)S(1)} %collective-permute-done.2.s0.refs_4_, f32[440,256]{1,0:T(8,128)S(1)} %collective-permute-done.3.s3.refs_5_, f32[440,256]{1,0:T(8,128)S(1)} %collective-permute-done.4.s2.refs_6_, ...), custom_call_target="tpu_custom_call" | custom-call | bytes 1 | tf_op jit(solution)/shard_map/pallas_call | solution.py:174
  79.8 2.9 %shard_map.50 = (f32[3,64,256]{2,1,0:T(8,128)S(1)}, f32[3,64,256]{2,1,0:T(8,128)}, f32[3,64,256]{2,1,0:T(8,128)S(1)}, f32[3,64,256]{2,1,0:T(8,128)S(1)}) custom-call(s32[9]{0:T(128)S(1)} %copy-done.5, f32[3,64,1024]{2,1,0:T(8,128)S(1)} %shard_map.48.f_ref, f32[3,256]{1,0:T(4,128)S(1)} %get-tuple-element.54.a_ref, f32[3,256]{1,0:T(4,128)S(1)} %get-tuple-element.55.b_ref, ...), custom_call_target="tpu_custom_call" | custom-call | bytes 1 | tf_op jit(solution)/shard_map/pallas_call | solution.py:422
  82.8 0.7 copy-done.3
  83.5 0.7 copy-done.6
  84.1 0.7 copy-done.7
  84.8 4.1 %collective-permute-start.16 = (f32[3,64,256]{2,1,0:T(8,128)}, f32[3,64,256]{2,1,0:T(8,128)}, u32[]{:S(2)}, u32[]{:S(2)}) collective-permute-start(f32[3,64,256]{2,1,0:T(8,128)} %get-tuple-element.59), channel_id=1, source_target_pairs={{0,1},{1,2},{2,3},{3,0},{4,5},{5,6},{6,7},{7,4},{8,9},{9,10},{10,1... | collective-permute-start | bytes 589832 | tf_op jit(solution)/shard_map/ppermute | solution.py:451
  89.0 1.9 %collective-permute-start.15 = (f32[3,64,256]{2,1,0:T(8,128)}, f32[3,64,256]{2,1,0:T(8,128)S(1)}, u32[]{:S(2)}, u32[]{:S(2)}) collective-permute-start(f32[3,64,256]{2,1,0:T(8,128)} %copy-done.7), channel_id=1, source_target_pairs={{0,2},{1,3},{2,0},{3,1},{4,6},{5,7},{6,4},{7,5},{8,10},{9,11},{10,... | collective-permute-start | bytes 589832 | tf_op jit(solution)/shard_map/ppermute | solution.py:451
  90.9 2.1 %collective-permute-start.17 = (f32[3,64,256]{2,1,0:T(8,128)}, f32[3,64,256]{2,1,0:T(8,128)S(1)}, u32[]{:S(2)}, u32[]{:S(2)}) collective-permute-start(f32[3,64,256]{2,1,0:T(8,128)} %copy-done.6), channel_id=1, source_target_pairs={{0,3},{1,0},{2,1},{3,2},{4,7},{5,4},{6,5},{7,6},{8,11},{9,8},{10,9... | collective-permute-start | bytes 589832 | tf_op jit(solution)/shard_map/ppermute | solution.py:451
  93.0 5.2 %shard_map.51.f_ref = f32[3,64,1024]{2,1,0:T(8,128)S(1)} custom-call(s32[9]{0:T(128)S(1)} %copy-done.5, f32[98]{0:T(128)S(1)} %sine_multiply_fusion.1.f_ref, f32[440,256]{1,0:T(8,128)S(1)} %collective-permute-done.2.s0.refs_4_, f32[440,256]{1,0:T(8,128)S(1)} %collective-permute-done.3.s3.refs_5_, f32[440,256]{1,0:T(8,128)S(1)} %collective-permute-done.4.s2.refs_6_, ...), custom_call_target="tpu_custom_call" | custom-call | bytes 1 | tf_op jit(solution)/shard_map/pallas_call | solution.py:174
  98.2 2.5 %shard_map.52 = (f32[3,64,256]{2,1,0:T(8,128)S(1)}, f32[3,64,256]{2,1,0:T(8,128)S(1)}, f32[3,64,256]{2,1,0:T(8,128)S(1)}, f32[3,64,256]{2,1,0:T(8,128)S(1)}) custom-call(s32[9]{0:T(128)S(1)} %copy-done.5, f32[3,64,1024]{2,1,0:T(8,128)S(1)} %shard_map.51.f_ref, f32[3,256]{1,0:T(4,128)S(1)} %get-tuple-element.54.a_ref, f32[3,256]{1,0:T(4,128)S(1)} %get-tuple-element.55.b_ref, ...), custom_call_target="tpu_custom_call" | custom-call | bytes 1 | tf_op jit(solution)/shard_map/pallas_call | solution.py:422
  100.8 2.1 %collective-permute-start.12 = (f32[3,64,256]{2,1,0:T(8,128)S(1)}, f32[3,64,256]{2,1,0:T(8,128)S(1)}, u32[]{:S(2)}, u32[]{:S(2)}) collective-permute-start(f32[3,64,256]{2,1,0:T(8,128)S(1)} %get-tuple-element.71), channel_id=1, source_target_pairs={{0,2},{1,3},{2,0},{3,1},{4,6},{5,7},{6,4},{7,5},{8,10},{9,11},{10,... | collective-permute-start | bytes 589832 | tf_op jit(solution)/shard_map/ppermute | solution.py:451
  102.9 2.9 %collective-permute-start.13 = (f32[3,64,256]{2,1,0:T(8,128)S(1)}, f32[3,64,256]{2,1,0:T(8,128)S(1)}, u32[]{:S(2)}, u32[]{:S(2)}) collective-permute-start(f32[3,64,256]{2,1,0:T(8,128)S(1)} %get-tuple-element.72), channel_id=1, source_target_pairs={{0,1},{1,2},{2,3},{3,0},{4,5},{5,6},{6,7},{7,4},{8,9},{9,10},{10,1... | collective-permute-start | bytes 589832 | tf_op jit(solution)/shard_map/ppermute | solution.py:451
  105.8 1.2 collective-permute-start.14
  107.0 1.1 collective-permute-done.15.r2
  108.1 10.0 %collective-permute-done.17.r3 = f32[3,64,256]{2,1,0:T(8,128)S(1)} collective-permute-done((f32[3,64,256]{2,1,0:T(8,128)}, f32[3,64,256]{2,1,0:T(8,128)S(1)}, u32[]{:S(2)}, u32[]{:S(2)}) %collective-permute-start.17) | collective-permute-done | bytes 196640 | tf_op jit(solution)/shard_map/ppermute | solution.py:451
  118.1 2.6 %shard_map.53.begun = f32[3,512,256]{2,1,0:T(8,128)} custom-call(s32[9]{0:T(128)S(1)} %copy-done.5, f32[3,64,256]{2,1,0:T(8,128)S(1)} %collective-permute-done.15.r2, f32[3,64,256]{2,1,0:T(8,128)} %collective-permute-done.16.r1, f32[3,64,256]{2,1,0:T(8,128)S(1)} %collective-permute-done.17.r3, f32[3,64,256]{2,1,0:T(8,128)S(1)} %copy-done.4), custom_call_target="tpu_custom_call" | custom-call | bytes 1 | tf_op jit(solution)/shard_map/pallas_call | solution.py:320
  120.9 1.5 %shard_map.54 = f32[3,512,256]{2,1,0:T(8,128)} custom-call(s32[9]{0:T(128)S(1)} %copy-done.5, f32[3,64,256]{2,1,0:T(8,128)S(1)} %collective-permute-done.12.r2, f32[3,64,256]{2,1,0:T(8,128)S(1)} %collective-permute-done.13.r1, f32[3,64,256]{2,1,0:T(8,128)S(1)} %collective-permute-done.14.r3, ...), custom_call_target="tpu_custom_call", output_to_operand_aliasing={{}: (5, {})} | custom-call | bytes 1 | tf_op jit(solution)/shard_map/pallas_call | solution.py:341
  (40 shorter events, 1.7 us)
Async XLA Ops:
  0.0 23.9 %copy-start = (f32[3,513]{1,0:T(4,128)S(1)}, f32[3,513]{1,0:T(4,128)}, u32[]{:S(2)}) copy-start(f32[3,513]{1,0:T(4,128)} %param.6) | copy-start | bytes 18472
  0.8 8.0 %collective-permute-start.1 = (f32[3,16,256]{2,1,0:T(8,128)S(1)}, f32[3,16,256]{2,1,0:T(8,128)S(1)}, u32[]{:S(2)}, u32[]{:S(2)}) collective-permute-start(f32[3,16,256]{2,1,0:T(8,128)S(1)} %get-tuple-element.75), channel_id=1, source_target_pairs={{0,28},{4,0},{8,4},{12,8},{16,12},{20,16},{24,20},{28,24},{1,29},{... | collective-permute-start | bytes 147464 | tf_op jit(solution)/shard_map/ppermute | solution.py:467
  1.6 7.2 %collective-permute-start = (f32[3,16,256]{2,1,0:T(8,128)S(1)}, f32[3,16,256]{2,1,0:T(8,128)S(1)}, u32[]{:S(2)}, u32[]{:S(2)}) collective-permute-start(f32[3,16,256]{2,1,0:T(8,128)S(1)} %get-tuple-element.76), channel_id=1, source_target_pairs={{0,4},{4,8},{8,12},{12,16},{16,20},{20,24},{24,28},{28,0},{1,5},{5... | collective-permute-start | bytes 147464 | tf_op jit(solution)/shard_map/ppermute | solution.py:466
  8.8 0.6 copy-start.8
  8.8 0.6 copy-start.9
  12.0 12.0 %collective-permute-start.2 = (f32[440,256]{1,0:T(8,128)}, f32[440,256]{1,0:T(8,128)S(1)}, u32[]{:S(2)}, u32[]{:S(2)}) collective-permute-start(f32[440,256]{1,0:T(8,128)} %get-tuple-element.44.refs_0_), channel_id=1, source_target_pairs={{0,32},{1,33},{2,34},{3,35},{32,64},{33,65},{34,66},{35,67},{64,96... | collective-permute-start | bytes 1351688 | tf_op jit(solution)/shard_map/ppermute | solution.py:447
  12.0 29.1 %collective-permute-start.4 = (f32[440,256]{1,0:T(8,128)}, f32[440,256]{1,0:T(8,128)S(1)}, u32[]{:S(2)}, u32[]{:S(2)}) collective-permute-start(f32[440,256]{1,0:T(8,128)} %get-tuple-element.46), channel_id=1, source_target_pairs={{0,34},{1,35},{2,32},{3,33},{32,66},{33,67},{34,64},{35,65},{64,98... | collective-permute-start | bytes 1351688 | tf_op jit(solution)/shard_map/ppermute | solution.py:447
  20.4 41.9 %collective-permute-start.3 = (f32[440,256]{1,0:T(8,128)}, f32[440,256]{1,0:T(8,128)S(1)}, u32[]{:S(2)}, u32[]{:S(2)}) collective-permute-start(f32[440,256]{1,0:T(8,128)} %get-tuple-element.45), channel_id=1, source_target_pairs={{0,35},{1,32},{2,33},{3,34},{32,67},{33,64},{34,65},{35,66},{64,99... | collective-permute-start | bytes 1351688 | tf_op jit(solution)/shard_map/ppermute | solution.py:447
  20.4 41.9 %collective-permute-start.5 = (f32[440,256]{1,0:T(8,128)}, f32[440,256]{1,0:T(8,128)S(1)}, u32[]{:S(2)}, u32[]{:S(2)}) collective-permute-start(f32[440,256]{1,0:T(8,128)} %get-tuple-element.47), channel_id=1, source_target_pairs={{0,33},{1,34},{2,35},{3,32},{32,65},{33,66},{34,67},{35,64},{64,97... | collective-permute-start | bytes 1351688 | tf_op jit(solution)/shard_map/ppermute | solution.py:447
  41.1 31.0 %collective-permute-start.7 = (f32[440,256]{1,0:T(8,128)S(1)}, f32[440,256]{1,0:T(8,128)S(1)}, u32[]{:S(2)}, u32[]{:S(2)}) collective-permute-start(f32[440,256]{1,0:T(8,128)S(1)} %collective-permute-done.4.s2.refs_6_), channel_id=1, source_target_pairs={{0,224},{32,0},{64,32},{96,64},{128,96},{160,128},{192,160},{224,1... | collective-permute-start | bytes 1351688 | tf_op jit(solution)/shard_map/ppermute | solution.py:488
  41.1 33.5 %copy-start.5 = (s32[9]{0:T(128)S(1)}, s32[9]{0:T(128)}, u32[]{:S(2)}) copy-start(s32[9]{0:T(128)} %compare_select_fusion.3.t_ref) | copy-start | bytes 112
  44.0 35.8 %copy-start.1 = (f32[440,256]{1,0:T(8,128)S(1)}, f32[440,256]{1,0:T(8,128)}, u32[]{:S(2)}) copy-start(f32[440,256]{1,0:T(8,128)} %get-tuple-element.44.refs_0_) | copy-start | bytes 1351684
  62.3 17.5 %collective-permute-start.8 = (f32[440,256]{1,0:T(8,128)S(1)}, f32[440,256]{1,0:T(8,128)S(1)}, u32[]{:S(2)}, u32[]{:S(2)}) collective-permute-start(f32[440,256]{1,0:T(8,128)S(1)} %collective-permute-done.5.s1.refs_7_), channel_id=1, source_target_pairs={{0,224},{32,0},{64,32},{96,64},{128,96},{160,128},{192,160},{224,1... | collective-permute-start | bytes 1351688 | tf_op jit(solution)/shard_map/ppermute | solution.py:488
  62.5 17.3 %collective-permute-start.6 = (f32[440,256]{1,0:T(8,128)S(1)}, f32[440,256]{1,0:T(8,128)}, u32[]{:S(2)}, u32[]{:S(2)}) collective-permute-start(f32[440,256]{1,0:T(8,128)S(1)} %collective-permute-done.3.s3.refs_5_), channel_id=1, source_target_pairs={{0,224},{32,0},{64,32},{96,64},{128,96},{160,128},{192,160},{224,1... | collective-permute-start | bytes 1351688 | tf_op jit(solution)/shard_map/ppermute | solution.py:488
  63.9 27.1 %collective-permute-start.9 = (f32[3,64,256]{2,1,0:T(8,128)}, f32[3,64,256]{2,1,0:T(8,128)}, u32[]{:S(2)}, u32[]{:S(2)}) collective-permute-start(f32[3,64,256]{2,1,0:T(8,128)} %get-tuple-element.63), channel_id=1, source_target_pairs={{0,3},{1,0},{2,1},{3,2},{224,227},{225,224},{226,225},{227,226},{4... | collective-permute-start | bytes 589832 | tf_op jit(solution)/shard_map/ppermute | solution.py:486
  68.3 24.7 %collective-permute-start.10 = (f32[3,64,256]{2,1,0:T(8,128)}, f32[3,64,256]{2,1,0:T(8,128)}, u32[]{:S(2)}, u32[]{:S(2)}) collective-permute-start(f32[3,64,256]{2,1,0:T(8,128)} %get-tuple-element.64), channel_id=1, source_target_pairs={{0,2},{1,3},{2,0},{3,1},{224,226},{225,227},{226,224},{227,225},{4... | collective-permute-start | bytes 589832 | tf_op jit(solution)/shard_map/ppermute | solution.py:486
  72.1 20.9 %collective-permute-start.11 = (f32[3,64,256]{2,1,0:T(8,128)}, f32[3,64,256]{2,1,0:T(8,128)}, u32[]{:S(2)}, u32[]{:S(2)}) collective-permute-start(f32[3,64,256]{2,1,0:T(8,128)} %get-tuple-element.65), channel_id=1, source_target_pairs={{0,1},{1,2},{2,3},{3,0},{224,225},{225,226},{226,227},{227,224},{4... | collective-permute-start | bytes 589832 | tf_op jit(solution)/shard_map/ppermute | solution.py:486
  82.8 0.7 copy-start.3
  83.5 0.7 copy-start.6
  84.1 0.7 copy-start.7
  84.8 13.4 %copy-start.2 = (f32[3,64,256]{2,1,0:T(8,128)S(1)}, f32[3,64,256]{2,1,0:T(8,128)}, u32[]{:S(2)}) copy-start(f32[3,64,256]{2,1,0:T(8,128)} %get-tuple-element.67.refs_4_) | copy-start | bytes 589828
  84.8 21.0 %collective-permute-start.16 = (f32[3,64,256]{2,1,0:T(8,128)}, f32[3,64,256]{2,1,0:T(8,128)}, u32[]{:S(2)}, u32[]{:S(2)}) collective-permute-start(f32[3,64,256]{2,1,0:T(8,128)} %get-tuple-element.59), channel_id=1, source_target_pairs={{0,1},{1,2},{2,3},{3,0},{4,5},{5,6},{6,7},{7,4},{8,9},{9,10},{10,1... | collective-permute-start | bytes 589832 | tf_op jit(solution)/shard_map/ppermute | solution.py:451
  89.0 19.1 %collective-permute-start.15 = (f32[3,64,256]{2,1,0:T(8,128)}, f32[3,64,256]{2,1,0:T(8,128)S(1)}, u32[]{:S(2)}, u32[]{:S(2)}) collective-permute-start(f32[3,64,256]{2,1,0:T(8,128)} %copy-done.7), channel_id=1, source_target_pairs={{0,2},{1,3},{2,0},{3,1},{4,6},{5,7},{6,4},{7,5},{8,10},{9,11},{10,... | collective-permute-start | bytes 589832 | tf_op jit(solution)/shard_map/ppermute | solution.py:451
  90.9 27.2 %collective-permute-start.17 = (f32[3,64,256]{2,1,0:T(8,128)}, f32[3,64,256]{2,1,0:T(8,128)S(1)}, u32[]{:S(2)}, u32[]{:S(2)}) collective-permute-start(f32[3,64,256]{2,1,0:T(8,128)} %copy-done.6), channel_id=1, source_target_pairs={{0,3},{1,0},{2,1},{3,2},{4,7},{5,4},{6,5},{7,6},{8,11},{9,8},{10,9... | collective-permute-start | bytes 589832 | tf_op jit(solution)/shard_map/ppermute | solution.py:451
  98.2 19.9 %copy-start.4 = (f32[3,64,256]{2,1,0:T(8,128)S(1)}, f32[3,64,256]{2,1,0:T(8,128)}, u32[]{:S(2)}) copy-start(f32[3,64,256]{2,1,0:T(8,128)} %copy-done.3) | copy-start | bytes 589828
  100.8 19.9 %collective-permute-start.12 = (f32[3,64,256]{2,1,0:T(8,128)S(1)}, f32[3,64,256]{2,1,0:T(8,128)S(1)}, u32[]{:S(2)}, u32[]{:S(2)}) collective-permute-start(f32[3,64,256]{2,1,0:T(8,128)S(1)} %get-tuple-element.71), channel_id=1, source_target_pairs={{0,2},{1,3},{2,0},{3,1},{4,6},{5,7},{6,4},{7,5},{8,10},{9,11},{10,... | collective-permute-start | bytes 589832 | tf_op jit(solution)/shard_map/ppermute | solution.py:451
  102.9 17.8 %collective-permute-start.13 = (f32[3,64,256]{2,1,0:T(8,128)S(1)}, f32[3,64,256]{2,1,0:T(8,128)S(1)}, u32[]{:S(2)}, u32[]{:S(2)}) collective-permute-start(f32[3,64,256]{2,1,0:T(8,128)S(1)} %get-tuple-element.72), channel_id=1, source_target_pairs={{0,1},{1,2},{2,3},{3,0},{4,5},{5,6},{6,7},{7,4},{8,9},{9,10},{10,1... | collective-permute-start | bytes 589832 | tf_op jit(solution)/shard_map/ppermute | solution.py:451
  105.8 15.0 %collective-permute-start.14 = (f32[3,64,256]{2,1,0:T(8,128)S(1)}, f32[3,64,256]{2,1,0:T(8,128)S(1)}, u32[]{:S(2)}, u32[]{:S(2)}) collective-permute-start(f32[3,64,256]{2,1,0:T(8,128)S(1)} %get-tuple-element.73), channel_id=1, source_target_pairs={{0,3},{1,0},{2,1},{3,2},{4,7},{5,4},{6,5},{7,6},{8,11},{9,8},{10,9... | collective-permute-start | bytes 589832 | tf_op jit(solution)/shard_map/ppermute | solution.py:451
